TPU v7x, 32 devices: a whole 2x2x4 slice. The times are simulated.
32 devices in a mesh: groups: 2 (over y), tensor: 4 (over z), section: 2 (over x), seq: 2 (over core).
Axes of the slice: x: 2, y: 2, z: 4, core: 2. Of those that a mesh axis runs over, the one named last changes fastest.
Arguments:
- token_ids: int32 [4, 96], P('groups'), parts along dimension 0, may hold values from 0 to 511
- leading_span_index: int32 [2], P('groups'), parts along dimension 0, may hold values from 8 to 4103
- embed_table: float32 [512, 8192], P(None, 'tensor'), may hold values from -6 to 6
- norm_gain: float32 [2, 8192], P('section', 'tensor'), may hold values from 0.25 to 1.75
- decay_rates: float32 [2, 16, 8192], P('section', None, 'tensor'), may hold values from 0.0002 to 0.03
- residues: float32 [2, 16, 8192], P('section', None, 'tensor'), may hold values from -0.12 to 0.12
- history: float32 [2, 8, 192, 8192], P('section', 'seq', 'groups', 'tensor'), parts along dimension 2, may hold values from -6 to 6
- mix_weight: bfloat16 [2, 8192, 8192], P('section', None, ('tensor', 'seq')), may hold values from -0.0625 to 0.0625
Outputs:
- section_out: float32 [2, 2, 192, 8192], P('section', None, 'groups', ('tensor', 'seq')), parts along dimension 2
There are 2 independent parts, one for each index of `groups`. A program takes and returns all parts, laid end to end along the dimension named above; an argument that names none is the same for every part. Nothing has to cross between parts.
Inputs may be any that keep to these rules, and one draw needn't show every extreme that they name: `leading_span_index`: index of the first span of the run; the span before it is the newest one in history.
All inputs are finite; a program needn't handle non-finite values.
Results may differ from a plain program's by a relative error of at most 0.0036.
Values may be sent and summed in bfloat16 or wider, within the bound.
No kernel may reach another device: no remote copies, remote signals or barrier semaphores. Data moves between devices by JAX's collectives and lax.ppermute only.
A program may use at most 128 MiB of HBM per device.

v0:
```python
import functools

import jax
import jax.numpy as jnp
from jax import lax
from jax.experimental import pallas as pl
from jax.experimental.pallas import tpu as pltpu
from jax.sharding import PartitionSpec as P


epsilon = 1e-05
highest = lax.Precision.HIGHEST
LANES = 128
SUB = 8
f32 = jnp.float32
VMEM_BYTES = 24 << 20


def params(**more):
    return pltpu.CompilerParams(vmem_limit_bytes=VMEM_BYTES, **more)


def in_hbm(value):
    return pltpu.with_memory_space_constraint(value, pltpu.HBM)


def cost(flops, moved):
    return pl.CostEstimate(flops=int(flops), bytes_accessed=int(moved), transcendentals=0)


def row_sums(squares):
    ones = jnp.ones((SUB, squares.shape[1]), f32)
    return lax.dot_general(
        ones, squares, (((1,), (1,)), ((), ())), precision=highest, preferred_element_type=f32
    )


def lane_tiles_squared(block):
    total = block[:, :LANES] * block[:, :LANES]
    for start in range(LANES, block.shape[1], LANES):
        piece = block[:, start : start + LANES]
        total = total + piece * piece
    return total


def embed_body(chunks, ids, meta, table, x_out, sums_out, held, rows_buf, sems):
    spans, rows = sums_out.shape[0], sums_out.shape[2]
    half = x_out.shape[2]
    width = held.shape[1]
    depth = held.shape[0] // chunks
    copies = [
        pltpu.make_async_copy(
            table.at[pl.ds(c * depth, depth), :], held.at[pl.ds(c * depth, depth), :], sems.at[c]
        )
        for c in range(chunks)
    ]
    for copy in copies:
        copy.start()
    for copy in copies:
        copy.wait()
    for span in range(spans):

        def fetch(i, carry):
            rows_buf[pl.ds(i, 1), :] = held[pl.ds(ids[span, i], 1), :]
            return carry

        lax.fori_loop(0, rows, fetch, 0, unroll=8)
        sums_out[span] = row_sums(lane_tiles_squared(rows_buf[...]))
        for part in range(width // half):

            @pl.when(meta[1] == part)
            def _():
                x_out[span] = rows_buf[:, part * half : (part + 1) * half]


def embed_rows(ids, meta, table, half):
    spans, rows = ids.shape
    words, width = table.shape
    chunks = 4 if words % (4 * SUB) == 0 else 1
    return pl.pallas_call(
        functools.partial(embed_body, chunks),
        out_shape=(
            jax.ShapeDtypeStruct((spans, rows, half), f32),
            jax.ShapeDtypeStruct((spans, SUB, rows), f32),
        ),
        in_specs=[
            pl.BlockSpec(memory_space=pltpu.SMEM),
            pl.BlockSpec(memory_space=pltpu.SMEM),
            pl.BlockSpec(memory_space=pl.ANY),
        ],
        out_specs=(
            pl.BlockSpec(memory_space=pltpu.VMEM),
            pl.BlockSpec(memory_space=pltpu.VMEM),
        ),
        scratch_shapes=[
            pltpu.VMEM((words, width), f32),
            pltpu.VMEM((rows, width), f32),
            pltpu.SemaphoreType.DMA((chunks,)),
        ],
        compiler_params=params(),
        cost_estimate=cost(4 * spans * rows * width, 4 * words * width),
        name="embed_rows",
    )(ids, meta, in_hbm(table))


def mode_rows(first, step8, rows, store):
    run = list(first)
    for k in range(rows // SUB):
        total = run[0]
        for q in run[1:]:
            total = total + q
        store(k, total)
        if k + 1 < rows // SUB:
            run = [q * d for q, d in zip(run, step8)]


def spread(values, m):
    return jnp.broadcast_to(values[m : m + 1, :], (SUB, values.shape[1]))


def history_body(chunk, wide, slot_total, meta, cache, rates_any, resid_any, *rest):
    states, taps, rates_out, resid_out, held_rows, rates_ref, resid_ref, sems, mode_sems = rest
    slots, rows, _ = cache.shape
    half = taps.shape[1]
    modes = rates_ref.shape[0]
    per_half = half // chunk
    first_span, rank = meta[0], meta[1]

    def lane_start(j):
        part = 1 - rank if j < per_half else rank
        return pl.multiple_of(part * half + (j % per_half) * chunk, LANES)

    copies = [
        pltpu.make_async_copy(
            cache.at[:, :, pl.ds(lane_start(j), chunk)],
            held_rows.at[:, :, pl.ds(j * chunk, chunk)],
            sems.at[j],
        )
        for j in range(2 * per_half)
    ]
    mode_copies = [
        pltpu.make_async_copy(rates_any, rates_ref, mode_sems.at[0]),
        pltpu.make_async_copy(resid_any, resid_ref, mode_sems.at[1]),
    ]
    for copy in mode_copies + copies:
        copy.start()
    for copy in mode_copies:
        copy.wait()
    own = pl.ds(pl.multiple_of(rank * half, LANES), half)
    rates_out[...] = rates_ref[:, own]
    resid_out[...] = resid_ref[:, own]

    for j in range(2 * per_half):
        copies[j].wait()

        def one_tile(t, carry, j=j):
            at = pl.ds(pl.multiple_of(j * chunk + t * wide, LANES), wide)
            rates = rates_ref[:, pl.ds(pl.multiple_of(lane_start(j) + t * wide, LANES), wide)]
            decay = jnp.exp(-rates)

            def advance(i, held):
                base = pl.multiple_of(i * SUB, SUB)
                block = [held_rows[s, pl.ds(base, SUB), at] for s in range(slots)]
                for r in range(SUB):
                    held = tuple(
                        h * decay + jnp.broadcast_to(block[s][r : r + 1, :], (modes, wide))
                        for s, h in enumerate(held)
                    )
                return held

            held = lax.fori_loop(
                0,
                rows // SUB,
                advance,
                tuple(jnp.zeros((modes, wide), f32) for _ in range(slots)),
            )
            part_a = jnp.zeros((modes, wide), f32)
            part_b = jnp.zeros((modes, wide), f32)
            for s in range(slots):
                slot = rank * slots + s
                age = lax.rem(first_span - slot - 1 + slot_total, slot_total) + 1
                far = (age * rows).astype(f32)
                kept = jnp.where(age < slot_total, 1.0, 0.0).astype(f32)
                part_a = part_a + (held[s] * decay) * jnp.exp(-rates * (far - float(rows)))
                part_b = part_b + (held[s] * decay) * (jnp.exp(-rates * far) * kept)
            out_at = pl.ds(pl.multiple_of((j % per_half) * chunk + t * wide, LANES), wide)
            states[j // per_half, 0, :, out_at] = part_a
            states[j // per_half, 1, :, out_at] = part_b
            return carry

        lax.fori_loop(0, chunk // wide, one_tile, 0)

    def tap_tile(t, carry):
        at = pl.ds(pl.multiple_of(rank * half + t * LANES, LANES), LANES)
        out_at = pl.ds(pl.multiple_of(t * LANES, LANES), LANES)
        rates, resid = rates_ref[:, at], resid_ref[:, at]
        place = lax.broadcasted_iota(jnp.int32, (SUB, LANES), 0).astype(f32)
        step8 = jnp.exp(-rates * float(SUB))
        first = [spread(resid, m) * jnp.exp(-spread(rates, m) * place) for m in range(modes)]

        def store(k, value):
            taps[k * SUB : (k + 1) * SUB, out_at] = value

        mode_rows(first, [spread(step8, m) for m in range(modes)], rows, store)
        return carry

    lax.fori_loop(0, half // LANES, tap_tile, 0)


def history_states(meta, cache, rates, resid, half, slot_total):
    slots, rows, width = cache.shape
    modes = rates.shape[0]
    chunk = 512 if half % 512 == 0 else LANES
    wide = 2 * LANES if chunk % (2 * LANES) == 0 else LANES
    vmem = pl.BlockSpec(memory_space=pltpu.VMEM)
    return pl.pallas_call(
        functools.partial(history_body, chunk, wide, slot_total),
        out_shape=(
            jax.ShapeDtypeStruct((2, 2, modes, half), f32),
            jax.ShapeDtypeStruct((rows, half), f32),
            jax.ShapeDtypeStruct((modes, half), f32),
            jax.ShapeDtypeStruct((modes, half), f32),
        ),
        in_specs=[pl.BlockSpec(memory_space=pltpu.SMEM)] + [pl.BlockSpec(memory_space=pl.ANY)] * 3,
        out_specs=(vmem, vmem, vmem, vmem),
        scratch_shapes=[
            pltpu.VMEM((slots, rows, width), f32),
            pltpu.VMEM((modes, width), f32),
            pltpu.VMEM((modes, width), f32),
            pltpu.SemaphoreType.DMA((2 * half // chunk,)),
            pltpu.SemaphoreType.DMA((2,)),
        ],
        compiler_params=params(),
        cost_estimate=cost(2 * slots * rows * modes * width, 4 * slots * rows * width),
        name="history_states",
    )(meta, in_hbm(cache), in_hbm(rates), in_hbm(resid))


def gate_body(channels, span, counts, meta, base, *rest):
    n_delta, n_first, n_later, n_before, n_out = counts
    rest = list(rest)

    def take(n):
        return [rest.pop(0) for _ in range(n)]

    delta = take(n_delta)
    gain, rates_ref, resid_ref, taps, mine, theirs = take(6)
    first_sums, later_sums, before = take(n_first), take(n_later), take(n_before)
    gated = rest.pop(0)
    normed_out = take(n_out)
    padded, state_buf = rest
    rows, half = gated.shape
    modes = rates_ref.shape[0]
    blocks = rows // SUB
    is_first = meta[2] == 1
    wide = 4 * LANES if half % (4 * LANES) == 0 else LANES

    if n_before:

        def chain(t, carry):
            at = pl.ds(pl.multiple_of(t * wide, LANES), wide)
            decay = jnp.exp(-rates_ref[:, at])

            def advance(i, held):
                block = before[0][pl.ds(pl.multiple_of(i * SUB, SUB), SUB), at]
                for r in range(SUB):
                    held = held * decay + jnp.broadcast_to(block[r : r + 1, :], (modes, wide))
                return held

            held = lax.fori_loop(0, blocks, advance, jnp.zeros((modes, wide), f32))
            state_buf[:, at] = held * decay + (mine[1, span, :, at] + theirs[span, :, at])
            return carry

        lax.fori_loop(0, half // wide, chain, 0)
    else:
        state_buf[...] = mine[1, span] + theirs[span]

    sums = first_sums[0][span, 0:1, :]
    for ref in first_sums[1:]:
        sums = sums + ref[span, 0:1, :]
    if n_later:
        later = later_sums[0][0:1, :]
        for ref in later_sums[1:]:
            later = later + ref[0:1, :]
        sums = jnp.where(is_first, sums, later)
    here = lax.broadcasted_iota(jnp.int32, (rows, rows), 0)
    there = lax.broadcasted_iota(jnp.int32, (rows, rows), 1)
    column = jnp.sum(
        jnp.where(here == there, jnp.broadcast_to(sums, (rows, rows)), 0.0), axis=1, keepdims=True
    )
    scale = jnp.broadcast_to(lax.rsqrt(column / float(channels) + epsilon), (rows, LANES))
    padded[0:SUB, :] = jnp.zeros((SUB, LANES), f32)

    def tile(t, carry):
        at = pl.ds(pl.multiple_of(t * LANES, LANES), LANES)
        own = pl.ds(pl.multiple_of(meta[1] * half + t * LANES, LANES), LANES)
        current = base[span, :, at]
        if n_delta:
            current = current + jnp.where(is_first, 0.0, delta[0][:, at].astype(f32))
        normed = current * scale * gain[:, own]
        padded[SUB:, :] = normed
        if n_out:
            normed_out[0][:, at] = normed
        rates = rates_ref[:, at]
        weighted = resid_ref[:, at] * state_buf[:, at]
        step8 = jnp.exp(-rates * float(SUB))
        place = lax.broadcasted_iota(jnp.int32, (SUB, LANES), 0).astype(f32)
        first = [spread(weighted, m) * jnp.exp(-spread(rates, m) * place) for m in range(modes)]
        total = [None] * blocks

        def store(k, value):
            total[k] = value

        mode_rows(first, [spread(step8, m) for m in range(modes)], rows, store)
        for b in range(SUB):
            shifted = [
                padded[SUB + k * SUB - b : 2 * SUB + k * SUB - b, :] for k in range(blocks)
            ]
            for a in range(blocks):
                j = a * SUB + b
                tap = jnp.broadcast_to(taps[j : j + 1, at], (SUB, LANES))
                for k in range(a, blocks):
                    total[k] = total[k] + tap * shifted[k - a]
        for k in range(blocks):
            rows_at = pl.ds(SUB + k * SUB, SUB)
            gated[k * SUB : (k + 1) * SUB, at] = (padded[rows_at, :] * total[k]).astype(gated.dtype)
        return carry

    lax.fori_loop(0, half // LANES, tile, 0)


def gate(meta, base, delta, gain, modes_here, taps, first_sums, later_sums, states, before, channels, span):
    spans, rows, half = base.shape
    modes = modes_here[0].shape[0]
    vmem = pl.BlockSpec(memory_space=pltpu.VMEM)
    deltas = [] if delta is None else [delta]
    want = int(span + 1 < spans)
    operands = [base, *deltas, gain, *modes_here, taps, *states, *first_sums, *later_sums, *before]
    counts = (len(deltas), len(first_sums), len(later_sums), len(before), want)
    out_shape = [jax.ShapeDtypeStruct((rows, half), jnp.bfloat16)]
    if want:
        out_shape.append(jax.ShapeDtypeStruct((rows, half), f32))
    return pl.pallas_call(
        functools.partial(gate_body, channels, span, counts),
        out_shape=tuple(out_shape),
        in_specs=[pl.BlockSpec(memory_space=pltpu.SMEM)] + [vmem] * len(operands),
        out_specs=tuple(vmem for _ in out_shape),
        scratch_shapes=[pltpu.VMEM((rows + SUB, LANES), f32), pltpu.VMEM((modes, half), f32)],
        compiler_params=params(),
        cost_estimate=cost(rows * rows * half + 4 * modes * rows * half, 12 * rows * half),
        name="gate",
    )(meta, *operands)


def mix_body(kind, chosen, counts, out_tile, blocks, *refs):
    parts, n_acc, n_base, n_delta, n_done = counts
    refs = list(refs)

    def take(n):
        return [refs.pop(0) for _ in range(n)]

    pieces = [take(len(chosen)) for _ in range(parts)]
    (weight,) = take(1)
    acc_in, base, delta, done = take(n_acc), take(n_base), take(n_delta), take(n_done)
    held, sems = refs[-2:]
    rows, depth = pieces[0][0].shape
    out = weight.shape[1]
    tiles = out // out_tile
    copies = []
    for n in range(tiles):
        for p in range(parts):
            at = pl.ds(pl.multiple_of(blocks[p] * depth, depth), depth)
            columns = pl.ds(n * out_tile, out_tile)
            copies.append(
                pltpu.make_async_copy(
                    weight.at[at, columns], held.at[p, :, columns], sems.at[n * parts + p]
                )
            )
    for copy in copies:
        copy.start()
    span = chosen[0]
    squares = jnp.zeros((rows, LANES), f32)
    for n in range(tiles):
        at = slice(n * out_tile, (n + 1) * out_tile)
        for p in range(parts):
            copies[n * parts + p].wait()
        total = None
        for p in range(parts):
            lhs = jnp.concatenate([piece[...] for piece in pieces[p]], axis=0)
            more = jnp.dot(lhs, held[p, :, at], preferred_element_type=f32)
            total = more if total is None else total + more
        if n_acc and acc_in[0].shape[0] == total.shape[0]:
            total = total + acc_in[0][:, at]
        elif n_acc:
            total = total + acc_in[0][span * rows : (span + 1) * rows, at]
        if kind == "part":
            refs[0][:, at] = total
            continue
        if n_delta:
            total = total + jnp.where(blocks[parts] == 1, 0.0, delta[0][:, at].astype(f32))
        fresh = base[0][span, :, at] + total
        if kind == "hop":
            refs[0][:, at] = total.astype(refs[0].dtype)
            squares = squares + lane_tiles_squared(fresh)
        elif kind == "done":
            refs[0][:, at] = fresh
        else:
            refs[0][0, span, :, at] = fresh
            for i, ref in enumerate(done):
                refs[0][0, i, :, at] = ref[:, at]
    if kind == "hop":
        refs[1][...] = row_sums(squares)


def mix(kind, blocks, pieces, chosen, weight, acc, base, delta, done=()):
    rows, depth = pieces[0][0].shape
    out = weight.shape[1]
    vmem = pl.BlockSpec(memory_space=pltpu.VMEM)
    accs = [] if acc is None else [acc]
    bases = [] if kind == "part" else [base]
    deltas = [] if kind == "part" or delta is None else [delta]
    flat = [piece for part in pieces for piece in part]
    operands = [*flat, in_hbm(weight), *accs, *bases, *deltas, *done]
    counts = (len(pieces), len(accs), len(bases), len(deltas), len(done))
    whole = jax.ShapeDtypeStruct((rows * len(chosen), out), f32)
    out_shape, out_specs = whole, vmem
    if kind == "hop":
        out_shape = (
            jax.ShapeDtypeStruct((rows, out), jnp.bfloat16),
            jax.ShapeDtypeStruct((SUB, rows), f32),
        )
        out_specs = (vmem, vmem)
    elif kind == "out":
        out_shape = jax.ShapeDtypeStruct((1, len(done) + 1, rows, out), f32)
    out_tile = 4 * LANES if out % (4 * LANES) == 0 else LANES
    in_specs = [vmem] * len(operands)
    in_specs[len(flat)] = pl.BlockSpec(memory_space=pl.ANY)
    return pl.pallas_call(
        functools.partial(mix_body, kind, chosen, counts, out_tile),
        out_shape=out_shape,
        in_specs=[pl.BlockSpec(memory_space=pltpu.SMEM)] + in_specs,
        out_specs=out_specs,
        scratch_shapes=[
            pltpu.VMEM((len(pieces), depth, out), weight.dtype),
            pltpu.SemaphoreType.DMA((len(pieces) * (out // out_tile),)),
        ],
        compiler_params=params(),
        cost_estimate=cost(
            2 * rows * len(chosen) * depth * out * len(pieces), 2 * depth * out * len(pieces)
        ),
    )(blocks, *operands)


def ring_order(count):
    return list(range(0, 1)) + list(range(1, count, 2)) + list(range(2, count, 2))[::-1]


def local(token_ids, leading_span_index, embed_table, norm_gain, decay_rates, residues, history, mix_weight):
    section_rank = lax.axis_index("section")
    sections = lax.axis_size("section")
    seq_rank = lax.axis_index("seq")
    seqs = lax.axis_size("seq")
    tensor_rank = lax.axis_index("tensor")
    tensors = lax.axis_size("tensor")
    rates, resid, cache, weight = decay_rates[0], residues[0], history[0], mix_weight[0]
    spans, _ = token_ids.shape
    slots, _, _ = cache.shape
    half = weight.shape[1]
    channels = weight.shape[0]
    slot_total = slots * seqs
    order = ring_order(tensors)
    place = jnp.array([order.index(t) for t in range(tensors)], jnp.int32)[tensor_rank]
    order_array = jnp.array(order, jnp.int32)

    def along_ring(value, shift):
        return lax.ppermute(
            value, "tensor", [(order[i], order[(i + shift) % tensors]) for i in range(tensors)]
        )

    def swapped(value):
        return lax.ppermute(value, "seq", [(i, seqs - 1 - i) for i in range(seqs)])

    def to_next(value):
        return lax.ppermute(value, "section", [(i, (i + 1) % sections) for i in range(sections)])

    def to_next_shifted(value, shift):
        route = []
        for i in range(tensors):
            for s in range(sections):
                here = order[i] * sections + s
                there = order[(i + shift) % tensors] * sections + (s + 1) % sections
                route.append((here, there))
        return lax.ppermute(value, ("tensor", "section"), route)

    first_span = lax.rem(leading_span_index[0], slot_total)
    is_first = (section_rank == 0).astype(jnp.int32)
    meta = jnp.stack([first_span, seq_rank, is_first]).astype(jnp.int32)

    base, sums = embed_rows(token_ids, meta, embed_table, half)
    small_ring = tensors <= 8
    first_sums = [sums]
    if small_ring:
        for k in range(1, tensors):
            first_sums.append(along_ring(sums, k))
    else:
        first_sums = [lax.psum(sums, "tensor")]
    states, taps, *modes_here = history_states(meta, cache, rates, resid, half, slot_total)
    partner = swapped(states[0])

    blocks = []
    for k in range(tensors):
        source = order_array[lax.rem(place - k + tensors, tensors)]
        blocks.append(
            jnp.stack([source * seqs + seq_rank, source * seqs + seqs - 1 - seq_rank, is_first])
        )

    every = tuple(range(spans))
    deltas = [None] * spans
    later_sums = [[]] * spans
    order_all = jnp.stack([jnp.int32(0), is_first])
    for stage in range(sections):
        last_stage = stage + 1 == sections
        gates = []
        before = []
        for span in every:
            got = gate(
                meta, base, deltas[span], norm_gain, modes_here, taps, first_sums,
                later_sums[span], [states, partner], before, channels, span,
            )
            gates.append(got[0])
            before = list(got[1:])
        acc = None
        moving = list(gates)
        results = []
        steps = tensors if small_ring else 1
        for k in range(steps):
            final = k + 1 == steps
            if small_ring:
                rows_of = blocks[k]
                crossed = []
                for span in every:
                    crossed.append(swapped(moving[span]))
                pairs = [list(moving), crossed]
                if not final:
                    for span in every:
                        moving[span] = along_ring(moving[span], 1)
            else:
                rows_of = order_all
                pairs = [[lax.all_gather(g, ("tensor", "seq"), axis=1, tiled=True) for g in gates]]
            if not final:
                acc = mix("part", rows_of, pairs, every, weight, acc, None, None)
                continue
            for span in every:
                kind = "hop" if not last_stage else "out" if span + 1 == spans else "done"
                done = tuple(results) if kind == "out" else ()
                results.append(
                    mix(
                        kind, rows_of, [[part[span]] for part in pairs], (span,), weight, acc,
                        base, deltas[span], done,
                    )
                )
        if not last_stage:
            new_deltas, new_sums = [], []
            for span in every:
                moved, partial = results[span]
                new_deltas.append(to_next(moved))
                both = partial + swapped(partial)
                if small_ring:
                    got = []
                    for k in range(tensors):
                        got.append(to_next_shifted(both, k))
                    new_sums.append(got)
                else:
                    new_sums.append([to_next(lax.psum(both, "tensor"))])
            deltas, later_sums = new_deltas, new_sums
    return results[-1]


def solution(mesh):
    placed = (
        P("groups", None),
        P("groups"),
        P(None, "tensor"),
        P("section", "tensor"),
        P("section", None, "tensor"),
        P("section", None, "tensor"),
        P("section", "seq", "groups", "tensor"),
        P("section", None, ("tensor", "seq")),
    )
    return jax.shard_map(
        local,
        mesh=mesh,
        in_specs=placed,
        out_specs=P("section", None, "groups", ("tensor", "seq")),
        check_vma=False,
    )
```

profile of v0, /device:TPU:1, one launch (start us, length us, event | category | flops | bytes accessed | tf_op | source)
XLA Modules:
  0.0 143.6 jit_solution(2232404855055868104)
XLA Ops:
  0.8 7.0 %history_states.1 = (f32[2,2,16,1024]{3,2,1,0:T(8,128)S(1)}, f32[96,1024]{1,0:T(8,128)S(1)}, f32[16,1024]{1,0:T(8,128)S(1)}, f32[16,1024]{1,0:T(8,128)S(1)}) custom-call(s32[3]{0:T(128)S(1)} %add_add_fusion.1.meta, f32[4,96,2048]{2,1,0:T(8,128)} %bitcast.39, f32[16,2048]{1,0:T(8,128)} %bitcast.40, f32[16,2048]{1,0:T(8,128)} %bitcast.41), custom_call_target="tpu_custom_call" | custom-call | flops 25165824 | bytes 3145728 | tf_op jit(solution)/shard_map/history_states/pallas_call | solution.py:216
  8.5 4.4 %embed_rows.1 = (f32[2,96,1024]{2,1,0:T(8,128)S(1)}, f32[2,8,96]{2,1,0:T(8,128)S(1)}) custom-call(s32[2,96]{1,0:T(2,128)S(1)} %copy-done.1, s32[3]{0:T(128)S(1)} %add_add_fusion.1.meta, f32[512,2048]{1,0:T(8,128)} %table.1), custom_call_target="tpu_custom_call" | custom-call | flops 1572864 | bytes 4194304 | tf_op jit(solution)/shard_map/embed_rows/pallas_call | solution.py:80
  13.0 2.8 %collective-permute-start.1 = (f32[2,8,96]{2,1,0:T(8,128)S(1)}, f32[2,8,96]{2,1,0:T(8,128)S(1)}, u32[]{:S(2)}, u32[]{:S(2)}) collective-permute-start(f32[2,8,96]{2,1,0:T(8,128)S(1)} %get-tuple-element.24.rest_6_.rest_7_), channel_id=1, source_target_pairs={{0,4},{4,12},{12,8},{8,0},{1,5},{5,13},{13,9},{9,1},{2,6},{6,14},{... | collective-permute-start | bytes 18440 | tf_op jit(solution)/shard_map/ppermute | solution.py:476
  15.8 2.2 %collective-permute-start.2 = (f32[2,8,96]{2,1,0:T(8,128)S(1)}, f32[2,8,96]{2,1,0:T(8,128)S(1)}, u32[]{:S(2)}, u32[]{:S(2)}) collective-permute-start(f32[2,8,96]{2,1,0:T(8,128)S(1)} %get-tuple-element.24.rest_6_.rest_7_), channel_id=1, source_target_pairs={{0,12},{4,8},{12,0},{8,4},{1,13},{5,9},{13,1},{9,5},{2,14},{6,10},... | collective-permute-start | bytes 18440 | tf_op jit(solution)/shard_map/ppermute | solution.py:476
  18.0 1.3 collective-permute-start.3
  20.8 2.7 %gate.4 = (bf16[96,1024]{1,0:T(8,128)(2,1)S(1)}, f32[96,1024]{1,0:T(8,128)S(1)}) custom-call(s32[3]{0:T(128)S(1)} %add_add_fusion.1.meta, f32[2,96,1024]{2,1,0:T(8,128)S(1)} %get-tuple-element.19.base.refs_4_, f32[1,2048]{1,0:T(1,128)S(1)} %copy-done, f32[16,1024]{1,0:T(8,128)S(1)} %get-tuple-element.20.rest_1_.rest_2_, ...), custom_call_target="tpu_custom_call" | custom-call | flops 15728640 | bytes 1179648 | tf_op jit(solution)/shard_map/gate/pallas_call | solution.py:343
  23.5 3.2 %gate.5.refs_1_ = bf16[96,1024]{1,0:T(8,128)(2,1)S(1)} custom-call(s32[3]{0:T(128)S(1)} %add_add_fusion.1.meta, f32[2,96,1024]{2,1,0:T(8,128)S(1)} %get-tuple-element.19.base.refs_4_, f32[1,2048]{1,0:T(1,128)S(1)} %copy-done, f32[16,1024]{1,0:T(8,128)S(1)} %get-tuple-element.20.rest_1_.rest_2_, f32[16,1024]{1,0:T(8,128)S(1)} %get-tuple-element.21.rest_2_.rest_3_, ...), custom_call_target="tpu_custom_call" | custom-call | flops 15728640 | bytes 1179648 | tf_op jit(solution)/shard_map/gate/pallas_call | solution.py:343
  27.4 1.1 collective-permute-start.8
  34.3 2.0 %collective-permute-start.15 = (bf16[96,1024]{1,0:T(8,128)(2,1)S(1)}, bf16[96,1024]{1,0:T(8,128)(2,1)S(1)}, u32[]{:S(2)}, u32[]{:S(2)}) collective-permute-start(bf16[96,1024]{1,0:T(8,128)(2,1)S(1)} %gate.5.refs_1_), channel_id=1, source_target_pairs={{0,1},{1,0},{2,3},{3,2},{4,5},{5,4},{6,7},{7,6},{8,9},{9,8},{10,11... | collective-permute-start | bytes 589832 | tf_op jit(solution)/shard_map/ppermute | solution.py:481
  36.3 1.9 %collective-permute-start.5 = (bf16[96,1024]{1,0:T(8,128)(2,1)S(1)}, bf16[96,1024]{1,0:T(8,128)(2,1)S(1)}, u32[]{:S(2)}, u32[]{:S(2)}) collective-permute-start(bf16[96,1024]{1,0:T(8,128)(2,1)S(1)} %collective-permute-done.4.refs_1_), channel_id=1, source_target_pairs={{0,4},{4,12},{12,8},{8,0},{1,5},{5,13},{13,9},{9,1},{2,6},{6,14},{... | collective-permute-start | bytes 589832 | tf_op jit(solution)/shard_map/ppermute | solution.py:476
  38.4 0.9 collective-permute-start.14
  39.9 7.5 %collective-permute-done.9.refs_0_ = bf16[96,1024]{1,0:T(8,128)(2,1)S(1)} collective-permute-done((bf16[96,1024]{1,0:T(8,128)(2,1)S(1)}, bf16[96,1024]{1,0:T(8,128)(2,1)S(1)}, u32[]{:S(2)}, u32[]{:S(2)}) %collective-permute-start.9) | collective-permute-done | bytes 196640 | tf_op jit(solution)/shard_map/ppermute | solution.py:476
  47.4 1.3 collective-permute-start.22
  48.7 0.9 collective-permute-start.6
  50.4 1.7 %collective-permute-start.11 = (bf16[96,1024]{1,0:T(8,128)(2,1)S(1)}, bf16[96,1024]{1,0:T(8,128)(2,1)S(1)}, u32[]{:S(2)}, u32[]{:S(2)}) collective-permute-start(bf16[96,1024]{1,0:T(8,128)(2,1)S(1)} %collective-permute-done.5.refs_1_), channel_id=1, source_target_pairs={{0,1},{1,0},{2,3},{3,2},{4,5},{5,4},{6,7},{7,6},{8,9},{9,8},{10,11... | collective-permute-start | bytes 589832 | tf_op jit(solution)/shard_map/ppermute | solution.py:481
  52.2 1.2 collective-permute-done.22.refs_0_
  53.5 3.9 %collective-permute-start.23 = (bf16[96,1024]{1,0:T(8,128)(2,1)S(1)}, bf16[96,1024]{1,0:T(8,128)(2,1)S(1)}, u32[]{:S(2)}, u32[]{:S(2)}) collective-permute-start(bf16[96,1024]{1,0:T(8,128)(2,1)S(1)} %collective-permute-done.22.refs_0_), channel_id=1, source_target_pairs={{0,1},{1,0},{2,3},{3,2},{4,5},{5,4},{6,7},{7,6},{8,9},{9,8},{10,11... | collective-permute-start | bytes 589832 | tf_op jit(solution)/shard_map/ppermute | solution.py:481
  57.7 2.2 %collective-permute-start.7 = (bf16[96,1024]{1,0:T(8,128)(2,1)S(1)}, bf16[96,1024]{1,0:T(8,128)(2,1)S(1)}, u32[]{:S(2)}, u32[]{:S(2)}) collective-permute-start(bf16[96,1024]{1,0:T(8,128)(2,1)S(1)} %collective-permute-done.6.refs_0_), channel_id=1, source_target_pairs={{0,1},{1,0},{2,3},{3,2},{4,5},{5,4},{6,7},{7,6},{8,9},{9,8},{10,11... | collective-permute-start | bytes 589832 | tf_op jit(solution)/shard_map/ppermute | solution.py:481
  59.8 3.7 %shard_map.100.refs_5_ = f32[192,1024]{1,0:T(8,128)S(1)} custom-call(s32[3]{0:T(128)S(1)} %add_add_fusion.4.blocks, bf16[96,1024]{1,0:T(8,128)(2,1)S(1)} %get-tuple-element.26.refs_0_, bf16[96,1024]{1,0:T(8,128)(2,1)S(1)} %gate.5.refs_1_, bf16[96,1024]{1,0:T(8,128)(2,1)} %collective-permute-done.14.refs_2_, ...), custom_call_target="tpu_custom_call" | custom-call | flops 805306368 | bytes 4194304 | tf_op jit(solution)/shard_map/pallas_call | solution.py:438
  63.6 3.8 %shard_map.101.refs_5_ = f32[192,1024]{1,0:T(8,128)S(1)} custom-call(s32[3]{0:T(128)S(1)} %add_add_fusion.3.blocks, bf16[96,1024]{1,0:T(8,128)(2,1)S(1)} %collective-permute-done.8.refs_0_, bf16[96,1024]{1,0:T(8,128)(2,1)S(1)} %collective-permute-done.4.refs_1_, bf16[96,1024]{1,0:T(8,128)(2,1)} %collective-permute-done.12.refs_2_, ...), custom_call_target="tpu_custom_call" | custom-call | flops 805306368 | bytes 4194304 | tf_op jit(solution)/shard_map/pallas_call | solution.py:438
  67.4 3.3 %shard_map.102.refs_3_ = f32[192,1024]{1,0:T(8,128)S(1)} custom-call(s32[3]{0:T(128)S(1)} %add_add_fusion.2.blocks, bf16[96,1024]{1,0:T(8,128)(2,1)S(1)} %collective-permute-done.9.refs_0_, bf16[96,1024]{1,0:T(8,128)(2,1)S(1)} %collective-permute-done.5.refs_1_, bf16[96,1024]{1,0:T(8,128)(2,1)S(1)} %collective-permute-done.10.refs_2_, ...), custom_call_target="tpu_custom_call" | custom-call | flops 805306368 | bytes 4194304 | tf_op jit(solution)/shard_map/pallas_call | solution.py:438
  70.8 3.5 %shard_map.104 = (bf16[96,1024]{1,0:T(8,128)(2,1)S(1)}, f32[8,96]{1,0:T(8,128)S(1)}) custom-call(s32[3]{0:T(128)S(1)} %add_add_fusion.blocks, bf16[96,1024]{1,0:T(8,128)(2,1)S(1)} %collective-permute-done.22.refs_0_, bf16[96,1024]{1,0:T(8,128)(2,1)S(1)} %collective-permute-done.23.refs_1_, bf16[8192,1024]{1,0:T(8,128)(2,1)} %bitcast.32, ...), custom_call_target="tpu_custom_call" | custom-call | flops 402653184 | bytes 4194304 | tf_op jit(solution)/shard_map/pallas_call | solution.py:438
  74.3 1.3 collective-permute-start.24
  75.6 3.5 %shard_map.103 = (bf16[96,1024]{1,0:T(8,128)(2,1)S(1)}, f32[8,96]{1,0:T(8,128)S(1)}) custom-call(s32[3]{0:T(128)S(1)} %add_add_fusion.blocks, bf16[96,1024]{1,0:T(8,128)(2,1)S(1)} %collective-permute-done.6.refs_0_, bf16[96,1024]{1,0:T(8,128)(2,1)S(1)} %collective-permute-done.7.refs_1_, bf16[8192,1024]{1,0:T(8,128)(2,1)} %bitcast.33, ...), custom_call_target="tpu_custom_call" | custom-call | flops 402653184 | bytes 4194304 | tf_op jit(solution)/shard_map/pallas_call | solution.py:438
  79.9 0.8 collective-permute-done.25
  80.8 1.2 collective-permute-start.26
  82.4 1.6 %collective-permute-start.28 = (f32[8,96]{1,0:T(8,128)S(1)}, f32[8,96]{1,0:T(8,128)S(1)}, u32[]{:S(2)}, u32[]{:S(2)}) collective-permute-start(f32[8,96]{1,0:T(8,128)S(1)} %add.100), channel_id=1, source_target_pairs={{0,14},{2,12},{4,10},{6,8},{12,2},{14,0},{8,6},{10,4},{1,15},{3,13... | collective-permute-start | bytes 9224 | tf_op jit(solution)/shard_map/ppermute | solution.py:493
  84.0 1.4 collective-permute-done.26.rest_11_
  85.4 0.9 collective-permute-start.29
  86.3 1.2 collective-permute-start.18
  87.5 1.2 collective-permute-start.19
  89.0 2.4 %collective-permute-start.20 = (f32[8,96]{1,0:T(8,128)S(1)}, f32[8,96]{1,0:T(8,128)S(1)}, u32[]{:S(2)}, u32[]{:S(2)}) collective-permute-start(f32[8,96]{1,0:T(8,128)S(1)} %add.99), channel_id=1, source_target_pairs={{0,14},{2,12},{4,10},{6,8},{12,2},{14,0},{8,6},{10,4},{1,15},{3,13... | collective-permute-start | bytes 9224 | tf_op jit(solution)/shard_map/ppermute | solution.py:493
  92.2 2.7 %gate.6 = (bf16[96,1024]{1,0:T(8,128)(2,1)S(1)}, f32[96,1024]{1,0:T(8,128)S(1)}) custom-call(s32[3]{0:T(128)S(1)} %add_add_fusion.1.meta, f32[2,96,1024]{2,1,0:T(8,128)S(1)} %get-tuple-element.19.base.refs_4_, bf16[96,1024]{1,0:T(8,128)(2,1)S(1)} %collective-permute-done.24.rest_0_.refs_5_, f32[1,2048]{1,0:T(1,128)S(1)} %copy-done, ...), custom_call_target="tpu_custom_call" | custom-call | flops 15728640 | bytes 1179648 | tf_op jit(solution)/shard_map/gate/pallas_call | solution.py:343
  95.0 0.9 collective-permute-start.34
  95.9 3.2 %gate.7.refs_1_ = bf16[96,1024]{1,0:T(8,128)(2,1)S(1)} custom-call(s32[3]{0:T(128)S(1)} %add_add_fusion.1.meta, f32[2,96,1024]{2,1,0:T(8,128)S(1)} %get-tuple-element.19.base.refs_4_, bf16[96,1024]{1,0:T(8,128)(2,1)S(1)} %collective-permute-done.16.rest_0_.refs_5_, f32[1,2048]{1,0:T(1,128)S(1)} %copy-done, f32[16,1024]{1,0:T(8,128)S(1)} %get-tuple-element.20.rest_1_.rest_2_, ...), custom_call_target="tpu_custom_call" | custom-call | flops 15728640 | bytes 1179648 | tf_op jit(solution)/shard_map/gate/pallas_call | solution.py:343
  99.1 1.3 collective-permute-start.30
  101.1 4.8 %collective-permute-done.30.refs_1_ = bf16[96,1024]{1,0:T(8,128)(2,1)S(1)} collective-permute-done((bf16[96,1024]{1,0:T(8,128)(2,1)S(1)}, bf16[96,1024]{1,0:T(8,128)(2,1)S(1)}, u32[]{:S(2)}, u32[]{:S(2)}) %collective-permute-start.30) | collective-permute-done | bytes 196640 | tf_op jit(solution)/shard_map/ppermute | solution.py:476
  105.8 5.9 %collective-permute-start.41 = (bf16[96,1024]{1,0:T(8,128)(2,1)S(1)}, bf16[96,1024]{1,0:T(8,128)(2,1)S(1)}, u32[]{:S(2)}, u32[]{:S(2)}) collective-permute-start(bf16[96,1024]{1,0:T(8,128)(2,1)S(1)} %gate.7.refs_1_), channel_id=1, source_target_pairs={{0,1},{1,0},{2,3},{3,2},{4,5},{5,4},{6,7},{7,6},{8,9},{9,8},{10,11... | collective-permute-start | bytes 589832 | tf_op jit(solution)/shard_map/ppermute | solution.py:481
  112.2 1.1 collective-permute-start.42
  113.4 0.9 collective-permute-done.31.refs_1_
  114.3 4.6 %collective-permute-start.38 = (bf16[96,1024]{1,0:T(8,128)(2,1)S(1)}, bf16[96,1024]{1,0:T(8,128)(2,1)S(1)}, u32[]{:S(2)}, u32[]{:S(2)}) collective-permute-start(bf16[96,1024]{1,0:T(8,128)(2,1)S(1)} %collective-permute-done.34.refs_0_), channel_id=1, source_target_pairs={{0,1},{1,0},{2,3},{3,2},{4,5},{5,4},{6,7},{7,6},{8,9},{9,8},{10,11... | collective-permute-start | bytes 589832 | tf_op jit(solution)/shard_map/ppermute | solution.py:481
  119.5 4.1 %collective-permute-start.43 = (bf16[96,1024]{1,0:T(8,128)(2,1)S(1)}, bf16[96,1024]{1,0:T(8,128)(2,1)S(1)}, u32[]{:S(2)}, u32[]{:S(2)}) collective-permute-start(bf16[96,1024]{1,0:T(8,128)(2,1)S(1)} %collective-permute-done.42.refs_0_), channel_id=1, source_target_pairs={{0,1},{1,0},{2,3},{3,2},{4,5},{5,4},{6,7},{7,6},{8,9},{9,8},{10,11... | collective-permute-start | bytes 589832 | tf_op jit(solution)/shard_map/ppermute | solution.py:481
  123.7 2.3 %collective-permute-start.33 = (bf16[96,1024]{1,0:T(8,128)(2,1)S(1)}, bf16[96,1024]{1,0:T(8,128)(2,1)S(1)}, u32[]{:S(2)}, u32[]{:S(2)}) collective-permute-start(bf16[96,1024]{1,0:T(8,128)(2,1)S(1)} %collective-permute-done.32.refs_0_), channel_id=1, source_target_pairs={{0,1},{1,0},{2,3},{3,2},{4,5},{5,4},{6,7},{7,6},{8,9},{9,8},{10,11... | collective-permute-start | bytes 589832 | tf_op jit(solution)/shard_map/ppermute | solution.py:481
  126.0 3.3 %shard_map.105.refs_5_ = f32[192,1024]{1,0:T(8,128)S(1)} custom-call(s32[3]{0:T(128)S(1)} %add_add_fusion.4.blocks, bf16[96,1024]{1,0:T(8,128)(2,1)S(1)} %get-tuple-element.32.refs_0_, bf16[96,1024]{1,0:T(8,128)(2,1)S(1)} %gate.7.refs_1_, bf16[96,1024]{1,0:T(8,128)(2,1)S(1)} %collective-permute-done.40.refs_2_, ...), custom_call_target="tpu_custom_call" | custom-call | flops 805306368 | bytes 4194304 | tf_op jit(solution)/shard_map/pallas_call | solution.py:438
  129.3 3.4 %shard_map.106.refs_5_ = f32[192,1024]{1,0:T(8,128)S(1)} custom-call(s32[3]{0:T(128)S(1)} %add_add_fusion.3.blocks, bf16[96,1024]{1,0:T(8,128)(2,1)S(1)} %collective-permute-done.34.refs_0_, bf16[96,1024]{1,0:T(8,128)(2,1)S(1)} %collective-permute-done.30.refs_1_, bf16[96,1024]{1,0:T(8,128)(2,1)S(1)} %collective-permute-done.38.refs_2_, ...), custom_call_target="tpu_custom_call" | custom-call | flops 805306368 | bytes 4194304 | tf_op jit(solution)/shard_map/pallas_call | solution.py:438
  132.7 3.4 %shard_map.107.refs_3_ = f32[192,1024]{1,0:T(8,128)S(1)} custom-call(s32[3]{0:T(128)S(1)} %add_add_fusion.2.blocks, bf16[96,1024]{1,0:T(8,128)(2,1)S(1)} %collective-permute-done.35.refs_0_, bf16[96,1024]{1,0:T(8,128)(2,1)S(1)} %collective-permute-done.31.refs_1_, bf16[96,1024]{1,0:T(8,128)(2,1)S(1)} %collective-permute-done.36.refs_2_, ...), custom_call_target="tpu_custom_call" | custom-call | flops 805306368 | bytes 4194304 | tf_op jit(solution)/shard_map/pallas_call | solution.py:438
  136.1 3.2 %shard_map.108.refs_6_ = f32[96,1024]{1,0:T(8,128)S(1)} custom-call(s32[3]{0:T(128)S(1)} %add_add_fusion.blocks, bf16[96,1024]{1,0:T(8,128)(2,1)S(1)} %collective-permute-done.42.refs_0_, bf16[96,1024]{1,0:T(8,128)(2,1)S(1)} %collective-permute-done.43.refs_1_, bf16[8192,1024]{1,0:T(8,128)(2,1)} %bitcast.37, f32[192,1024]{1,0:T(8,128)S(1)} %shard_map.107.refs_3_, ...), custom_call_target="tpu_custom_call" | custom-call | flops 402653184 | bytes 4194304 | tf_op jit(solution)/shard_map/pallas_call | solution.py:438
  139.3 4.1 %shard_map.109 = f32[1,2,96,1024]{3,2,1,0:T(8,128)} custom-call(s32[3]{0:T(128)S(1)} %add_add_fusion.blocks, bf16[96,1024]{1,0:T(8,128)(2,1)S(1)} %collective-permute-done.32.refs_0_, bf16[96,1024]{1,0:T(8,128)(2,1)S(1)} %collective-permute-done.33.refs_1_, bf16[8192,1024]{1,0:T(8,128)(2,1)} %bitcast.38, f32[192,1024]{1,0:T(8,128)S(1)} %shard_map.107.refs_3_, ...), custom_call_target="tpu_custom_call" | custom-call | flops 402653184 | bytes 4194304 | tf_op jit(solution)/shard_map/pallas_call | solution.py:438
  (72 shorter events, 10.0 us)
Async XLA Ops:
  0.0 20.8 %copy-start = (f32[1,2048]{1,0:T(1,128)S(1)}, f32[1,2048]{1,0:T(1,128)}, u32[]{:S(2)}) copy-start(f32[1,2048]{1,0:T(1,128)} %rest_1_.3) | copy-start | bytes 24580
  7.7 13.0 %collective-permute-start = (f32[2,16,1024]{2,1,0:T(8,128)S(1)}, f32[2,16,1024]{2,1,0:T(8,128)S(1)}, u32[]{:S(2)}, u32[]{:S(2)}) collective-permute-start(f32[2,16,1024]{2,1,0:T(8,128)S(1)} %slice_bitcast_fusion), channel_id=1, source_target_pairs={{0,1},{1,0},{2,3},{3,2},{4,5},{5,4},{6,7},{7,6},{8,9},{9,8},{10,11... | collective-permute-start | bytes 393224 | tf_op jit(solution)/shard_map/ppermute | solution.py:481
  7.8 0.7 copy-start.1
  8.5 20.0 %copy-start.2 = (s32[4]{0:T(128)S(1)}, s32[4]{0:T(128)}, u32[]{:S(2)}) copy-start(s32[4]{0:T(128)} %constant.60.clone) | copy-start | bytes 52
  13.0 6.3 %collective-permute-start.1 = (f32[2,8,96]{2,1,0:T(8,128)S(1)}, f32[2,8,96]{2,1,0:T(8,128)S(1)}, u32[]{:S(2)}, u32[]{:S(2)}) collective-permute-start(f32[2,8,96]{2,1,0:T(8,128)S(1)} %get-tuple-element.24.rest_6_.rest_7_), channel_id=1, source_target_pairs={{0,4},{4,12},{12,8},{8,0},{1,5},{5,13},{13,9},{9,1},{2,6},{6,14},{... | collective-permute-start | bytes 18440 | tf_op jit(solution)/shard_map/ppermute | solution.py:476
  15.8 4.3 %collective-permute-start.2 = (f32[2,8,96]{2,1,0:T(8,128)S(1)}, f32[2,8,96]{2,1,0:T(8,128)S(1)}, u32[]{:S(2)}, u32[]{:S(2)}) collective-permute-start(f32[2,8,96]{2,1,0:T(8,128)S(1)} %get-tuple-element.24.rest_6_.rest_7_), channel_id=1, source_target_pairs={{0,12},{4,8},{12,0},{8,4},{1,13},{5,9},{13,1},{9,5},{2,14},{6,10},... | collective-permute-start | bytes 18440 | tf_op jit(solution)/shard_map/ppermute | solution.py:476
  18.0 2.8 %collective-permute-start.3 = (f32[2,8,96]{2,1,0:T(8,128)S(1)}, f32[2,8,96]{2,1,0:T(8,128)S(1)}, u32[]{:S(2)}, u32[]{:S(2)}) collective-permute-start(f32[2,8,96]{2,1,0:T(8,128)S(1)} %get-tuple-element.24.rest_6_.rest_7_), channel_id=1, source_target_pairs={{0,8},{4,0},{12,4},{8,12},{1,9},{5,1},{13,5},{9,13},{2,10},{6,2},{... | collective-permute-start | bytes 18440 | tf_op jit(solution)/shard_map/ppermute | solution.py:476
  26.6 9.6 %collective-permute-start.4 = (bf16[96,1024]{1,0:T(8,128)(2,1)S(1)}, bf16[96,1024]{1,0:T(8,128)(2,1)S(1)}, u32[]{:S(2)}, u32[]{:S(2)}) collective-permute-start(bf16[96,1024]{1,0:T(8,128)(2,1)S(1)} %gate.5.refs_1_), channel_id=1, source_target_pairs={{0,4},{4,12},{12,8},{8,0},{1,5},{5,13},{13,9},{9,1},{2,6},{6,14},{... | collective-permute-start | bytes 589832 | tf_op jit(solution)/shard_map/ppermute | solution.py:476
  27.4 10.7 %collective-permute-start.8 = (bf16[96,1024]{1,0:T(8,128)(2,1)S(1)}, bf16[96,1024]{1,0:T(8,128)(2,1)S(1)}, u32[]{:S(2)}, u32[]{:S(2)}) collective-permute-start(bf16[96,1024]{1,0:T(8,128)(2,1)S(1)} %get-tuple-element.26.refs_0_), channel_id=1, source_target_pairs={{0,4},{4,12},{12,8},{8,0},{1,5},{5,13},{13,9},{9,1},{2,6},{6,14},{... | collective-permute-start | bytes 589832 | tf_op jit(solution)/shard_map/ppermute | solution.py:476
  34.3 5.2 %collective-permute-start.15 = (bf16[96,1024]{1,0:T(8,128)(2,1)S(1)}, bf16[96,1024]{1,0:T(8,128)(2,1)S(1)}, u32[]{:S(2)}, u32[]{:S(2)}) collective-permute-start(bf16[96,1024]{1,0:T(8,128)(2,1)S(1)} %gate.5.refs_1_), channel_id=1, source_target_pairs={{0,1},{1,0},{2,3},{3,2},{4,5},{5,4},{6,7},{7,6},{8,9},{9,8},{10,11... | collective-permute-start | bytes 589832 | tf_op jit(solution)/shard_map/ppermute | solution.py:481
  36.3 12.5 %collective-permute-start.5 = (bf16[96,1024]{1,0:T(8,128)(2,1)S(1)}, bf16[96,1024]{1,0:T(8,128)(2,1)S(1)}, u32[]{:S(2)}, u32[]{:S(2)}) collective-permute-start(bf16[96,1024]{1,0:T(8,128)(2,1)S(1)} %collective-permute-done.4.refs_1_), channel_id=1, source_target_pairs={{0,4},{4,12},{12,8},{8,0},{1,5},{5,13},{13,9},{9,1},{2,6},{6,14},{... | collective-permute-start | bytes 589832 | tf_op jit(solution)/shard_map/ppermute | solution.py:476
  38.1 9.3 %collective-permute-start.9 = (bf16[96,1024]{1,0:T(8,128)(2,1)S(1)}, bf16[96,1024]{1,0:T(8,128)(2,1)S(1)}, u32[]{:S(2)}, u32[]{:S(2)}) collective-permute-start(bf16[96,1024]{1,0:T(8,128)(2,1)S(1)} %collective-permute-done.8.refs_0_), channel_id=1, source_target_pairs={{0,4},{4,12},{12,8},{8,0},{1,5},{5,13},{13,9},{9,1},{2,6},{6,14},{... | collective-permute-start | bytes 589832 | tf_op jit(solution)/shard_map/ppermute | solution.py:476
  38.4 12.0 %collective-permute-start.14 = (bf16[96,1024]{1,0:T(8,128)(2,1)S(1)}, bf16[96,1024]{1,0:T(8,128)(2,1)}, u32[]{:S(2)}, u32[]{:S(2)}) collective-permute-start(bf16[96,1024]{1,0:T(8,128)(2,1)S(1)} %get-tuple-element.26.refs_0_), channel_id=1, source_target_pairs={{0,1},{1,0},{2,3},{3,2},{4,5},{5,4},{6,7},{7,6},{8,9},{9,8},{10,11... | collective-permute-start | bytes 589832 | tf_op jit(solution)/shard_map/ppermute | solution.py:481
  39.3 12.8 %collective-permute-start.13 = (bf16[96,1024]{1,0:T(8,128)(2,1)S(1)}, bf16[96,1024]{1,0:T(8,128)(2,1)}, u32[]{:S(2)}, u32[]{:S(2)}) collective-permute-start(bf16[96,1024]{1,0:T(8,128)(2,1)S(1)} %collective-permute-done.4.refs_1_), channel_id=1, source_target_pairs={{0,1},{1,0},{2,3},{3,2},{4,5},{5,4},{6,7},{7,6},{8,9},{9,8},{10,11... | collective-permute-start | bytes 589832 | tf_op jit(solution)/shard_map/ppermute | solution.py:481
  39.4 24.1 %collective-permute-start.12 = (bf16[96,1024]{1,0:T(8,128)(2,1)S(1)}, bf16[96,1024]{1,0:T(8,128)(2,1)}, u32[]{:S(2)}, u32[]{:S(2)}) collective-permute-start(bf16[96,1024]{1,0:T(8,128)(2,1)S(1)} %collective-permute-done.8.refs_0_), channel_id=1, source_target_pairs={{0,1},{1,0},{2,3},{3,2},{4,5},{5,4},{6,7},{7,6},{8,9},{9,8},{10,11... | collective-permute-start | bytes 589832 | tf_op jit(solution)/shard_map/ppermute | solution.py:481
  47.4 6.1 %collective-permute-start.22 = (bf16[96,1024]{1,0:T(8,128)(2,1)S(1)}, bf16[96,1024]{1,0:T(8,128)(2,1)S(1)}, u32[]{:S(2)}, u32[]{:S(2)}) collective-permute-start(bf16[96,1024]{1,0:T(8,128)(2,1)S(1)} %collective-permute-done.9.refs_0_), channel_id=1, source_target_pairs={{0,4},{4,12},{12,8},{8,0},{1,5},{5,13},{13,9},{9,1},{2,6},{6,14},{... | collective-permute-start | bytes 589832 | tf_op jit(solution)/shard_map/ppermute | solution.py:476
  48.7 9.0 %collective-permute-start.6 = (bf16[96,1024]{1,0:T(8,128)(2,1)S(1)}, bf16[96,1024]{1,0:T(8,128)(2,1)S(1)}, u32[]{:S(2)}, u32[]{:S(2)}) collective-permute-start(bf16[96,1024]{1,0:T(8,128)(2,1)S(1)} %collective-permute-done.5.refs_1_), channel_id=1, source_target_pairs={{0,4},{4,12},{12,8},{8,0},{1,5},{5,13},{13,9},{9,1},{2,6},{6,14},{... | collective-permute-start | bytes 589832 | tf_op jit(solution)/shard_map/ppermute | solution.py:476
  50.4 17.1 %collective-permute-start.11 = (bf16[96,1024]{1,0:T(8,128)(2,1)S(1)}, bf16[96,1024]{1,0:T(8,128)(2,1)S(1)}, u32[]{:S(2)}, u32[]{:S(2)}) collective-permute-start(bf16[96,1024]{1,0:T(8,128)(2,1)S(1)} %collective-permute-done.5.refs_1_), channel_id=1, source_target_pairs={{0,1},{1,0},{2,3},{3,2},{4,5},{5,4},{6,7},{7,6},{8,9},{9,8},{10,11... | collective-permute-start | bytes 589832 | tf_op jit(solution)/shard_map/ppermute | solution.py:481
  52.1 15.4 %collective-permute-start.10 = (bf16[96,1024]{1,0:T(8,128)(2,1)S(1)}, bf16[96,1024]{1,0:T(8,128)(2,1)S(1)}, u32[]{:S(2)}, u32[]{:S(2)}) collective-permute-start(bf16[96,1024]{1,0:T(8,128)(2,1)S(1)} %collective-permute-done.9.refs_0_), channel_id=1, source_target_pairs={{0,1},{1,0},{2,3},{3,2},{4,5},{5,4},{6,7},{7,6},{8,9},{9,8},{10,11... | collective-permute-start | bytes 589832 | tf_op jit(solution)/shard_map/ppermute | solution.py:481
  53.5 17.3 %collective-permute-start.23 = (bf16[96,1024]{1,0:T(8,128)(2,1)S(1)}, bf16[96,1024]{1,0:T(8,128)(2,1)S(1)}, u32[]{:S(2)}, u32[]{:S(2)}) collective-permute-start(bf16[96,1024]{1,0:T(8,128)(2,1)S(1)} %collective-permute-done.22.refs_0_), channel_id=1, source_target_pairs={{0,1},{1,0},{2,3},{3,2},{4,5},{5,4},{6,7},{7,6},{8,9},{9,8},{10,11... | collective-permute-start | bytes 589832 | tf_op jit(solution)/shard_map/ppermute | solution.py:481
  57.7 17.9 %collective-permute-start.7 = (bf16[96,1024]{1,0:T(8,128)(2,1)S(1)}, bf16[96,1024]{1,0:T(8,128)(2,1)S(1)}, u32[]{:S(2)}, u32[]{:S(2)}) collective-permute-start(bf16[96,1024]{1,0:T(8,128)(2,1)S(1)} %collective-permute-done.6.refs_0_), channel_id=1, source_target_pairs={{0,1},{1,0},{2,3},{3,2},{4,5},{5,4},{6,7},{7,6},{8,9},{9,8},{10,11... | collective-permute-start | bytes 589832 | tf_op jit(solution)/shard_map/ppermute | solution.py:481
  74.3 17.1 %collective-permute-start.24 = (bf16[96,1024]{1,0:T(8,128)(2,1)S(1)}, bf16[96,1024]{1,0:T(8,128)(2,1)S(1)}, u32[]{:S(2)}, u32[]{:S(2)}) collective-permute-start(bf16[96,1024]{1,0:T(8,128)(2,1)S(1)} %get-tuple-element.29), channel_id=1, source_target_pairs={{0,2},{2,0},{1,3},{3,1},{4,6},{6,4},{5,7},{7,5},{8,10},{10,8},{9,1... | collective-permute-start | bytes 589832 | tf_op jit(solution)/shard_map/ppermute | solution.py:484
  79.1 16.8 %collective-permute-start.16 = (bf16[96,1024]{1,0:T(8,128)(2,1)S(1)}, bf16[96,1024]{1,0:T(8,128)(2,1)S(1)}, u32[]{:S(2)}, u32[]{:S(2)}) collective-permute-start(bf16[96,1024]{1,0:T(8,128)(2,1)S(1)} %get-tuple-element.27), channel_id=1, source_target_pairs={{0,2},{2,0},{1,3},{3,1},{4,6},{6,4},{5,7},{7,5},{8,10},{10,8},{9,1... | collective-permute-start | bytes 589832 | tf_op jit(solution)/shard_map/ppermute | solution.py:484
  79.4 1.4 collective-permute-start.25
  79.9 2.4 %collective-permute-start.17 = (f32[8,96]{1,0:T(8,128)S(1)}, f32[8,96]{1,0:T(8,128)S(1)}, u32[]{:S(2)}, u32[]{:S(2)}) collective-permute-start(f32[8,96]{1,0:T(8,128)S(1)} %get-tuple-element.28), channel_id=1, source_target_pairs={{0,1},{1,0},{2,3},{3,2},{4,5},{5,4},{6,7},{7,6},{8,9},{9,8},{10,11... | collective-permute-start | bytes 9224 | tf_op jit(solution)/shard_map/ppermute | solution.py:481
  80.8 4.6 %collective-permute-start.26 = (f32[8,96]{1,0:T(8,128)S(1)}, f32[8,96]{1,0:T(8,128)S(1)}, u32[]{:S(2)}, u32[]{:S(2)}) collective-permute-start(f32[8,96]{1,0:T(8,128)S(1)} %add.100), channel_id=1, source_target_pairs={{0,2},{2,0},{4,6},{6,4},{12,14},{14,12},{8,10},{10,8},{1,3},{3,1},... | collective-permute-start | bytes 9224 | tf_op jit(solution)/shard_map/ppermute | solution.py:493
  82.0 4.3 %collective-permute-start.27 = (f32[8,96]{1,0:T(8,128)S(1)}, f32[8,96]{1,0:T(8,128)S(1)}, u32[]{:S(2)}, u32[]{:S(2)}) collective-permute-start(f32[8,96]{1,0:T(8,128)S(1)} %add.100), channel_id=1, source_target_pairs={{0,6},{2,4},{4,14},{6,12},{12,10},{14,8},{8,2},{10,0},{1,7},{3,5},... | collective-permute-start | bytes 9224 | tf_op jit(solution)/shard_map/ppermute | solution.py:493
  82.4 5.2 %collective-permute-start.28 = (f32[8,96]{1,0:T(8,128)S(1)}, f32[8,96]{1,0:T(8,128)S(1)}, u32[]{:S(2)}, u32[]{:S(2)}) collective-permute-start(f32[8,96]{1,0:T(8,128)S(1)} %add.100), channel_id=1, source_target_pairs={{0,14},{2,12},{4,10},{6,8},{12,2},{14,0},{8,6},{10,4},{1,15},{3,13... | collective-permute-start | bytes 9224 | tf_op jit(solution)/shard_map/ppermute | solution.py:493
  85.4 3.7 %collective-permute-start.29 = (f32[8,96]{1,0:T(8,128)S(1)}, f32[8,96]{1,0:T(8,128)S(1)}, u32[]{:S(2)}, u32[]{:S(2)}) collective-permute-start(f32[8,96]{1,0:T(8,128)S(1)} %add.100), channel_id=1, source_target_pairs={{0,10},{2,8},{4,2},{6,0},{12,6},{14,4},{8,14},{10,12},{1,11},{3,9}... | collective-permute-start | bytes 9224 | tf_op jit(solution)/shard_map/ppermute | solution.py:493
  86.3 8.7 %collective-permute-start.18 = (f32[8,96]{1,0:T(8,128)S(1)}, f32[8,96]{1,0:T(8,128)S(1)}, u32[]{:S(2)}, u32[]{:S(2)}) collective-permute-start(f32[8,96]{1,0:T(8,128)S(1)} %add.99), channel_id=1, source_target_pairs={{0,2},{2,0},{4,6},{6,4},{12,14},{14,12},{8,10},{10,8},{1,3},{3,1},... | collective-permute-start | bytes 9224 | tf_op jit(solution)/shard_map/ppermute | solution.py:493
  87.5 8.4 %collective-permute-start.19 = (f32[8,96]{1,0:T(8,128)S(1)}, f32[8,96]{1,0:T(8,128)S(1)}, u32[]{:S(2)}, u32[]{:S(2)}) collective-permute-start(f32[8,96]{1,0:T(8,128)S(1)} %add.99), channel_id=1, source_target_pairs={{0,6},{2,4},{4,14},{6,12},{12,10},{14,8},{8,2},{10,0},{1,7},{3,5},... | collective-permute-start | bytes 9224 | tf_op jit(solution)/shard_map/ppermute | solution.py:493
  89.0 6.9 %collective-permute-start.20 = (f32[8,96]{1,0:T(8,128)S(1)}, f32[8,96]{1,0:T(8,128)S(1)}, u32[]{:S(2)}, u32[]{:S(2)}) collective-permute-start(f32[8,96]{1,0:T(8,128)S(1)} %add.99), channel_id=1, source_target_pairs={{0,14},{2,12},{4,10},{6,8},{12,2},{14,0},{8,6},{10,4},{1,15},{3,13... | collective-permute-start | bytes 9224 | tf_op jit(solution)/shard_map/ppermute | solution.py:493
  91.4 4.5 %collective-permute-start.21 = (f32[8,96]{1,0:T(8,128)S(1)}, f32[8,96]{1,0:T(8,128)S(1)}, u32[]{:S(2)}, u32[]{:S(2)}) collective-permute-start(f32[8,96]{1,0:T(8,128)S(1)} %add.99), channel_id=1, source_target_pairs={{0,10},{2,8},{4,2},{6,0},{12,6},{14,4},{8,14},{10,12},{1,11},{3,9}... | collective-permute-start | bytes 9224 | tf_op jit(solution)/shard_map/ppermute | solution.py:493
  95.0 5.5 %collective-permute-start.34 = (bf16[96,1024]{1,0:T(8,128)(2,1)S(1)}, bf16[96,1024]{1,0:T(8,128)(2,1)S(1)}, u32[]{:S(2)}, u32[]{:S(2)}) collective-permute-start(bf16[96,1024]{1,0:T(8,128)(2,1)S(1)} %get-tuple-element.32.refs_0_), channel_id=1, source_target_pairs={{0,4},{4,12},{12,8},{8,0},{1,5},{5,13},{13,9},{9,1},{2,6},{6,14},{... | collective-permute-start | bytes 589832 | tf_op jit(solution)/shard_map/ppermute | solution.py:476
  99.1 6.7 %collective-permute-start.30 = (bf16[96,1024]{1,0:T(8,128)(2,1)S(1)}, bf16[96,1024]{1,0:T(8,128)(2,1)S(1)}, u32[]{:S(2)}, u32[]{:S(2)}) collective-permute-start(bf16[96,1024]{1,0:T(8,128)(2,1)S(1)} %gate.7.refs_1_), channel_id=1, source_target_pairs={{0,4},{4,12},{12,8},{8,0},{1,5},{5,13},{13,9},{9,1},{2,6},{6,14},{... | collective-permute-start | bytes 589832 | tf_op jit(solution)/shard_map/ppermute | solution.py:476
  100.5 11.7 %collective-permute-start.35 = (bf16[96,1024]{1,0:T(8,128)(2,1)S(1)}, bf16[96,1024]{1,0:T(8,128)(2,1)S(1)}, u32[]{:S(2)}, u32[]{:S(2)}) collective-permute-start(bf16[96,1024]{1,0:T(8,128)(2,1)S(1)} %collective-permute-done.34.refs_0_), channel_id=1, source_target_pairs={{0,4},{4,12},{12,8},{8,0},{1,5},{5,13},{13,9},{9,1},{2,6},{6,14},{... | collective-permute-start | bytes 589832 | tf_op jit(solution)/shard_map/ppermute | solution.py:476
  105.8 8.5 %collective-permute-start.31 = (bf16[96,1024]{1,0:T(8,128)(2,1)S(1)}, bf16[96,1024]{1,0:T(8,128)(2,1)S(1)}, u32[]{:S(2)}, u32[]{:S(2)}) collective-permute-start(bf16[96,1024]{1,0:T(8,128)(2,1)S(1)} %collective-permute-done.30.refs_1_), channel_id=1, source_target_pairs={{0,4},{4,12},{12,8},{8,0},{1,5},{5,13},{13,9},{9,1},{2,6},{6,14},{... | collective-permute-start | bytes 589832 | tf_op jit(solution)/shard_map/ppermute | solution.py:476
  105.8 8.5 %collective-permute-start.41 = (bf16[96,1024]{1,0:T(8,128)(2,1)S(1)}, bf16[96,1024]{1,0:T(8,128)(2,1)S(1)}, u32[]{:S(2)}, u32[]{:S(2)}) collective-permute-start(bf16[96,1024]{1,0:T(8,128)(2,1)S(1)} %gate.7.refs_1_), channel_id=1, source_target_pairs={{0,1},{1,0},{2,3},{3,2},{4,5},{5,4},{6,7},{7,6},{8,9},{9,8},{10,11... | collective-permute-start | bytes 589832 | tf_op jit(solution)/shard_map/ppermute | solution.py:481
  111.7 7.2 %collective-permute-start.40 = (bf16[96,1024]{1,0:T(8,128)(2,1)S(1)}, bf16[96,1024]{1,0:T(8,128)(2,1)S(1)}, u32[]{:S(2)}, u32[]{:S(2)}) collective-permute-start(bf16[96,1024]{1,0:T(8,128)(2,1)S(1)} %get-tuple-element.32.refs_0_), channel_id=1, source_target_pairs={{0,1},{1,0},{2,3},{3,2},{4,5},{5,4},{6,7},{7,6},{8,9},{9,8},{10,11... | collective-permute-start | bytes 589832 | tf_op jit(solution)/shard_map/ppermute | solution.py:481
  111.7 7.3 %collective-permute-start.39 = (bf16[96,1024]{1,0:T(8,128)(2,1)S(1)}, bf16[96,1024]{1,0:T(8,128)(2,1)S(1)}, u32[]{:S(2)}, u32[]{:S(2)}) collective-permute-start(bf16[96,1024]{1,0:T(8,128)(2,1)S(1)} %collective-permute-done.30.refs_1_), channel_id=1, source_target_pairs={{0,1},{1,0},{2,3},{3,2},{4,5},{5,4},{6,7},{7,6},{8,9},{9,8},{10,11... | collective-permute-start | bytes 589832 | tf_op jit(solution)/shard_map/ppermute | solution.py:481
  112.2 7.3 %collective-permute-start.42 = (bf16[96,1024]{1,0:T(8,128)(2,1)S(1)}, bf16[96,1024]{1,0:T(8,128)(2,1)S(1)}, u32[]{:S(2)}, u32[]{:S(2)}) collective-permute-start(bf16[96,1024]{1,0:T(8,128)(2,1)S(1)} %collective-permute-done.35.refs_0_), channel_id=1, source_target_pairs={{0,4},{4,12},{12,8},{8,0},{1,5},{5,13},{13,9},{9,1},{2,6},{6,14},{... | collective-permute-start | bytes 589832 | tf_op jit(solution)/shard_map/ppermute | solution.py:476
  114.3 9.4 %collective-permute-start.32 = (bf16[96,1024]{1,0:T(8,128)(2,1)S(1)}, bf16[96,1024]{1,0:T(8,128)(2,1)S(1)}, u32[]{:S(2)}, u32[]{:S(2)}) collective-permute-start(bf16[96,1024]{1,0:T(8,128)(2,1)S(1)} %collective-permute-done.31.refs_1_), channel_id=1, source_target_pairs={{0,4},{4,12},{12,8},{8,0},{1,5},{5,13},{13,9},{9,1},{2,6},{6,14},{... | collective-permute-start | bytes 589832 | tf_op jit(solution)/shard_map/ppermute | solution.py:476
  114.3 15.0 %collective-permute-start.38 = (bf16[96,1024]{1,0:T(8,128)(2,1)S(1)}, bf16[96,1024]{1,0:T(8,128)(2,1)S(1)}, u32[]{:S(2)}, u32[]{:S(2)}) collective-permute-start(bf16[96,1024]{1,0:T(8,128)(2,1)S(1)} %collective-permute-done.34.refs_0_), channel_id=1, source_target_pairs={{0,1},{1,0},{2,3},{3,2},{4,5},{5,4},{6,7},{7,6},{8,9},{9,8},{10,11... | collective-permute-start | bytes 589832 | tf_op jit(solution)/shard_map/ppermute | solution.py:481
  118.9 13.8 %collective-permute-start.37 = (bf16[96,1024]{1,0:T(8,128)(2,1)S(1)}, bf16[96,1024]{1,0:T(8,128)(2,1)S(1)}, u32[]{:S(2)}, u32[]{:S(2)}) collective-permute-start(bf16[96,1024]{1,0:T(8,128)(2,1)S(1)} %collective-permute-done.31.refs_1_), channel_id=1, source_target_pairs={{0,1},{1,0},{2,3},{3,2},{4,5},{5,4},{6,7},{7,6},{8,9},{9,8},{10,11... | collective-permute-start | bytes 589832 | tf_op jit(solution)/shard_map/ppermute | solution.py:481
  119.0 13.7 %collective-permute-start.36 = (bf16[96,1024]{1,0:T(8,128)(2,1)S(1)}, bf16[96,1024]{1,0:T(8,128)(2,1)S(1)}, u32[]{:S(2)}, u32[]{:S(2)}) collective-permute-start(bf16[96,1024]{1,0:T(8,128)(2,1)S(1)} %collective-permute-done.35.refs_0_), channel_id=1, source_target_pairs={{0,1},{1,0},{2,3},{3,2},{4,5},{5,4},{6,7},{7,6},{8,9},{9,8},{10,11... | collective-permute-start | bytes 589832 | tf_op jit(solution)/shard_map/ppermute | solution.py:481
  119.5 16.6 %collective-permute-start.43 = (bf16[96,1024]{1,0:T(8,128)(2,1)S(1)}, bf16[96,1024]{1,0:T(8,128)(2,1)S(1)}, u32[]{:S(2)}, u32[]{:S(2)}) collective-permute-start(bf16[96,1024]{1,0:T(8,128)(2,1)S(1)} %collective-permute-done.42.refs_0_), channel_id=1, source_target_pairs={{0,1},{1,0},{2,3},{3,2},{4,5},{5,4},{6,7},{7,6},{8,9},{9,8},{10,11... | collective-permute-start | bytes 589832 | tf_op jit(solution)/shard_map/ppermute | solution.py:481
  123.7 15.6 %collective-permute-start.33 = (bf16[96,1024]{1,0:T(8,128)(2,1)S(1)}, bf16[96,1024]{1,0:T(8,128)(2,1)S(1)}, u32[]{:S(2)}, u32[]{:S(2)}) collective-permute-start(bf16[96,1024]{1,0:T(8,128)(2,1)S(1)} %collective-permute-done.32.refs_0_), channel_id=1, source_target_pairs={{0,1},{1,0},{2,3},{3,2},{4,5},{5,4},{6,7},{7,6},{8,9},{9,8},{10,11... | collective-permute-start | bytes 589832 | tf_op jit(solution)/shard_map/ppermute | solution.py:481
where the time goes:
time: 144 us
  Pallas kernels  58.4 us (41%)
  starting transfers between devices  57.5 us (40%)
  waiting for transfers between devices  19.1 us (13%)
  between operations  6.3 us (4%)
  local copies, waits for them, and re-layouts  1.93 us (1%)
    pallas_call x10, Pallas kernels, mix(): pl.pallas_call(functools.partial(mix_body, kind, chosen, counts, out_tile...  35.3 us
    ppermute x19, starting transfers between devices, swapped(): return lax.ppermute(value, 'seq', [(i, seqs - 1 - i) for i in range(seqs)])  29.8 us
    ppermute x15, waiting for transfers between devices, along_ring(): lax.ppermute(value, 'tensor', [(order[i], order[(i + shift) % tensors]) f...  16.5 us
    ppermute x15, starting transfers between devices, along_ring(): lax.ppermute(value, 'tensor', [(order[i], order[(i + shift) % tensors]) f...  16.4 us
    pallas_call x4, Pallas kernels, gate(): pl.pallas_call(functools.partial(gate_body, channels, span, counts), out_...  11.8 us
    ppermute x8, starting transfers between devices, to_next_shifted(): return lax.ppermute(value, ('tensor', 'section'), route)  9.74 us
    pallas_call x1, Pallas kernels, history_states(): pl.pallas_call(functools.partial(history_body, chunk, wide, slot_total),...  6.97 us
    pallas_call x1, Pallas kernels, embed_rows(): pl.pallas_call(functools.partial(embed_body, chunks), out_shape=(jax.Shap...  4.44 us
  transfers between devices with their start and end apart: 44, of which 12 were waited for; matrix products, arithmetic and copies ran while one was open for 1% of the time, Pallas kernels for 29%

commit v1 on v0

v1 whole, which is shorter than its diff:
```python
import functools

import jax
import jax.numpy as jnp
from jax import lax
from jax.experimental import pallas as pl
from jax.experimental.pallas import tpu as pltpu
from jax.sharding import PartitionSpec as P


epsilon = 1e-05
highest = lax.Precision.HIGHEST
LANES = 128
SUB = 8
f32 = jnp.float32
MIB = 1 << 20


def params(mib):
    return pltpu.CompilerParams(vmem_limit_bytes=mib * MIB)


def in_vmem(value):
    return pltpu.with_memory_space_constraint(value, pltpu.VMEM)


def row_spread(ref, row, at, lead=()):
    return ref.at[(*lead, slice(None), at)][pl.ds(row, SUB, stride=0), :]


def in_hbm(value):
    return pltpu.with_memory_space_constraint(value, pltpu.HBM)


def cost(flops, moved):
    return pl.CostEstimate(flops=int(flops), bytes_accessed=int(moved), transcendentals=0)


def row_sums(squares):
    ones = jnp.ones((SUB, squares.shape[1]), f32)
    return lax.dot_general(
        ones, squares, (((1,), (1,)), ((), ())), precision=highest, preferred_element_type=f32
    )


def lane_tiles_squared(block):
    total = block[:, :LANES] * block[:, :LANES]
    for start in range(LANES, block.shape[1], LANES):
        piece = block[:, start : start + LANES]
        total = total + piece * piece
    return total


def embed_body(chunks, meta, ids_any, table, x_out, sums_out, ids, held, rows_buf, sems):
    spans, rows = sums_out.shape[0], sums_out.shape[2]
    half = x_out.shape[2]
    width = held.shape[1]
    depth = held.shape[0] // chunks
    copies = [
        pltpu.make_async_copy(
            table.at[pl.ds(c * depth, depth), :], held.at[pl.ds(c * depth, depth), :], sems.at[c]
        )
        for c in range(chunks)
    ]
    copies.append(pltpu.make_async_copy(ids_any, ids, sems.at[chunks]))
    for copy in copies:
        copy.start()
    for copy in copies:
        copy.wait()
    for span in range(spans):

        def fetch(i, carry):
            rows_buf[pl.ds(i, 1), :] = held[pl.ds(ids[span, i], 1), :]
            return carry

        lax.fori_loop(0, rows, fetch, 0, unroll=8)
        sums_out[span] = row_sums(lane_tiles_squared(rows_buf[...]))
        for part in range(width // half):

            @pl.when(meta[1] == part)
            def _():
                x_out[span] = rows_buf[:, part * half : (part + 1) * half]


def embed_rows(ids, meta, table, half):
    spans, rows = ids.shape
    words, width = table.shape
    chunks = 4 if words % (4 * SUB) == 0 else 1
    return pl.pallas_call(
        functools.partial(embed_body, chunks),
        out_shape=(
            jax.ShapeDtypeStruct((spans, rows, half), f32),
            jax.ShapeDtypeStruct((spans, SUB, rows), f32),
        ),
        in_specs=[
            pl.BlockSpec(memory_space=pltpu.SMEM),
            pl.BlockSpec(memory_space=pl.ANY),
            pl.BlockSpec(memory_space=pl.ANY),
        ],
        out_specs=(
            pl.BlockSpec(memory_space=pltpu.VMEM),
            pl.BlockSpec(memory_space=pltpu.VMEM),
        ),
        scratch_shapes=[
            pltpu.SMEM((spans, rows), jnp.int32),
            pltpu.VMEM((words, width), f32),
            pltpu.VMEM((rows, width), f32),
            pltpu.SemaphoreType.DMA((chunks + 1,)),
        ],
        compiler_params=params(8),
        cost_estimate=cost(4 * spans * rows * width, 4 * words * width),
        name="embed_rows",
    )(meta, in_hbm(ids), in_hbm(table))


def mode_rows(first, step8, rows, store):
    run = list(first)
    for k in range(rows // SUB):
        total = run[0]
        for q in run[1:]:
            total = total + q
        store(k, total)
        if k + 1 < rows // SUB:
            run = [q * d for q, d in zip(run, step8)]


def spread(values, m):
    return jnp.broadcast_to(values[m : m + 1, :], (SUB, values.shape[1]))


def history_body(chunk, wide, slot_total, meta, cache, rates_any, resid_any, weight, *rest):
    states, taps, rates_out, resid_out, weight_out = rest[:5]
    held_rows, rates_ref, resid_ref, sems, mode_sems = rest[5:]
    slots, rows, width = cache.shape
    half = taps.shape[1]
    modes = rates_ref.shape[0]
    chunks = width // chunk
    per_chunk = chunk // wide
    first_span, rank = meta[0], meta[1]

    def lane_start(tile):
        part = jnp.where(tile * wide < half, 1 - rank, rank)
        return pl.multiple_of(part * half + lax.rem(tile * wide, half), LANES)

    def fetch(j):
        return pltpu.make_async_copy(
            cache.at[:, :, pl.ds(lane_start(j * per_chunk), chunk)],
            held_rows.at[:, :, pl.ds(pl.multiple_of(j * chunk, LANES), chunk)],
            sems.at[j],
        )

    mode_copies = [
        pltpu.make_async_copy(rates_any, rates_ref, mode_sems.at[0]),
        pltpu.make_async_copy(resid_any, resid_ref, mode_sems.at[1]),
    ]
    weight_copy = pltpu.make_async_copy(weight, weight_out, mode_sems.at[2])
    for copy in mode_copies:
        copy.start()
    for j in range(chunks):
        fetch(j).start()
    weight_copy.start()
    for copy in mode_copies:
        copy.wait()
    own = pl.ds(pl.multiple_of(rank * half, LANES), half)
    rates_out[...] = rates_ref[:, own]
    resid_out[...] = resid_ref[:, own]

    def one_tile(t, carry):
        @pl.when(lax.rem(t, per_chunk) == 0)
        def _():
            fetch(t // per_chunk).wait()

        at = pl.ds(pl.multiple_of(t * wide, LANES), wide)
        rates = rates_ref[:, pl.ds(lane_start(t), wide)]
        decay = jnp.exp(-rates)
        groups = [decay[g : g + SUB, :] for g in range(0, modes, SUB)]
        held = [[jnp.zeros((SUB, wide), f32) for _ in groups] for _ in range(slots)]
        for r in range(rows):
            for s in range(slots):
                row = row_spread(held_rows, r, at, (s,))
                held[s] = [h * d + row for h, d in zip(held[s], groups)]
        part_a = jnp.zeros((modes, wide), f32)
        part_b = jnp.zeros((modes, wide), f32)
        for s in range(slots):
            slot = rank * slots + s
            age = lax.rem(first_span - slot - 1 + slot_total, slot_total) + 1
            far = (age * rows).astype(f32)
            kept = jnp.where(age < slot_total, 1.0, 0.0).astype(f32)
            total = jnp.concatenate(held[s], axis=0) * decay
            part_a = part_a + total * jnp.exp(-rates * (far - float(rows)))
            part_b = part_b + total * (jnp.exp(-rates * far) * kept)
        out_at = pl.ds(pl.multiple_of(lax.rem(t * wide, half), LANES), wide)
        side = (t * wide) // half
        states[side, 0, :, out_at] = part_a
        states[side, 1, :, out_at] = part_b
        return carry

    lax.fori_loop(0, width // wide, one_tile, 0)

    def tap_tile(t, carry):
        at = pl.ds(pl.multiple_of(rank * half + t * LANES, LANES), LANES)
        out_at = pl.ds(pl.multiple_of(t * LANES, LANES), LANES)
        rates, resid = rates_ref[:, at], resid_ref[:, at]
        place = lax.broadcasted_iota(jnp.int32, (SUB, LANES), 0).astype(f32)
        step8 = jnp.exp(-rates * float(SUB))
        first = [spread(resid, m) * jnp.exp(-spread(rates, m) * place) for m in range(modes)]

        def store(k, value):
            taps[k * SUB : (k + 1) * SUB, out_at] = value

        mode_rows(first, [spread(step8, m) for m in range(modes)], rows, store)
        return carry

    lax.fori_loop(0, half // LANES, tap_tile, 0)
    weight_copy.wait()


def history_states(meta, cache, rates, resid, weight, slot_total):
    slots, rows, width = cache.shape
    modes = rates.shape[0]
    half = weight.shape[1]
    chunk = 512 if half % 512 == 0 else LANES
    wide = 2 * LANES if chunk % (2 * LANES) == 0 else LANES
    vmem = pl.BlockSpec(memory_space=pltpu.VMEM)
    return pl.pallas_call(
        functools.partial(history_body, chunk, wide, slot_total),
        out_shape=(
            jax.ShapeDtypeStruct((2, 2, modes, half), f32),
            jax.ShapeDtypeStruct((rows, half), f32),
            jax.ShapeDtypeStruct((modes, half), f32),
            jax.ShapeDtypeStruct((modes, half), f32),
            pltpu.VMEM(weight.shape, weight.dtype),
        ),
        in_specs=[pl.BlockSpec(memory_space=pltpu.SMEM)] + [pl.BlockSpec(memory_space=pl.ANY)] * 4,
        out_specs=(vmem, vmem, vmem, vmem, vmem),
        scratch_shapes=[
            pltpu.VMEM((slots, rows, width), f32),
            pltpu.VMEM((modes, width), f32),
            pltpu.VMEM((modes, width), f32),
            pltpu.SemaphoreType.DMA((width // chunk,)),
            pltpu.SemaphoreType.DMA((3,)),
        ],
        compiler_params=params(6),
        cost_estimate=cost(2 * slots * rows * modes * width, 4 * slots * rows * width),
        name="history_states",
    )(meta, in_hbm(cache), in_hbm(rates), in_hbm(resid), in_hbm(weight))


def gate_body(channels, span, counts, meta, base, *rest):
    n_delta, n_first, n_later, n_before, n_out = counts
    rest = list(rest)

    def take(n):
        return [rest.pop(0) for _ in range(n)]

    delta = take(n_delta)
    gain, rates_ref, resid_ref, taps, mine, theirs = take(6)
    take(1)
    first_sums, later_sums, before = take(n_first), take(n_later), take(n_before)
    gated = rest.pop(0)
    normed_out = take(n_out)
    padded, state_buf = rest
    rows, half = gated.shape
    modes = rates_ref.shape[0]
    blocks = rows // SUB
    is_first = meta[2] == 1
    wide = 4 * LANES if half % (4 * LANES) == 0 else LANES

    if n_before:

        def chain(t, carry):
            at = pl.ds(pl.multiple_of(t * wide, LANES), wide)
            decay = jnp.exp(-rates_ref[:, at])
            groups = [decay[g : g + SUB, :] for g in range(0, modes, SUB)]
            held = [jnp.zeros((SUB, wide), f32) for _ in groups]
            for r in range(rows):
                row = row_spread(before[0], r, at)
                held = [h * d + row for h, d in zip(held, groups)]
            state_buf[:, at] = jnp.concatenate(held, axis=0) * decay + (
                mine[1, span, :, at] + theirs[span, :, at]
            )
            return carry

        lax.fori_loop(0, half // wide, chain, 0)
    else:
        state_buf[...] = mine[1, span] + theirs[span]

    sums = first_sums[0][span, 0:1, :]
    for ref in first_sums[1:]:
        sums = sums + ref[span, 0:1, :]
    if n_later:
        later = later_sums[0][0:1, :]
        for ref in later_sums[1:]:
            later = later + ref[0:1, :]
        sums = jnp.where(is_first, sums, later)
    here = lax.broadcasted_iota(jnp.int32, (rows, rows), 0)
    there = lax.broadcasted_iota(jnp.int32, (rows, rows), 1)
    column = jnp.sum(
        jnp.where(here == there, jnp.broadcast_to(sums, (rows, rows)), 0.0), axis=1, keepdims=True
    )
    scale = jnp.broadcast_to(lax.rsqrt(column / float(channels) + epsilon), (rows, LANES))
    padded[0:SUB, :] = jnp.zeros((SUB, LANES), f32)

    def tile(t, carry):
        at = pl.ds(pl.multiple_of(t * LANES, LANES), LANES)
        own = pl.ds(pl.multiple_of(meta[1] * half + t * LANES, LANES), LANES)
        current = base[span, :, at]
        if n_delta:
            current = current + jnp.where(is_first, 0.0, delta[0][:, at].astype(f32))
        normed = current * scale * gain[:, own]
        padded[SUB:, :] = normed
        if n_out:
            normed_out[0][:, at] = normed
        rates = rates_ref[:, at]
        weighted = resid_ref[:, at] * state_buf[:, at]
        step8 = jnp.exp(-rates * float(SUB))
        place = lax.broadcasted_iota(jnp.int32, (SUB, LANES), 0).astype(f32)
        first = [spread(weighted, m) * jnp.exp(-spread(rates, m) * place) for m in range(modes)]
        total = [None] * blocks

        def store(k, value):
            total[k] = value

        mode_rows(first, [spread(step8, m) for m in range(modes)], rows, store)
        for b in range(SUB):
            shifted = [
                padded[SUB + k * SUB - b : 2 * SUB + k * SUB - b, :] for k in range(blocks)
            ]
            for a in range(blocks):
                j = a * SUB + b
                tap = row_spread(taps, j, at)
                for k in range(a, blocks):
                    total[k] = total[k] + tap * shifted[k - a]
        for k in range(blocks):
            rows_at = pl.ds(SUB + k * SUB, SUB)
            gated[k * SUB : (k + 1) * SUB, at] = (padded[rows_at, :] * total[k]).astype(gated.dtype)
        return carry

    lax.fori_loop(0, half // LANES, tile, 0)


def gate(meta, base, delta, gain, modes_here, taps, weight, first_sums, later_sums, states, before, span):
    spans, rows, half = base.shape
    modes = modes_here[0].shape[0]
    vmem = pl.BlockSpec(memory_space=pltpu.VMEM)
    deltas = [] if delta is None else [delta]
    want = int(span + 1 < spans)
    head = [base, *deltas, gain, *modes_here, taps, *states]
    operands = [*head, in_vmem(weight), *first_sums, *later_sums, *before]
    in_specs = [vmem] * len(operands)
    in_specs[len(head)] = pl.BlockSpec(memory_space=pl.ANY)
    counts = (len(deltas), len(first_sums), len(later_sums), len(before), want)
    out_shape = [jax.ShapeDtypeStruct((rows, half), jnp.bfloat16)]
    if want:
        out_shape.append(jax.ShapeDtypeStruct((rows, half), f32))
    return pl.pallas_call(
        functools.partial(gate_body, weight.shape[0], span, counts),
        out_shape=tuple(out_shape),
        in_specs=[pl.BlockSpec(memory_space=pltpu.SMEM)] + in_specs,
        out_specs=tuple(vmem for _ in out_shape),
        scratch_shapes=[pltpu.VMEM((rows + SUB, LANES), f32), pltpu.VMEM((modes, half), f32)],
        compiler_params=params(2),
        cost_estimate=cost(rows * rows * half + 4 * modes * rows * half, 12 * rows * half),
        name="gate",
    )(meta, *operands)


def source_of(step, rank, count):
    place = jnp.where(lax.rem(rank, 2) == 1, (rank + 1) // 2, lax.rem(count - rank // 2, count))
    came = lax.rem(place - step + count, count)
    return jnp.where(came <= count // 2, jnp.maximum(2 * came - 1, 0), 2 * (count - came))


def mix_body(kind, chosen, counts, out_tile, step, meta, *refs):
    parts, n_acc, n_base, n_delta, n_done, seqs, tensors = counts
    refs = list(refs)

    def take(n):
        return [refs.pop(0) for _ in range(n)]

    pieces = [take(len(chosen)) for _ in range(parts)]
    (weight,) = take(1)
    acc_in, base, delta, done = take(n_acc), take(n_base), take(n_delta), take(n_done)
    rows, depth = pieces[0][0].shape
    out = weight.shape[1]
    if step is None:
        starts = [0] * parts
    else:
        source = source_of(step, meta[3], tensors) * seqs
        starts = [
            pl.multiple_of((source + jnp.where(p == 0, meta[1], seqs - 1 - meta[1])) * depth, depth)
            for p in range(parts)
        ]
    span = chosen[0]
    squares = jnp.zeros((rows, LANES), f32)
    for n in range(out // out_tile):
        at = slice(n * out_tile, (n + 1) * out_tile)
        total = None
        for p in range(parts):
            lhs = jnp.concatenate([piece[...] for piece in pieces[p]], axis=0)
            more = jnp.dot(lhs, weight[pl.ds(starts[p], depth), at], preferred_element_type=f32)
            total = more if total is None else total + more
        if n_acc and acc_in[0].shape[0] == total.shape[0]:
            total = total + acc_in[0][:, at]
        elif n_acc:
            total = total + acc_in[0][span * rows : (span + 1) * rows, at]
        if kind == "part":
            refs[0][:, at] = total
            continue
        if n_delta:
            total = total + jnp.where(meta[2] == 1, 0.0, delta[0][:, at].astype(f32))
        fresh = base[0][span, :, at] + total
        if kind == "hop":
            refs[0][:, at] = total.astype(refs[0].dtype)
            squares = squares + lane_tiles_squared(fresh)
        elif kind == "done":
            refs[0][:, at] = fresh
        else:
            refs[0][0, span, :, at] = fresh
            for i, ref in enumerate(done):
                refs[0][0, i, :, at] = ref[:, at]
    if kind == "hop":
        refs[1][...] = row_sums(squares)


def mix(kind, meta, step, pieces, chosen, weight, acc, base, delta, seqs, tensors, done=()):
    rows, depth = pieces[0][0].shape
    out = weight.shape[1]
    vmem = pl.BlockSpec(memory_space=pltpu.VMEM)
    accs = [] if acc is None else [acc]
    bases = [] if kind == "part" else [base]
    deltas = [] if kind == "part" or delta is None else [delta]
    flat = [piece for part in pieces for piece in part]
    operands = [*flat, in_vmem(weight), *accs, *bases, *deltas, *done]
    counts = (len(pieces), len(accs), len(bases), len(deltas), len(done), seqs, tensors)
    whole = jax.ShapeDtypeStruct((rows * len(chosen), out), f32)
    out_shape, out_specs = whole, vmem
    if kind == "hop":
        out_shape = (
            jax.ShapeDtypeStruct((rows, out), jnp.bfloat16),
            jax.ShapeDtypeStruct((SUB, rows), f32),
        )
        out_specs = (vmem, vmem)
    elif kind == "out":
        out_shape = jax.ShapeDtypeStruct((1, len(done) + 1, rows, out), f32)
    out_tile = 4 * LANES if out % (4 * LANES) == 0 else LANES
    return pl.pallas_call(
        functools.partial(mix_body, kind, chosen, counts, out_tile, step),
        out_shape=out_shape,
        in_specs=[pl.BlockSpec(memory_space=pltpu.SMEM)] + [vmem] * len(operands),
        out_specs=out_specs,
        compiler_params=params(8),
        cost_estimate=cost(
            2 * rows * len(chosen) * depth * out * len(pieces), 2 * depth * out * len(pieces)
        ),
    )(meta, *operands)


def ring_fits(tensors):
    return tensors in (2, 4, 8)


def ring_order(count):
    return list(range(0, 1)) + list(range(1, count, 2)) + list(range(2, count, 2))[::-1]


def local(token_ids, leading_span_index, embed_table, norm_gain, decay_rates, residues, history, mix_weight):
    section_rank = lax.axis_index("section")
    sections = lax.axis_size("section")
    seq_rank = lax.axis_index("seq")
    seqs = lax.axis_size("seq")
    tensor_rank = lax.axis_index("tensor")
    tensors = lax.axis_size("tensor")
    rates, resid, cache, weight = decay_rates[0], residues[0], history[0], mix_weight[0]
    spans, _ = token_ids.shape
    slots, _, _ = cache.shape
    half = weight.shape[1]
    slot_total = slots * seqs
    order = ring_order(tensors)

    def along_ring(value, shift):
        return lax.ppermute(
            value, "tensor", [(order[i], order[(i + shift) % tensors]) for i in range(tensors)]
        )

    def swapped(value):
        return lax.ppermute(value, "seq", [(i, seqs - 1 - i) for i in range(seqs)])

    def to_next(value):
        return lax.ppermute(value, "section", [(i, (i + 1) % sections) for i in range(sections)])

    def across(value, flip):
        return lax.ppermute(value, "tensor", [(i, i ^ flip) for i in range(tensors)])

    def to_next_across(value, flip):
        route = []
        for i in range(tensors):
            for s in range(sections):
                route.append((i * sections + s, (i ^ flip) * sections + (s + 1) % sections))
        return lax.ppermute(value, ("tensor", "section"), route)

    first_span = lax.rem(leading_span_index[0], slot_total)
    is_first = (section_rank == 0).astype(jnp.int32)
    meta = jnp.stack([first_span, seq_rank, is_first, tensor_rank]).astype(jnp.int32)

    base, sums = embed_rows(token_ids, meta, embed_table, half)
    small_ring = ring_fits(tensors)
    first_sums = [sums]
    if small_ring:
        for k in range(1, tensors):
            first_sums.append(along_ring(sums, k))
    else:
        first_sums = [lax.psum(sums, "tensor")]
    states, taps, *modes_here = history_states(meta, cache, rates, resid, weight, slot_total)
    weight = modes_here.pop()
    partner = swapped(states[0])

    every = tuple(range(spans))
    deltas = [None] * spans
    later_sums = [[]] * spans
    for stage in range(sections):
        last_stage = stage + 1 == sections
        gates = []
        before = []
        for span in every:
            got = gate(
                meta, base, deltas[span], norm_gain, modes_here, taps, weight, first_sums,
                later_sums[span], [states, partner], before, span,
            )
            gates.append(got[0])
            before = list(got[1:])
        acc = None
        moving = list(gates)
        results = []
        steps = tensors if small_ring else 1
        for k in range(steps):
            final = k + 1 == steps
            if small_ring:
                step = k
                crossed = []
                for span in every:
                    crossed.append(swapped(moving[span]))
                pairs = [list(moving), crossed]
                if not final:
                    for span in every:
                        moving[span] = along_ring(moving[span], 1)
            else:
                step = None
                pairs = [[lax.all_gather(g, ("tensor", "seq"), axis=1, tiled=True) for g in gates]]
            if not final:
                acc = mix("part", meta, step, pairs, every, weight, acc, None, None, seqs, tensors)
                continue
            for span in every:
                kind = "hop" if not last_stage else "out" if span + 1 == spans else "done"
                done = tuple(results) if kind == "out" else ()
                results.append(
                    mix(
                        kind, meta, step, [[part[span]] for part in pairs], (span,), weight,
                        acc, base, deltas[span], seqs, tensors, done,
                    )
                )
        if not last_stage:
            new_deltas, new_sums = [], []
            for span in every:
                moved, partial = results[span]
                new_deltas.append(to_next(moved))
                both = partial + swapped(partial)
                if small_ring:
                    bits = tensors.bit_length() - 1
                    for bit in range(bits - 1):
                        both = both + across(both, 1 << bit)
                    got = []
                    for k in range(2):
                        got.append(to_next_across(both, k * tensors // 2))
                    new_sums.append(got)
                else:
                    new_sums.append([to_next(lax.psum(both, "tensor"))])
            deltas, later_sums = new_deltas, new_sums
    return results[-1]


def solution(mesh):
    placed = (
        P("groups", None),
        P("groups"),
        P(None, "tensor"),
        P("section", "tensor"),
        P("section", None, "tensor"),
        P("section", None, "tensor"),
        P("section", "seq", "groups", "tensor"),
        P("section", None, ("tensor", "seq")),
    )
    return jax.shard_map(
        local,
        mesh=mesh,
        in_specs=placed,
        out_specs=P("section", None, "groups", ("tensor", "seq")),
        check_vma=False,
    )
```

time: 144 us -> 114 us (0.79)
  Pallas kernels: 58.4 us -> 40 us
  waiting for transfers between devices: 19.1 us -> 13.7 us
  between operations: 6.3 us -> 0.9 us
  local copies, waits for them, and re-layouts: 1.93 us -> 0.01 us
  starting transfers between devices: 57.5 us -> 59 us
    pallas_call x10, Pallas kernels: 35.3 us -> 16.4 us  [mix(): pl.pallas_call(functools.partial(mix_body, kind, chosen, counts, out_tile...]
    ppermute x15, waiting for transfers between devices: 16.5 us -> 11.3 us  [along_ring(): lax.ppermute(value, 'tensor', [(order[i], order[(i + shift) % tensors]) f...]
    ppermute x19, starting transfers between devices: 29.8 us -> 34.6 us  [swapped(): return lax.ppermute(value, 'seq', [(i, seqs - 1 - i) for i in range(seqs)])]
    ppermute x8 -> x6, starting transfers between devices: 9.74 us -> 6.67 us  [the longest x4 5.35 us: to_next_across(): return lax.ppermute(value, ('tensor', 'section'), route)]
  transfers between devices with their start and end apart: 44 -> 42, of which waited for: 12 -> 11; matrix products, arithmetic and copies ran while one was open for 1% -> 0% of each run, Pallas kernels for 29% -> 24%
where the time goes in v1:
time: 114 us
  starting transfers between devices  59 us (52%)
  Pallas kernels  40 us (35%)
  waiting for transfers between devices  13.7 us (12%)
    ppermute x19, starting transfers between devices, swapped(): return lax.ppermute(value, 'seq', [(i, seqs - 1 - i) for i in range(seqs)])  34.6 us
    pallas_call x10, Pallas kernels, mix(): pl.pallas_call(functools.partial(mix_body, kind, chosen, counts, out_tile...  16.4 us
    ppermute x15, starting transfers between devices, along_ring(): lax.ppermute(value, 'tensor', [(order[i], order[(i + shift) % tensors]) f...  16.3 us
    pallas_call x4, Pallas kernels, gate(): pl.pallas_call(functools.partial(gate_body, weight.shape[0], span, counts...  11.7 us
    ppermute x15, waiting for transfers between devices, along_ring(): lax.ppermute(value, 'tensor', [(order[i], order[(i + shift) % tensors]) f...  11.3 us
    pallas_call x1, Pallas kernels, history_states(): pl.pallas_call(functools.partial(history_body, chunk, wide, slot_total),...  7.44 us
    ppermute x4, starting transfers between devices, to_next_across(): return lax.ppermute(value, ('tensor', 'section'), route)  5.35 us
    pallas_call x1, Pallas kernels, embed_rows(): pl.pallas_call(functools.partial(embed_body, chunks), out_shape=(jax.Shap...  4.47 us
  transfers between devices with their start and end apart: 42, of which 11 were waited for; matrix products, arithmetic and copies ran while one was open for 0% of the time, Pallas kernels for 24%

profile of v1, /device:TPU:1, one launch (start us, length us, event | category | flops | bytes accessed | tf_op | source)
XLA Modules:
  0.0 113.7 jit_solution(5549801506406027837)
XLA Ops:
  0.8 7.4 %history_states.1 = (f32[2,2,16,1024]{3,2,1,0:T(8,128)S(1)}, f32[96,1024]{1,0:T(8,128)S(1)}, f32[16,1024]{1,0:T(8,128)S(1)}, f32[16,1024]{1,0:T(8,128)S(1)}, bf16[8192,1024]{1,0:T(8,128)(2,1)S(1)}) custom-call(s32[4]{0:T(128)S(1)} %pad_add_fusion.meta, f32[4,96,2048]{2,1,0:T(8,128)} %bitcast.15, f32[16,2048]{1,0:T(8,128)} %bitcast.16, f32[16,2048]{1,0:T(8,128)} %bitcast.17, ...), custom_call_target="tpu_custom_call" | custom-call | flops 25165824 | bytes 3145728 | tf_op jit(solution)/shard_map/history_states/pallas_call | solution.py:225
  8.3 4.5 %embed_rows.1 = (f32[2,96,1024]{2,1,0:T(8,128)S(1)}, f32[2,8,96]{2,1,0:T(8,128)S(1)}) custom-call(s32[4]{0:T(128)S(1)} %pad_add_fusion.meta, s32[2,96]{1,0:T(2,128)} %ids_any.1, f32[512,2048]{1,0:T(8,128)} %table.1), custom_call_target="tpu_custom_call" | custom-call | flops 1572864 | bytes 4194304 | tf_op jit(solution)/shard_map/embed_rows/pallas_call | solution.py:89
  12.8 2.8 %collective-permute-start.1 = (f32[2,8,96]{2,1,0:T(8,128)S(1)}, f32[2,8,96]{2,1,0:T(8,128)S(1)}, u32[]{:S(2)}, u32[]{:S(2)}) collective-permute-start(f32[2,8,96]{2,1,0:T(8,128)S(1)} %get-tuple-element.26.rest_7_.rest_8_), channel_id=1, source_target_pairs={{0,4},{4,12},{12,8},{8,0},{1,5},{5,13},{13,9},{9,1},{2,6},{6,14},{... | collective-permute-start | bytes 18440 | tf_op jit(solution)/shard_map/ppermute | solution.py:482
  15.6 2.2 %collective-permute-start.2 = (f32[2,8,96]{2,1,0:T(8,128)S(1)}, f32[2,8,96]{2,1,0:T(8,128)S(1)}, u32[]{:S(2)}, u32[]{:S(2)}) collective-permute-start(f32[2,8,96]{2,1,0:T(8,128)S(1)} %get-tuple-element.26.rest_7_.rest_8_), channel_id=1, source_target_pairs={{0,12},{4,8},{12,0},{8,4},{1,13},{5,9},{13,1},{9,5},{2,14},{6,10},... | collective-permute-start | bytes 18440 | tf_op jit(solution)/shard_map/ppermute | solution.py:482
  17.8 1.3 %collective-permute-start.3 = (f32[2,8,96]{2,1,0:T(8,128)S(1)}, f32[2,8,96]{2,1,0:T(8,128)S(1)}, u32[]{:S(2)}, u32[]{:S(2)}) collective-permute-start(f32[2,8,96]{2,1,0:T(8,128)S(1)} %get-tuple-element.26.rest_7_.rest_8_), channel_id=1, source_target_pairs={{0,8},{4,0},{12,4},{8,12},{1,9},{5,1},{13,5},{9,13},{2,10},{6,2},{... | collective-permute-start | bytes 18440 | tf_op jit(solution)/shard_map/ppermute | solution.py:482
  19.1 0.8 collective-permute-done.2.rest_9_.rest_10_
  19.9 0.7 collective-permute-done.3.rest_10_.rest_11_
  20.6 2.7 %gate.4 = (bf16[96,1024]{1,0:T(8,128)(2,1)S(1)}, f32[96,1024]{1,0:T(8,128)S(1)}) custom-call(s32[4]{0:T(128)S(1)} %pad_add_fusion.meta, f32[2,96,1024]{2,1,0:T(8,128)S(1)} %get-tuple-element.20.base.refs_4_, f32[1,2048]{1,0:T(1,128)S(1)} %copy-done, f32[16,1024]{1,0:T(8,128)S(1)} %get-tuple-element.21.rest_1_.rest_2_, ...), custom_call_target="tpu_custom_call" | custom-call | flops 15728640 | bytes 1179648 | tf_op jit(solution)/shard_map/gate/pallas_call | solution.py:356
  23.3 0.8 collective-permute-start.8
  24.0 3.1 %gate.5.refs_1_ = bf16[96,1024]{1,0:T(8,128)(2,1)S(1)} custom-call(s32[4]{0:T(128)S(1)} %pad_add_fusion.meta, f32[2,96,1024]{2,1,0:T(8,128)S(1)} %get-tuple-element.20.base.refs_4_, f32[1,2048]{1,0:T(1,128)S(1)} %copy-done, f32[16,1024]{1,0:T(8,128)S(1)} %get-tuple-element.21.rest_1_.rest_2_, f32[16,1024]{1,0:T(8,128)S(1)} %get-tuple-element.22.rest_2_.rest_3_, ...), custom_call_target="tpu_custom_call" | custom-call | flops 15728640 | bytes 1179648 | tf_op jit(solution)/shard_map/gate/pallas_call | solution.py:356
  27.2 1.1 collective-permute-start.4
  28.3 1.0 collective-permute-done.8.refs_0_
  29.3 0.5 collective-permute-start.9
  29.9 3.7 %collective-permute-done.4.refs_1_ = bf16[96,1024]{1,0:T(8,128)(2,1)S(1)} collective-permute-done((bf16[96,1024]{1,0:T(8,128)(2,1)S(1)}, bf16[96,1024]{1,0:T(8,128)(2,1)S(1)}, u32[]{:S(2)}, u32[]{:S(2)}) %collective-permute-start.4) | collective-permute-done | bytes 196640 | tf_op jit(solution)/shard_map/ppermute | solution.py:482
  33.6 4.4 %collective-permute-start.15 = (bf16[96,1024]{1,0:T(8,128)(2,1)S(1)}, bf16[96,1024]{1,0:T(8,128)(2,1)S(1)}, u32[]{:S(2)}, u32[]{:S(2)}) collective-permute-start(bf16[96,1024]{1,0:T(8,128)(2,1)S(1)} %gate.5.refs_1_), channel_id=1, source_target_pairs={{0,1},{1,0},{2,3},{3,2},{4,5},{5,4},{6,7},{7,6},{8,9},{9,8},{10,11... | collective-permute-start | bytes 589832 | tf_op jit(solution)/shard_map/ppermute | solution.py:487
  38.5 2.8 %collective-permute-start.21 = (bf16[96,1024]{1,0:T(8,128)(2,1)S(1)}, bf16[96,1024]{1,0:T(8,128)(2,1)S(1)}, u32[]{:S(2)}, u32[]{:S(2)}) collective-permute-start(bf16[96,1024]{1,0:T(8,128)(2,1)S(1)} %collective-permute-done.9.refs_0_), channel_id=1, source_target_pairs={{0,4},{4,12},{12,8},{8,0},{1,5},{5,13},{13,9},{9,1},{2,6},{6,14},{... | collective-permute-start | bytes 589832 | tf_op jit(solution)/shard_map/ppermute | solution.py:482
  41.7 4.2 %collective-permute-start.12 = (bf16[96,1024]{1,0:T(8,128)(2,1)S(1)}, bf16[96,1024]{1,0:T(8,128)(2,1)S(1)}, u32[]{:S(2)}, u32[]{:S(2)}) collective-permute-start(bf16[96,1024]{1,0:T(8,128)(2,1)S(1)} %collective-permute-done.8.refs_0_), channel_id=1, source_target_pairs={{0,1},{1,0},{2,3},{3,2},{4,5},{5,4},{6,7},{7,6},{8,9},{9,8},{10,11... | collective-permute-start | bytes 589832 | tf_op jit(solution)/shard_map/ppermute | solution.py:487
  46.5 3.9 %collective-permute-start.22 = (bf16[96,1024]{1,0:T(8,128)(2,1)S(1)}, bf16[96,1024]{1,0:T(8,128)(2,1)S(1)}, u32[]{:S(2)}, u32[]{:S(2)}) collective-permute-start(bf16[96,1024]{1,0:T(8,128)(2,1)S(1)} %collective-permute-done.21.refs_0_), channel_id=1, source_target_pairs={{0,1},{1,0},{2,3},{3,2},{4,5},{5,4},{6,7},{7,6},{8,9},{9,8},{10,11... | collective-permute-start | bytes 589832 | tf_op jit(solution)/shard_map/ppermute | solution.py:487
  50.4 2.2 %collective-permute-start.7 = (bf16[96,1024]{1,0:T(8,128)(2,1)S(1)}, bf16[96,1024]{1,0:T(8,128)(2,1)S(1)}, u32[]{:S(2)}, u32[]{:S(2)}) collective-permute-start(bf16[96,1024]{1,0:T(8,128)(2,1)S(1)} %collective-permute-done.6.refs_0_), channel_id=1, source_target_pairs={{0,1},{1,0},{2,3},{3,2},{4,5},{5,4},{6,7},{7,6},{8,9},{9,8},{10,11... | collective-permute-start | bytes 589832 | tf_op jit(solution)/shard_map/ppermute | solution.py:487
  52.6 1.6 %shard_map.82.refs_5_ = f32[192,1024]{1,0:T(8,128)S(1)} custom-call(s32[4]{0:T(128)S(1)} %pad_add_fusion.meta, bf16[96,1024]{1,0:T(8,128)(2,1)S(1)} %get-tuple-element.28.refs_0_, bf16[96,1024]{1,0:T(8,128)(2,1)S(1)} %gate.5.refs_1_, bf16[96,1024]{1,0:T(8,128)(2,1)S(1)} %collective-permute-done.14.refs_2_, ...), custom_call_target="tpu_custom_call" | custom-call | flops 805306368 | bytes 4194304 | tf_op jit(solution)/shard_map/pallas_call | solution.py:447
  54.2 1.6 %shard_map.83.refs_5_ = f32[192,1024]{1,0:T(8,128)S(1)} custom-call(s32[4]{0:T(128)S(1)} %pad_add_fusion.meta, bf16[96,1024]{1,0:T(8,128)(2,1)S(1)} %collective-permute-done.8.refs_0_, bf16[96,1024]{1,0:T(8,128)(2,1)S(1)} %collective-permute-done.4.refs_1_, bf16[96,1024]{1,0:T(8,128)(2,1)S(1)} %collective-permute-done.12.refs_2_, ...), custom_call_target="tpu_custom_call" | custom-call | flops 805306368 | bytes 4194304 | tf_op jit(solution)/shard_map/pallas_call | solution.py:447
  55.8 1.6 %shard_map.84.refs_3_ = f32[192,1024]{1,0:T(8,128)S(1)} custom-call(s32[4]{0:T(128)S(1)} %pad_add_fusion.meta, bf16[96,1024]{1,0:T(8,128)(2,1)S(1)} %collective-permute-done.9.refs_0_, bf16[96,1024]{1,0:T(8,128)(2,1)S(1)} %collective-permute-done.5.refs_1_, bf16[96,1024]{1,0:T(8,128)(2,1)S(1)} %collective-permute-done.10.refs_2_, ...), custom_call_target="tpu_custom_call" | custom-call | flops 805306368 | bytes 4194304 | tf_op jit(solution)/shard_map/pallas_call | solution.py:447
  57.4 1.7 %shard_map.86 = (bf16[96,1024]{1,0:T(8,128)(2,1)S(1)}, f32[8,96]{1,0:T(8,128)S(1)}) custom-call(s32[4]{0:T(128)S(1)} %pad_add_fusion.meta, bf16[96,1024]{1,0:T(8,128)(2,1)S(1)} %collective-permute-done.21.refs_0_, bf16[96,1024]{1,0:T(8,128)(2,1)S(1)} %collective-permute-done.22.refs_1_, ...), custom_call_target="tpu_custom_call" | custom-call | flops 402653184 | bytes 4194304 | tf_op jit(solution)/shard_map/pallas_call | solution.py:447
  59.0 1.2 %collective-permute-start.23 = (bf16[96,1024]{1,0:T(8,128)(2,1)S(1)}, bf16[96,1024]{1,0:T(8,128)(2,1)S(1)}, u32[]{:S(2)}, u32[]{:S(2)}) collective-permute-start(bf16[96,1024]{1,0:T(8,128)(2,1)S(1)} %get-tuple-element.31), channel_id=1, source_target_pairs={{0,2},{2,0},{1,3},{3,1},{4,6},{6,4},{5,7},{7,5},{8,10},{10,8},{9,1... | collective-permute-start | bytes 589832 | tf_op jit(solution)/shard_map/ppermute | solution.py:490
  60.3 1.7 %shard_map.85 = (bf16[96,1024]{1,0:T(8,128)(2,1)S(1)}, f32[8,96]{1,0:T(8,128)S(1)}) custom-call(s32[4]{0:T(128)S(1)} %pad_add_fusion.meta, bf16[96,1024]{1,0:T(8,128)(2,1)S(1)} %collective-permute-done.6.refs_0_, bf16[96,1024]{1,0:T(8,128)(2,1)S(1)} %collective-permute-done.7.refs_1_, ...), custom_call_target="tpu_custom_call" | custom-call | flops 402653184 | bytes 4194304 | tf_op jit(solution)/shard_map/pallas_call | solution.py:447
  62.2 0.6 collective-permute-start.24
  62.8 0.8 collective-permute-done.24
  64.0 1.1 collective-permute-start.18
  65.1 1.3 %collective-permute-done.25 = f32[8,96]{1,0:T(8,128)S(1)} collective-permute-done((f32[8,96]{1,0:T(8,128)S(1)}, f32[8,96]{1,0:T(8,128)S(1)}, u32[]{:S(2)}, u32[]{:S(2)}) %collective-permute-start.25) | collective-permute-done | bytes 3104 | tf_op jit(solution)/shard_map/ppermute | solution.py:493
  66.4 1.2 %collective-permute-start.26 = (f32[8,96]{1,0:T(8,128)S(1)}, f32[8,96]{1,0:T(8,128)S(1)}, u32[]{:S(2)}, u32[]{:S(2)}) collective-permute-start(f32[8,96]{1,0:T(8,128)S(1)} %add.15), channel_id=1, source_target_pairs={{0,2},{2,0},{4,6},{6,4},{8,10},{10,8},{12,14},{14,12},{1,3},{3,1},... | collective-permute-start | bytes 9224 | tf_op jit(solution)/shard_map/ppermute | solution.py:500
  67.6 1.4 %collective-permute-start.27 = (f32[8,96]{1,0:T(8,128)S(1)}, f32[8,96]{1,0:T(8,128)S(1)}, u32[]{:S(2)}, u32[]{:S(2)}) collective-permute-start(f32[8,96]{1,0:T(8,128)S(1)} %add.15), channel_id=1, source_target_pairs={{0,10},{2,8},{4,14},{6,12},{8,2},{10,0},{12,6},{14,4},{1,11},{3,9}... | collective-permute-start | bytes 9224 | tf_op jit(solution)/shard_map/ppermute | solution.py:500
  69.0 1.2 %collective-permute-start.19 = (f32[8,96]{1,0:T(8,128)S(1)}, f32[8,96]{1,0:T(8,128)S(1)}, u32[]{:S(2)}, u32[]{:S(2)}) collective-permute-start(f32[8,96]{1,0:T(8,128)S(1)} %add.13), channel_id=1, source_target_pairs={{0,2},{2,0},{4,6},{6,4},{8,10},{10,8},{12,14},{14,12},{1,3},{3,1},... | collective-permute-start | bytes 9224 | tf_op jit(solution)/shard_map/ppermute | solution.py:500
  70.2 1.6 %collective-permute-start.20 = (f32[8,96]{1,0:T(8,128)S(1)}, f32[8,96]{1,0:T(8,128)S(1)}, u32[]{:S(2)}, u32[]{:S(2)}) collective-permute-start(f32[8,96]{1,0:T(8,128)S(1)} %add.13), channel_id=1, source_target_pairs={{0,10},{2,8},{4,14},{6,12},{8,2},{10,0},{12,6},{14,4},{1,11},{3,9}... | collective-permute-start | bytes 9224 | tf_op jit(solution)/shard_map/ppermute | solution.py:500
  71.9 2.7 %gate.6 = (bf16[96,1024]{1,0:T(8,128)(2,1)S(1)}, f32[96,1024]{1,0:T(8,128)S(1)}) custom-call(s32[4]{0:T(128)S(1)} %pad_add_fusion.meta, f32[2,96,1024]{2,1,0:T(8,128)S(1)} %get-tuple-element.20.base.refs_4_, bf16[96,1024]{1,0:T(8,128)(2,1)S(1)} %collective-permute-done.23.rest_0_.refs_5_, f32[1,2048]{1,0:T(1,128)S(1)} %copy-done, ...), custom_call_target="tpu_custom_call" | custom-call | flops 15728640 | bytes 1179648 | tf_op jit(solution)/shard_map/gate/pallas_call | solution.py:356
  74.6 1.8 %collective-permute-start.32 = (bf16[96,1024]{1,0:T(8,128)(2,1)S(1)}, bf16[96,1024]{1,0:T(8,128)(2,1)S(1)}, u32[]{:S(2)}, u32[]{:S(2)}) collective-permute-start(bf16[96,1024]{1,0:T(8,128)(2,1)S(1)} %get-tuple-element.34.refs_0_), channel_id=1, source_target_pairs={{0,4},{4,12},{12,8},{8,0},{1,5},{5,13},{13,9},{9,1},{2,6},{6,14},{... | collective-permute-start | bytes 589832 | tf_op jit(solution)/shard_map/ppermute | solution.py:482
  76.4 3.2 %gate.7.refs_1_ = bf16[96,1024]{1,0:T(8,128)(2,1)S(1)} custom-call(s32[4]{0:T(128)S(1)} %pad_add_fusion.meta, f32[2,96,1024]{2,1,0:T(8,128)S(1)} %get-tuple-element.20.base.refs_4_, bf16[96,1024]{1,0:T(8,128)(2,1)S(1)} %collective-permute-done.16.rest_0_.refs_5_, f32[1,2048]{1,0:T(1,128)S(1)} %copy-done, f32[16,1024]{1,0:T(8,128)S(1)} %get-tuple-element.21.rest_1_.rest_2_, ...), custom_call_target="tpu_custom_call" | custom-call | flops 15728640 | bytes 1179648 | tf_op jit(solution)/shard_map/gate/pallas_call | solution.py:356
  79.6 1.1 %collective-permute-start.28 = (bf16[96,1024]{1,0:T(8,128)(2,1)S(1)}, bf16[96,1024]{1,0:T(8,128)(2,1)S(1)}, u32[]{:S(2)}, u32[]{:S(2)}) collective-permute-start(bf16[96,1024]{1,0:T(8,128)(2,1)S(1)} %gate.7.refs_1_), channel_id=1, source_target_pairs={{0,4},{4,12},{12,8},{8,0},{1,5},{5,13},{13,9},{9,1},{2,6},{6,14},{... | collective-permute-start | bytes 589832 | tf_op jit(solution)/shard_map/ppermute | solution.py:482
  80.9 4.3 %collective-permute-done.28.refs_1_ = bf16[96,1024]{1,0:T(8,128)(2,1)S(1)} collective-permute-done((bf16[96,1024]{1,0:T(8,128)(2,1)S(1)}, bf16[96,1024]{1,0:T(8,128)(2,1)S(1)}, u32[]{:S(2)}, u32[]{:S(2)}) %collective-permute-start.28) | collective-permute-done | bytes 196640 | tf_op jit(solution)/shard_map/ppermute | solution.py:482
  85.5 6.2 %collective-permute-start.39 = (bf16[96,1024]{1,0:T(8,128)(2,1)S(1)}, bf16[96,1024]{1,0:T(8,128)(2,1)S(1)}, u32[]{:S(2)}, u32[]{:S(2)}) collective-permute-start(bf16[96,1024]{1,0:T(8,128)(2,1)S(1)} %gate.7.refs_1_), channel_id=1, source_target_pairs={{0,1},{1,0},{2,3},{3,2},{4,5},{5,4},{6,7},{7,6},{8,9},{9,8},{10,11... | collective-permute-start | bytes 589832 | tf_op jit(solution)/shard_map/ppermute | solution.py:487
  92.2 1.3 %collective-permute-start.40 = (bf16[96,1024]{1,0:T(8,128)(2,1)S(1)}, bf16[96,1024]{1,0:T(8,128)(2,1)S(1)}, u32[]{:S(2)}, u32[]{:S(2)}) collective-permute-start(bf16[96,1024]{1,0:T(8,128)(2,1)S(1)} %collective-permute-done.33.refs_0_), channel_id=1, source_target_pairs={{0,4},{4,12},{12,8},{8,0},{1,5},{5,13},{13,9},{9,1},{2,6},{6,14},{... | collective-permute-start | bytes 589832 | tf_op jit(solution)/shard_map/ppermute | solution.py:482
  93.9 4.5 %collective-permute-start.36 = (bf16[96,1024]{1,0:T(8,128)(2,1)S(1)}, bf16[96,1024]{1,0:T(8,128)(2,1)S(1)}, u32[]{:S(2)}, u32[]{:S(2)}) collective-permute-start(bf16[96,1024]{1,0:T(8,128)(2,1)S(1)} %collective-permute-done.32.refs_0_), channel_id=1, source_target_pairs={{0,1},{1,0},{2,3},{3,2},{4,5},{5,4},{6,7},{7,6},{8,9},{9,8},{10,11... | collective-permute-start | bytes 589832 | tf_op jit(solution)/shard_map/ppermute | solution.py:487
  98.8 4.2 %collective-permute-start.41 = (bf16[96,1024]{1,0:T(8,128)(2,1)S(1)}, bf16[96,1024]{1,0:T(8,128)(2,1)S(1)}, u32[]{:S(2)}, u32[]{:S(2)}) collective-permute-start(bf16[96,1024]{1,0:T(8,128)(2,1)S(1)} %collective-permute-done.40.refs_0_), channel_id=1, source_target_pairs={{0,1},{1,0},{2,3},{3,2},{4,5},{5,4},{6,7},{7,6},{8,9},{9,8},{10,11... | collective-permute-start | bytes 589832 | tf_op jit(solution)/shard_map/ppermute | solution.py:487
  103.0 2.2 %collective-permute-start.31 = (bf16[96,1024]{1,0:T(8,128)(2,1)S(1)}, bf16[96,1024]{1,0:T(8,128)(2,1)S(1)}, u32[]{:S(2)}, u32[]{:S(2)}) collective-permute-start(bf16[96,1024]{1,0:T(8,128)(2,1)S(1)} %collective-permute-done.30.refs_0_), channel_id=1, source_target_pairs={{0,1},{1,0},{2,3},{3,2},{4,5},{5,4},{6,7},{7,6},{8,9},{9,8},{10,11... | collective-permute-start | bytes 589832 | tf_op jit(solution)/shard_map/ppermute | solution.py:487
  105.3 1.6 %shard_map.87.refs_5_ = f32[192,1024]{1,0:T(8,128)S(1)} custom-call(s32[4]{0:T(128)S(1)} %pad_add_fusion.meta, bf16[96,1024]{1,0:T(8,128)(2,1)S(1)} %get-tuple-element.34.refs_0_, bf16[96,1024]{1,0:T(8,128)(2,1)S(1)} %gate.7.refs_1_, bf16[96,1024]{1,0:T(8,128)(2,1)S(1)} %collective-permute-done.38.refs_2_, ...), custom_call_target="tpu_custom_call" | custom-call | flops 805306368 | bytes 4194304 | tf_op jit(solution)/shard_map/pallas_call | solution.py:447
  106.8 1.6 %shard_map.88.refs_5_ = f32[192,1024]{1,0:T(8,128)S(1)} custom-call(s32[4]{0:T(128)S(1)} %pad_add_fusion.meta, bf16[96,1024]{1,0:T(8,128)(2,1)S(1)} %collective-permute-done.32.refs_0_, bf16[96,1024]{1,0:T(8,128)(2,1)S(1)} %collective-permute-done.28.refs_1_, bf16[96,1024]{1,0:T(8,128)(2,1)S(1)} %collective-permute-done.36.refs_2_, ...), custom_call_target="tpu_custom_call" | custom-call | flops 805306368 | bytes 4194304 | tf_op jit(solution)/shard_map/pallas_call | solution.py:447
  108.4 1.6 %shard_map.89.refs_3_ = f32[192,1024]{1,0:T(8,128)S(1)} custom-call(s32[4]{0:T(128)S(1)} %pad_add_fusion.meta, bf16[96,1024]{1,0:T(8,128)(2,1)S(1)} %collective-permute-done.33.refs_0_, bf16[96,1024]{1,0:T(8,128)(2,1)S(1)} %collective-permute-done.29.refs_1_, bf16[96,1024]{1,0:T(8,128)(2,1)S(1)} %collective-permute-done.34.refs_2_, ...), custom_call_target="tpu_custom_call" | custom-call | flops 805306368 | bytes 4194304 | tf_op jit(solution)/shard_map/pallas_call | solution.py:447
  110.0 1.4 %shard_map.90.refs_6_ = f32[96,1024]{1,0:T(8,128)S(1)} custom-call(s32[4]{0:T(128)S(1)} %pad_add_fusion.meta, bf16[96,1024]{1,0:T(8,128)(2,1)S(1)} %collective-permute-done.40.refs_0_, bf16[96,1024]{1,0:T(8,128)(2,1)S(1)} %collective-permute-done.41.refs_1_, bf16[8192,1024]{1,0:T(8,128)(2,1)S(1)} %get-tuple-element.25.rest_6_.refs_4_.refs_2_.rest_7_, ...), custom_call_target="tpu_custom_call" | custom-call | flops 402653184 | bytes 4194304 | tf_op jit(solution)/shard_map/pallas_call | solution.py:447
  111.4 2.3 %shard_map.91 = f32[1,2,96,1024]{3,2,1,0:T(8,128)} custom-call(s32[4]{0:T(128)S(1)} %pad_add_fusion.meta, bf16[96,1024]{1,0:T(8,128)(2,1)S(1)} %collective-permute-done.30.refs_0_, bf16[96,1024]{1,0:T(8,128)(2,1)S(1)} %collective-permute-done.31.refs_1_, bf16[8192,1024]{1,0:T(8,128)(2,1)S(1)} %get-tuple-element.25.rest_6_.refs_4_.refs_2_.rest_7_, ...), custom_call_target="tpu_custom_call" | custom-call | flops 402653184 | bytes 4194304 | tf_op jit(solution)/shard_map/pallas_call | solution.py:447
  (60 shorter events, 4.2 us)
Async XLA Ops:
  0.0 20.6 %copy-start = (f32[1,2048]{1,0:T(1,128)S(1)}, f32[1,2048]{1,0:T(1,128)}, u32[]{:S(2)}) copy-start(f32[1,2048]{1,0:T(1,128)} %rest_1_.3) | copy-start | bytes 24580
  8.2 12.4 %collective-permute-start = (f32[2,16,1024]{2,1,0:T(8,128)S(1)}, f32[2,16,1024]{2,1,0:T(8,128)S(1)}, u32[]{:S(2)}, u32[]{:S(2)}) collective-permute-start(f32[2,16,1024]{2,1,0:T(8,128)S(1)} %slice_bitcast_fusion), channel_id=1, source_target_pairs={{0,1},{1,0},{2,3},{3,2},{4,5},{5,4},{6,7},{7,6},{8,9},{9,8},{10,11... | collective-permute-start | bytes 393224 | tf_op jit(solution)/shard_map/ppermute | solution.py:487
  12.8 6.3 %collective-permute-start.1 = (f32[2,8,96]{2,1,0:T(8,128)S(1)}, f32[2,8,96]{2,1,0:T(8,128)S(1)}, u32[]{:S(2)}, u32[]{:S(2)}) collective-permute-start(f32[2,8,96]{2,1,0:T(8,128)S(1)} %get-tuple-element.26.rest_7_.rest_8_), channel_id=1, source_target_pairs={{0,4},{4,12},{12,8},{8,0},{1,5},{5,13},{13,9},{9,1},{2,6},{6,14},{... | collective-permute-start | bytes 18440 | tf_op jit(solution)/shard_map/ppermute | solution.py:482
  15.6 4.3 %collective-permute-start.2 = (f32[2,8,96]{2,1,0:T(8,128)S(1)}, f32[2,8,96]{2,1,0:T(8,128)S(1)}, u32[]{:S(2)}, u32[]{:S(2)}) collective-permute-start(f32[2,8,96]{2,1,0:T(8,128)S(1)} %get-tuple-element.26.rest_7_.rest_8_), channel_id=1, source_target_pairs={{0,12},{4,8},{12,0},{8,4},{1,13},{5,9},{13,1},{9,5},{2,14},{6,10},... | collective-permute-start | bytes 18440 | tf_op jit(solution)/shard_map/ppermute | solution.py:482
  17.8 2.8 %collective-permute-start.3 = (f32[2,8,96]{2,1,0:T(8,128)S(1)}, f32[2,8,96]{2,1,0:T(8,128)S(1)}, u32[]{:S(2)}, u32[]{:S(2)}) collective-permute-start(f32[2,8,96]{2,1,0:T(8,128)S(1)} %get-tuple-element.26.rest_7_.rest_8_), channel_id=1, source_target_pairs={{0,8},{4,0},{12,4},{8,12},{1,9},{5,1},{13,5},{9,13},{2,10},{6,2},{... | collective-permute-start | bytes 18440 | tf_op jit(solution)/shard_map/ppermute | solution.py:482
  23.3 6.1 %collective-permute-start.8 = (bf16[96,1024]{1,0:T(8,128)(2,1)S(1)}, bf16[96,1024]{1,0:T(8,128)(2,1)S(1)}, u32[]{:S(2)}, u32[]{:S(2)}) collective-permute-start(bf16[96,1024]{1,0:T(8,128)(2,1)S(1)} %get-tuple-element.28.refs_0_), channel_id=1, source_target_pairs={{0,4},{4,12},{12,8},{8,0},{1,5},{5,13},{13,9},{9,1},{2,6},{6,14},{... | collective-permute-start | bytes 589832 | tf_op jit(solution)/shard_map/ppermute | solution.py:482
  27.2 6.4 %collective-permute-start.4 = (bf16[96,1024]{1,0:T(8,128)(2,1)S(1)}, bf16[96,1024]{1,0:T(8,128)(2,1)S(1)}, u32[]{:S(2)}, u32[]{:S(2)}) collective-permute-start(bf16[96,1024]{1,0:T(8,128)(2,1)S(1)} %gate.5.refs_1_), channel_id=1, source_target_pairs={{0,4},{4,12},{12,8},{8,0},{1,5},{5,13},{13,9},{9,1},{2,6},{6,14},{... | collective-permute-start | bytes 589832 | tf_op jit(solution)/shard_map/ppermute | solution.py:482
  29.3 9.2 %collective-permute-start.9 = (bf16[96,1024]{1,0:T(8,128)(2,1)S(1)}, bf16[96,1024]{1,0:T(8,128)(2,1)S(1)}, u32[]{:S(2)}, u32[]{:S(2)}) collective-permute-start(bf16[96,1024]{1,0:T(8,128)(2,1)S(1)} %collective-permute-done.8.refs_0_), channel_id=1, source_target_pairs={{0,4},{4,12},{12,8},{8,0},{1,5},{5,13},{13,9},{9,1},{2,6},{6,14},{... | collective-permute-start | bytes 589832 | tf_op jit(solution)/shard_map/ppermute | solution.py:482
  33.6 8.2 %collective-permute-start.5 = (bf16[96,1024]{1,0:T(8,128)(2,1)S(1)}, bf16[96,1024]{1,0:T(8,128)(2,1)S(1)}, u32[]{:S(2)}, u32[]{:S(2)}) collective-permute-start(bf16[96,1024]{1,0:T(8,128)(2,1)S(1)} %collective-permute-done.4.refs_1_), channel_id=1, source_target_pairs={{0,4},{4,12},{12,8},{8,0},{1,5},{5,13},{13,9},{9,1},{2,6},{6,14},{... | collective-permute-start | bytes 589832 | tf_op jit(solution)/shard_map/ppermute | solution.py:482
  33.6 8.2 %collective-permute-start.15 = (bf16[96,1024]{1,0:T(8,128)(2,1)S(1)}, bf16[96,1024]{1,0:T(8,128)(2,1)S(1)}, u32[]{:S(2)}, u32[]{:S(2)}) collective-permute-start(bf16[96,1024]{1,0:T(8,128)(2,1)S(1)} %gate.5.refs_1_), channel_id=1, source_target_pairs={{0,1},{1,0},{2,3},{3,2},{4,5},{5,4},{6,7},{7,6},{8,9},{9,8},{10,11... | collective-permute-start | bytes 589832 | tf_op jit(solution)/shard_map/ppermute | solution.py:487
  38.0 8.0 %collective-permute-start.14 = (bf16[96,1024]{1,0:T(8,128)(2,1)S(1)}, bf16[96,1024]{1,0:T(8,128)(2,1)S(1)}, u32[]{:S(2)}, u32[]{:S(2)}) collective-permute-start(bf16[96,1024]{1,0:T(8,128)(2,1)S(1)} %get-tuple-element.28.refs_0_), channel_id=1, source_target_pairs={{0,1},{1,0},{2,3},{3,2},{4,5},{5,4},{6,7},{7,6},{8,9},{9,8},{10,11... | collective-permute-start | bytes 589832 | tf_op jit(solution)/shard_map/ppermute | solution.py:487
  38.0 8.1 %collective-permute-start.13 = (bf16[96,1024]{1,0:T(8,128)(2,1)S(1)}, bf16[96,1024]{1,0:T(8,128)(2,1)S(1)}, u32[]{:S(2)}, u32[]{:S(2)}) collective-permute-start(bf16[96,1024]{1,0:T(8,128)(2,1)S(1)} %collective-permute-done.4.refs_1_), channel_id=1, source_target_pairs={{0,1},{1,0},{2,3},{3,2},{4,5},{5,4},{6,7},{7,6},{8,9},{9,8},{10,11... | collective-permute-start | bytes 589832 | tf_op jit(solution)/shard_map/ppermute | solution.py:487
  38.5 8.0 %collective-permute-start.21 = (bf16[96,1024]{1,0:T(8,128)(2,1)S(1)}, bf16[96,1024]{1,0:T(8,128)(2,1)S(1)}, u32[]{:S(2)}, u32[]{:S(2)}) collective-permute-start(bf16[96,1024]{1,0:T(8,128)(2,1)S(1)} %collective-permute-done.9.refs_0_), channel_id=1, source_target_pairs={{0,4},{4,12},{12,8},{8,0},{1,5},{5,13},{13,9},{9,1},{2,6},{6,14},{... | collective-permute-start | bytes 589832 | tf_op jit(solution)/shard_map/ppermute | solution.py:482
  41.7 8.7 %collective-permute-start.6 = (bf16[96,1024]{1,0:T(8,128)(2,1)S(1)}, bf16[96,1024]{1,0:T(8,128)(2,1)S(1)}, u32[]{:S(2)}, u32[]{:S(2)}) collective-permute-start(bf16[96,1024]{1,0:T(8,128)(2,1)S(1)} %collective-permute-done.5.refs_1_), channel_id=1, source_target_pairs={{0,4},{4,12},{12,8},{8,0},{1,5},{5,13},{13,9},{9,1},{2,6},{6,14},{... | collective-permute-start | bytes 589832 | tf_op jit(solution)/shard_map/ppermute | solution.py:482
  41.7 12.4 %collective-permute-start.12 = (bf16[96,1024]{1,0:T(8,128)(2,1)S(1)}, bf16[96,1024]{1,0:T(8,128)(2,1)S(1)}, u32[]{:S(2)}, u32[]{:S(2)}) collective-permute-start(bf16[96,1024]{1,0:T(8,128)(2,1)S(1)} %collective-permute-done.8.refs_0_), channel_id=1, source_target_pairs={{0,1},{1,0},{2,3},{3,2},{4,5},{5,4},{6,7},{7,6},{8,9},{9,8},{10,11... | collective-permute-start | bytes 589832 | tf_op jit(solution)/shard_map/ppermute | solution.py:487
  46.0 9.8 %collective-permute-start.11 = (bf16[96,1024]{1,0:T(8,128)(2,1)S(1)}, bf16[96,1024]{1,0:T(8,128)(2,1)S(1)}, u32[]{:S(2)}, u32[]{:S(2)}) collective-permute-start(bf16[96,1024]{1,0:T(8,128)(2,1)S(1)} %collective-permute-done.5.refs_1_), channel_id=1, source_target_pairs={{0,1},{1,0},{2,3},{3,2},{4,5},{5,4},{6,7},{7,6},{8,9},{9,8},{10,11... | collective-permute-start | bytes 589832 | tf_op jit(solution)/shard_map/ppermute | solution.py:487
  46.1 9.7 %collective-permute-start.10 = (bf16[96,1024]{1,0:T(8,128)(2,1)S(1)}, bf16[96,1024]{1,0:T(8,128)(2,1)S(1)}, u32[]{:S(2)}, u32[]{:S(2)}) collective-permute-start(bf16[96,1024]{1,0:T(8,128)(2,1)S(1)} %collective-permute-done.9.refs_0_), channel_id=1, source_target_pairs={{0,1},{1,0},{2,3},{3,2},{4,5},{5,4},{6,7},{7,6},{8,9},{9,8},{10,11... | collective-permute-start | bytes 589832 | tf_op jit(solution)/shard_map/ppermute | solution.py:487
  46.5 10.8 %collective-permute-start.22 = (bf16[96,1024]{1,0:T(8,128)(2,1)S(1)}, bf16[96,1024]{1,0:T(8,128)(2,1)S(1)}, u32[]{:S(2)}, u32[]{:S(2)}) collective-permute-start(bf16[96,1024]{1,0:T(8,128)(2,1)S(1)} %collective-permute-done.21.refs_0_), channel_id=1, source_target_pairs={{0,1},{1,0},{2,3},{3,2},{4,5},{5,4},{6,7},{7,6},{8,9},{9,8},{10,11... | collective-permute-start | bytes 589832 | tf_op jit(solution)/shard_map/ppermute | solution.py:487
  50.4 9.8 %collective-permute-start.7 = (bf16[96,1024]{1,0:T(8,128)(2,1)S(1)}, bf16[96,1024]{1,0:T(8,128)(2,1)S(1)}, u32[]{:S(2)}, u32[]{:S(2)}) collective-permute-start(bf16[96,1024]{1,0:T(8,128)(2,1)S(1)} %collective-permute-done.6.refs_0_), channel_id=1, source_target_pairs={{0,1},{1,0},{2,3},{3,2},{4,5},{5,4},{6,7},{7,6},{8,9},{9,8},{10,11... | collective-permute-start | bytes 589832 | tf_op jit(solution)/shard_map/ppermute | solution.py:487
  59.0 12.8 %collective-permute-start.23 = (bf16[96,1024]{1,0:T(8,128)(2,1)S(1)}, bf16[96,1024]{1,0:T(8,128)(2,1)S(1)}, u32[]{:S(2)}, u32[]{:S(2)}) collective-permute-start(bf16[96,1024]{1,0:T(8,128)(2,1)S(1)} %get-tuple-element.31), channel_id=1, source_target_pairs={{0,2},{2,0},{1,3},{3,1},{4,6},{6,4},{5,7},{7,5},{8,10},{10,8},{9,1... | collective-permute-start | bytes 589832 | tf_op jit(solution)/shard_map/ppermute | solution.py:490
  61.9 14.5 %collective-permute-start.16 = (bf16[96,1024]{1,0:T(8,128)(2,1)S(1)}, bf16[96,1024]{1,0:T(8,128)(2,1)S(1)}, u32[]{:S(2)}, u32[]{:S(2)}) collective-permute-start(bf16[96,1024]{1,0:T(8,128)(2,1)S(1)} %get-tuple-element.29), channel_id=1, source_target_pairs={{0,2},{2,0},{1,3},{3,1},{4,6},{6,4},{5,7},{7,5},{8,10},{10,8},{9,1... | collective-permute-start | bytes 589832 | tf_op jit(solution)/shard_map/ppermute | solution.py:490
  62.2 1.4 %collective-permute-start.24 = (f32[8,96]{1,0:T(8,128)S(1)}, f32[8,96]{1,0:T(8,128)S(1)}, u32[]{:S(2)}, u32[]{:S(2)}) collective-permute-start(f32[8,96]{1,0:T(8,128)S(1)} %get-tuple-element.32), channel_id=1, source_target_pairs={{0,1},{1,0},{2,3},{3,2},{4,5},{5,4},{6,7},{7,6},{8,9},{9,8},{10,11... | collective-permute-start | bytes 9224 | tf_op jit(solution)/shard_map/ppermute | solution.py:487
  62.8 1.2 %collective-permute-start.17 = (f32[8,96]{1,0:T(8,128)S(1)}, f32[8,96]{1,0:T(8,128)S(1)}, u32[]{:S(2)}, u32[]{:S(2)}) collective-permute-start(f32[8,96]{1,0:T(8,128)S(1)} %get-tuple-element.30), channel_id=1, source_target_pairs={{0,1},{1,0},{2,3},{3,2},{4,5},{5,4},{6,7},{7,6},{8,9},{9,8},{10,11... | collective-permute-start | bytes 9224 | tf_op jit(solution)/shard_map/ppermute | solution.py:487
  63.6 2.8 %collective-permute-start.25 = (f32[8,96]{1,0:T(8,128)S(1)}, f32[8,96]{1,0:T(8,128)S(1)}, u32[]{:S(2)}, u32[]{:S(2)}) collective-permute-start(f32[8,96]{1,0:T(8,128)S(1)} %add.14), channel_id=1, source_target_pairs={{0,4},{4,0},{8,12},{12,8},{1,5},{5,1},{9,13},{13,9},{2,6},{6,2},{1... | collective-permute-start | bytes 9224 | tf_op jit(solution)/shard_map/ppermute | solution.py:493
  64.0 5.0 %collective-permute-start.18 = (f32[8,96]{1,0:T(8,128)S(1)}, f32[8,96]{1,0:T(8,128)S(1)}, u32[]{:S(2)}, u32[]{:S(2)}) collective-permute-start(f32[8,96]{1,0:T(8,128)S(1)} %add.12), channel_id=1, source_target_pairs={{0,4},{4,0},{8,12},{12,8},{1,5},{5,1},{9,13},{13,9},{2,6},{6,2},{1... | collective-permute-start | bytes 9224 | tf_op jit(solution)/shard_map/ppermute | solution.py:493
  66.4 3.8 %collective-permute-start.26 = (f32[8,96]{1,0:T(8,128)S(1)}, f32[8,96]{1,0:T(8,128)S(1)}, u32[]{:S(2)}, u32[]{:S(2)}) collective-permute-start(f32[8,96]{1,0:T(8,128)S(1)} %add.15), channel_id=1, source_target_pairs={{0,2},{2,0},{4,6},{6,4},{8,10},{10,8},{12,14},{14,12},{1,3},{3,1},... | collective-permute-start | bytes 9224 | tf_op jit(solution)/shard_map/ppermute | solution.py:500
  67.6 4.3 %collective-permute-start.27 = (f32[8,96]{1,0:T(8,128)S(1)}, f32[8,96]{1,0:T(8,128)S(1)}, u32[]{:S(2)}, u32[]{:S(2)}) collective-permute-start(f32[8,96]{1,0:T(8,128)S(1)} %add.15), channel_id=1, source_target_pairs={{0,10},{2,8},{4,14},{6,12},{8,2},{10,0},{12,6},{14,4},{1,11},{3,9}... | collective-permute-start | bytes 9224 | tf_op jit(solution)/shard_map/ppermute | solution.py:500
  69.0 7.4 %collective-permute-start.19 = (f32[8,96]{1,0:T(8,128)S(1)}, f32[8,96]{1,0:T(8,128)S(1)}, u32[]{:S(2)}, u32[]{:S(2)}) collective-permute-start(f32[8,96]{1,0:T(8,128)S(1)} %add.13), channel_id=1, source_target_pairs={{0,2},{2,0},{4,6},{6,4},{8,10},{10,8},{12,14},{14,12},{1,3},{3,1},... | collective-permute-start | bytes 9224 | tf_op jit(solution)/shard_map/ppermute | solution.py:500
  70.2 6.2 %collective-permute-start.20 = (f32[8,96]{1,0:T(8,128)S(1)}, f32[8,96]{1,0:T(8,128)S(1)}, u32[]{:S(2)}, u32[]{:S(2)}) collective-permute-start(f32[8,96]{1,0:T(8,128)S(1)} %add.13), channel_id=1, source_target_pairs={{0,10},{2,8},{4,14},{6,12},{8,2},{10,0},{12,6},{14,4},{1,11},{3,9}... | collective-permute-start | bytes 9224 | tf_op jit(solution)/shard_map/ppermute | solution.py:500
  74.6 6.2 %collective-permute-start.32 = (bf16[96,1024]{1,0:T(8,128)(2,1)S(1)}, bf16[96,1024]{1,0:T(8,128)(2,1)S(1)}, u32[]{:S(2)}, u32[]{:S(2)}) collective-permute-start(bf16[96,1024]{1,0:T(8,128)(2,1)S(1)} %get-tuple-element.34.refs_0_), channel_id=1, source_target_pairs={{0,4},{4,12},{12,8},{8,0},{1,5},{5,13},{13,9},{9,1},{2,6},{6,14},{... | collective-permute-start | bytes 589832 | tf_op jit(solution)/shard_map/ppermute | solution.py:482
  79.6 5.6 %collective-permute-start.28 = (bf16[96,1024]{1,0:T(8,128)(2,1)S(1)}, bf16[96,1024]{1,0:T(8,128)(2,1)S(1)}, u32[]{:S(2)}, u32[]{:S(2)}) collective-permute-start(bf16[96,1024]{1,0:T(8,128)(2,1)S(1)} %gate.7.refs_1_), channel_id=1, source_target_pairs={{0,4},{4,12},{12,8},{8,0},{1,5},{5,13},{13,9},{9,1},{2,6},{6,14},{... | collective-permute-start | bytes 589832 | tf_op jit(solution)/shard_map/ppermute | solution.py:482
  80.8 11.5 %collective-permute-start.33 = (bf16[96,1024]{1,0:T(8,128)(2,1)S(1)}, bf16[96,1024]{1,0:T(8,128)(2,1)S(1)}, u32[]{:S(2)}, u32[]{:S(2)}) collective-permute-start(bf16[96,1024]{1,0:T(8,128)(2,1)S(1)} %collective-permute-done.32.refs_0_), channel_id=1, source_target_pairs={{0,4},{4,12},{12,8},{8,0},{1,5},{5,13},{13,9},{9,1},{2,6},{6,14},{... | collective-permute-start | bytes 589832 | tf_op jit(solution)/shard_map/ppermute | solution.py:482
  85.2 8.6 %collective-permute-start.29 = (bf16[96,1024]{1,0:T(8,128)(2,1)S(1)}, bf16[96,1024]{1,0:T(8,128)(2,1)S(1)}, u32[]{:S(2)}, u32[]{:S(2)}) collective-permute-start(bf16[96,1024]{1,0:T(8,128)(2,1)S(1)} %collective-permute-done.28.refs_1_), channel_id=1, source_target_pairs={{0,4},{4,12},{12,8},{8,0},{1,5},{5,13},{13,9},{9,1},{2,6},{6,14},{... | collective-permute-start | bytes 589832 | tf_op jit(solution)/shard_map/ppermute | solution.py:482
  85.5 8.3 %collective-permute-start.39 = (bf16[96,1024]{1,0:T(8,128)(2,1)S(1)}, bf16[96,1024]{1,0:T(8,128)(2,1)S(1)}, u32[]{:S(2)}, u32[]{:S(2)}) collective-permute-start(bf16[96,1024]{1,0:T(8,128)(2,1)S(1)} %gate.7.refs_1_), channel_id=1, source_target_pairs={{0,1},{1,0},{2,3},{3,2},{4,5},{5,4},{6,7},{7,6},{8,9},{9,8},{10,11... | collective-permute-start | bytes 589832 | tf_op jit(solution)/shard_map/ppermute | solution.py:487
  91.7 6.6 %collective-permute-start.38 = (bf16[96,1024]{1,0:T(8,128)(2,1)S(1)}, bf16[96,1024]{1,0:T(8,128)(2,1)S(1)}, u32[]{:S(2)}, u32[]{:S(2)}) collective-permute-start(bf16[96,1024]{1,0:T(8,128)(2,1)S(1)} %get-tuple-element.34.refs_0_), channel_id=1, source_target_pairs={{0,1},{1,0},{2,3},{3,2},{4,5},{5,4},{6,7},{7,6},{8,9},{9,8},{10,11... | collective-permute-start | bytes 589832 | tf_op jit(solution)/shard_map/ppermute | solution.py:487
  91.7 6.7 %collective-permute-start.37 = (bf16[96,1024]{1,0:T(8,128)(2,1)S(1)}, bf16[96,1024]{1,0:T(8,128)(2,1)S(1)}, u32[]{:S(2)}, u32[]{:S(2)}) collective-permute-start(bf16[96,1024]{1,0:T(8,128)(2,1)S(1)} %collective-permute-done.28.refs_1_), channel_id=1, source_target_pairs={{0,1},{1,0},{2,3},{3,2},{4,5},{5,4},{6,7},{7,6},{8,9},{9,8},{10,11... | collective-permute-start | bytes 589832 | tf_op jit(solution)/shard_map/ppermute | solution.py:487
  92.2 6.6 %collective-permute-start.40 = (bf16[96,1024]{1,0:T(8,128)(2,1)S(1)}, bf16[96,1024]{1,0:T(8,128)(2,1)S(1)}, u32[]{:S(2)}, u32[]{:S(2)}) collective-permute-start(bf16[96,1024]{1,0:T(8,128)(2,1)S(1)} %collective-permute-done.33.refs_0_), channel_id=1, source_target_pairs={{0,4},{4,12},{12,8},{8,0},{1,5},{5,13},{13,9},{9,1},{2,6},{6,14},{... | collective-permute-start | bytes 589832 | tf_op jit(solution)/shard_map/ppermute | solution.py:482
  93.8 9.2 %collective-permute-start.30 = (bf16[96,1024]{1,0:T(8,128)(2,1)S(1)}, bf16[96,1024]{1,0:T(8,128)(2,1)S(1)}, u32[]{:S(2)}, u32[]{:S(2)}) collective-permute-start(bf16[96,1024]{1,0:T(8,128)(2,1)S(1)} %collective-permute-done.29.refs_1_), channel_id=1, source_target_pairs={{0,4},{4,12},{12,8},{8,0},{1,5},{5,13},{13,9},{9,1},{2,6},{6,14},{... | collective-permute-start | bytes 589832 | tf_op jit(solution)/shard_map/ppermute | solution.py:482
  93.9 13.0 %collective-permute-start.36 = (bf16[96,1024]{1,0:T(8,128)(2,1)S(1)}, bf16[96,1024]{1,0:T(8,128)(2,1)S(1)}, u32[]{:S(2)}, u32[]{:S(2)}) collective-permute-start(bf16[96,1024]{1,0:T(8,128)(2,1)S(1)} %collective-permute-done.32.refs_0_), channel_id=1, source_target_pairs={{0,1},{1,0},{2,3},{3,2},{4,5},{5,4},{6,7},{7,6},{8,9},{9,8},{10,11... | collective-permute-start | bytes 589832 | tf_op jit(solution)/shard_map/ppermute | solution.py:487
  98.3 10.1 %collective-permute-start.35 = (bf16[96,1024]{1,0:T(8,128)(2,1)S(1)}, bf16[96,1024]{1,0:T(8,128)(2,1)S(1)}, u32[]{:S(2)}, u32[]{:S(2)}) collective-permute-start(bf16[96,1024]{1,0:T(8,128)(2,1)S(1)} %collective-permute-done.29.refs_1_), channel_id=1, source_target_pairs={{0,1},{1,0},{2,3},{3,2},{4,5},{5,4},{6,7},{7,6},{8,9},{9,8},{10,11... | collective-permute-start | bytes 589832 | tf_op jit(solution)/shard_map/ppermute | solution.py:487
  98.4 10.0 %collective-permute-start.34 = (bf16[96,1024]{1,0:T(8,128)(2,1)S(1)}, bf16[96,1024]{1,0:T(8,128)(2,1)S(1)}, u32[]{:S(2)}, u32[]{:S(2)}) collective-permute-start(bf16[96,1024]{1,0:T(8,128)(2,1)S(1)} %collective-permute-done.33.refs_0_), channel_id=1, source_target_pairs={{0,1},{1,0},{2,3},{3,2},{4,5},{5,4},{6,7},{7,6},{8,9},{9,8},{10,11... | collective-permute-start | bytes 589832 | tf_op jit(solution)/shard_map/ppermute | solution.py:487
  98.8 11.2 %collective-permute-start.41 = (bf16[96,1024]{1,0:T(8,128)(2,1)S(1)}, bf16[96,1024]{1,0:T(8,128)(2,1)S(1)}, u32[]{:S(2)}, u32[]{:S(2)}) collective-permute-start(bf16[96,1024]{1,0:T(8,128)(2,1)S(1)} %collective-permute-done.40.refs_0_), channel_id=1, source_target_pairs={{0,1},{1,0},{2,3},{3,2},{4,5},{5,4},{6,7},{7,6},{8,9},{9,8},{10,11... | collective-permute-start | bytes 589832 | tf_op jit(solution)/shard_map/ppermute | solution.py:487
  103.0 8.4 %collective-permute-start.31 = (bf16[96,1024]{1,0:T(8,128)(2,1)S(1)}, bf16[96,1024]{1,0:T(8,128)(2,1)S(1)}, u32[]{:S(2)}, u32[]{:S(2)}) collective-permute-start(bf16[96,1024]{1,0:T(8,128)(2,1)S(1)} %collective-permute-done.30.refs_0_), channel_id=1, source_target_pairs={{0,1},{1,0},{2,3},{3,2},{4,5},{5,4},{6,7},{7,6},{8,9},{9,8},{10,11... | collective-permute-start | bytes 589832 | tf_op jit(solution)/shard_map/ppermute | solution.py:487

commit v2 on v1

--- a/solution.py
+++ b/solution.py
@@ -49,68 +49,6 @@
         piece = block[:, start : start + LANES]
         total = total + piece * piece
     return total
-
-
-def embed_body(chunks, meta, ids_any, table, x_out, sums_out, ids, held, rows_buf, sems):
-    spans, rows = sums_out.shape[0], sums_out.shape[2]
-    half = x_out.shape[2]
-    width = held.shape[1]
-    depth = held.shape[0] // chunks
-    copies = [
-        pltpu.make_async_copy(
-            table.at[pl.ds(c * depth, depth), :], held.at[pl.ds(c * depth, depth), :], sems.at[c]
-        )
-        for c in range(chunks)
-    ]
-    copies.append(pltpu.make_async_copy(ids_any, ids, sems.at[chunks]))
-    for copy in copies:
-        copy.start()
-    for copy in copies:
-        copy.wait()
-    for span in range(spans):
-
-        def fetch(i, carry):
-            rows_buf[pl.ds(i, 1), :] = held[pl.ds(ids[span, i], 1), :]
-            return carry
-
-        lax.fori_loop(0, rows, fetch, 0, unroll=8)
-        sums_out[span] = row_sums(lane_tiles_squared(rows_buf[...]))
-        for part in range(width // half):
-
-            @pl.when(meta[1] == part)
-            def _():
-                x_out[span] = rows_buf[:, part * half : (part + 1) * half]
-
-
-def embed_rows(ids, meta, table, half):
-    spans, rows = ids.shape
-    words, width = table.shape
-    chunks = 4 if words % (4 * SUB) == 0 else 1
-    return pl.pallas_call(
-        functools.partial(embed_body, chunks),
-        out_shape=(
-            jax.ShapeDtypeStruct((spans, rows, half), f32),
-            jax.ShapeDtypeStruct((spans, SUB, rows), f32),
-        ),
-        in_specs=[
-            pl.BlockSpec(memory_space=pltpu.SMEM),
-            pl.BlockSpec(memory_space=pl.ANY),
-            pl.BlockSpec(memory_space=pl.ANY),
-        ],
-        out_specs=(
-            pl.BlockSpec(memory_space=pltpu.VMEM),
-            pl.BlockSpec(memory_space=pltpu.VMEM),
-        ),
-        scratch_shapes=[
-            pltpu.SMEM((spans, rows), jnp.int32),
-            pltpu.VMEM((words, width), f32),
-            pltpu.VMEM((rows, width), f32),
-            pltpu.SemaphoreType.DMA((chunks + 1,)),
-        ],
-        compiler_params=params(8),
-        cost_estimate=cost(4 * spans * rows * width, 4 * words * width),
-        name="embed_rows",
-    )(meta, in_hbm(ids), in_hbm(table))
 
 
 def mode_rows(first, step8, rows, store):
@@ -128,42 +66,11 @@
     return jnp.broadcast_to(values[m : m + 1, :], (SUB, values.shape[1]))
 
 
-def history_body(chunk, wide, slot_total, meta, cache, rates_any, resid_any, weight, *rest):
-    states, taps, rates_out, resid_out, weight_out = rest[:5]
-    held_rows, rates_ref, resid_ref, sems, mode_sems = rest[5:]
-    slots, rows, width = cache.shape
-    half = taps.shape[1]
+def half_states(side, wide, per_chunk, slot_total, meta, first_span, fetch, held_rows, rates_ref, states):
+    slots, rows, half = held_rows.shape
     modes = rates_ref.shape[0]
-    chunks = width // chunk
-    per_chunk = chunk // wide
-    first_span, rank = meta[0], meta[1]
-
-    def lane_start(tile):
-        part = jnp.where(tile * wide < half, 1 - rank, rank)
-        return pl.multiple_of(part * half + lax.rem(tile * wide, half), LANES)
-
-    def fetch(j):
-        return pltpu.make_async_copy(
-            cache.at[:, :, pl.ds(lane_start(j * per_chunk), chunk)],
-            held_rows.at[:, :, pl.ds(pl.multiple_of(j * chunk, LANES), chunk)],
-            sems.at[j],
-        )
-
-    mode_copies = [
-        pltpu.make_async_copy(rates_any, rates_ref, mode_sems.at[0]),
-        pltpu.make_async_copy(resid_any, resid_ref, mode_sems.at[1]),
-    ]
-    weight_copy = pltpu.make_async_copy(weight, weight_out, mode_sems.at[2])
-    for copy in mode_copies:
-        copy.start()
-    for j in range(chunks):
-        fetch(j).start()
-    weight_copy.start()
-    for copy in mode_copies:
-        copy.wait()
-    own = pl.ds(pl.multiple_of(rank * half, LANES), half)
-    rates_out[...] = rates_ref[:, own]
-    resid_out[...] = resid_ref[:, own]
+    rank = meta[0]
+    part = 1 - rank if side == 0 else rank
 
     def one_tile(t, carry):
         @pl.when(lax.rem(t, per_chunk) == 0)
@@ -171,7 +78,7 @@
             fetch(t // per_chunk).wait()
 
         at = pl.ds(pl.multiple_of(t * wide, LANES), wide)
-        rates = rates_ref[:, pl.ds(lane_start(t), wide)]
+        rates = rates_ref[:, pl.ds(pl.multiple_of(part * half + t * wide, LANES), wide)]
         decay = jnp.exp(-rates)
         groups = [decay[g : g + SUB, :] for g in range(0, modes, SUB)]
         held = [[jnp.zeros((SUB, wide), f32) for _ in groups] for _ in range(slots)]
@@ -189,13 +96,151 @@
             total = jnp.concatenate(held[s], axis=0) * decay
             part_a = part_a + total * jnp.exp(-rates * (far - float(rows)))
             part_b = part_b + total * (jnp.exp(-rates * far) * kept)
-        out_at = pl.ds(pl.multiple_of(lax.rem(t * wide, half), LANES), wide)
-        side = (t * wide) // half
-        states[side, 0, :, out_at] = part_a
-        states[side, 1, :, out_at] = part_b
+        states[0, :, at] = part_a
+        states[1, :, at] = part_b
         return carry
 
-    lax.fori_loop(0, width // wide, one_tile, 0)
+    lax.fori_loop(0, half // wide, one_tile, 0)
+
+
+def tile_sizes(half):
+    chunk = 512 if half % 512 == 0 else LANES
+    return chunk, 2 * LANES if chunk % (2 * LANES) == 0 else LANES
+
+
+def slot_fetch(side, chunk, meta, cache, held_rows, sems):
+    half = held_rows.shape[2]
+    part = 1 - meta[0] if side == 0 else meta[0]
+
+    def fetch(j):
+        return pltpu.make_async_copy(
+            cache.at[:, :, pl.ds(pl.multiple_of(part * half + j * chunk, LANES), chunk)],
+            held_rows.at[:, :, pl.ds(pl.multiple_of(j * chunk, LANES), chunk)],
+            sems.at[j],
+        )
+
+    return fetch
+
+
+def open_body(pieces, sizes, slot_total, meta, span_any, ids_any, table, cache, rates_any, weight, *rest):
+    x_out, sums_out, states, weight_out = rest[:4]
+    ids, span_here, words, rows_buf, held_rows, rates_ref, sems, slot_sems = rest[4:]
+    chunk, wide = sizes
+    spans, rows = sums_out.shape[0], sums_out.shape[2]
+    half = x_out.shape[2]
+    width = words.shape[1]
+    depth = words.shape[0] // pieces
+    deep = weight.shape[0] // 2
+    fetch = slot_fetch(0, chunk, meta, cache, held_rows, slot_sems)
+    small = [
+        pltpu.make_async_copy(span_any, span_here, sems.at[pieces]),
+        pltpu.make_async_copy(rates_any, rates_ref, sems.at[pieces + 1]),
+    ]
+    copies = [
+        pltpu.make_async_copy(
+            table.at[pl.ds(c * depth, depth), :], words.at[pl.ds(c * depth, depth), :], sems.at[c]
+        )
+        for c in range(pieces)
+    ]
+    copies.append(pltpu.make_async_copy(ids_any, ids, sems.at[pieces + 2]))
+    weight_copy = pltpu.make_async_copy(
+        weight.at[pl.ds(0, deep), :], weight_out.at[pl.ds(0, deep), :], sems.at[pieces + 3]
+    )
+    for copy in small:
+        copy.start()
+    for j in range(half // chunk):
+        fetch(j).start()
+    for copy in copies:
+        copy.start()
+    weight_copy.start()
+    for copy in small:
+        copy.wait()
+    first_span = lax.rem(span_here[0], slot_total)
+    half_states(
+        0, wide, chunk // wide, slot_total, meta, first_span, fetch, held_rows, rates_ref, states
+    )
+    for copy in copies:
+        copy.wait()
+    for span in range(spans):
+
+        def look_up(i, carry, span=span):
+            rows_buf[pl.ds(i, 1), :] = words[pl.ds(ids[span, i], 1), :]
+            return carry
+
+        lax.fori_loop(0, rows, look_up, 0, unroll=8)
+        sums_out[span] = row_sums(lane_tiles_squared(rows_buf[...]))
+        for part in range(width // half):
+
+            @pl.when(meta[0] == part)
+            def _(part=part, span=span):
+                x_out[span] = rows_buf[:, part * half : (part + 1) * half]
+
+    weight_copy.wait()
+
+
+def open_step(meta, first, ids, table, cache, rates, weight, slot_total):
+    spans, rows = ids.shape
+    words, width = table.shape
+    slots = cache.shape[0]
+    modes = rates.shape[0]
+    half = weight.shape[1]
+    pieces = 4 if words % (4 * SUB) == 0 else 1
+    sizes = tile_sizes(half)
+    vmem, anywhere = pl.BlockSpec(memory_space=pltpu.VMEM), pl.BlockSpec(memory_space=pl.ANY)
+    return pl.pallas_call(
+        functools.partial(open_body, pieces, sizes, slot_total),
+        out_shape=(
+            jax.ShapeDtypeStruct((spans, rows, half), f32),
+            jax.ShapeDtypeStruct((spans, SUB, rows), f32),
+            jax.ShapeDtypeStruct((2, modes, half), f32),
+            pltpu.VMEM(weight.shape, weight.dtype),
+        ),
+        in_specs=[pl.BlockSpec(memory_space=pltpu.SMEM)] + [anywhere] * 6,
+        out_specs=(vmem,) * 4,
+        scratch_shapes=[
+            pltpu.SMEM((spans, rows), jnp.int32),
+            pltpu.SMEM((1,), jnp.int32),
+            pltpu.VMEM((words, width), f32),
+            pltpu.VMEM((rows, width), f32),
+            pltpu.VMEM((slots, rows, half), f32),
+            pltpu.VMEM((modes, width), f32),
+            pltpu.SemaphoreType.DMA((pieces + 4,)),
+            pltpu.SemaphoreType.DMA((half // sizes[0],)),
+        ],
+        compiler_params=params(10),
+        cost_estimate=cost(2 * slots * rows * modes * half, 4 * words * width),
+        name="open_step",
+    )(meta, first, in_hbm(ids), in_hbm(table), in_hbm(cache), in_hbm(rates), in_hbm(weight))
+
+
+def history_body(sizes, slot_total, meta, span_any, cache, rates_any, resid_any, weight, held_weight, *rest):
+    del held_weight
+    states, taps, rates_out, resid_out, weight_out = rest[:5]
+    span_here, held_rows, rates_ref, resid_ref, sems, slot_sems = rest[5:]
+    chunk, wide = sizes
+    _, rows, half = held_rows.shape
+    modes = rates_ref.shape[0]
+    rank = meta[0]
+    deep = weight.shape[0] // 2
+    fetch = slot_fetch(1, chunk, meta, cache, held_rows, slot_sems)
+    small = [
+        pltpu.make_async_copy(span_any, span_here, sems.at[0]),
+        pltpu.make_async_copy(rates_any, rates_ref, sems.at[1]),
+        pltpu.make_async_copy(resid_any, resid_ref, sems.at[2]),
+    ]
+    weight_copy = pltpu.make_async_copy(
+        weight.at[pl.ds(deep, deep), :], weight_out.at[pl.ds(deep, deep), :], sems.at[3]
+    )
+    for copy in small:
+        copy.start()
+    for j in range(half // chunk):
+        fetch(j).start()
+    weight_copy.start()
+    for copy in small:
+        copy.wait()
+    own = pl.ds(pl.multiple_of(rank * half, LANES), half)
+    rates_out[...] = rates_ref[:, own]
+    resid_out[...] = resid_ref[:, own]
 
     def tap_tile(t, carry):
         at = pl.ds(pl.multiple_of(rank * half + t * LANES, LANES), LANES)
@@ -212,38 +257,46 @@
         return carry
 
     lax.fori_loop(0, half // LANES, tap_tile, 0)
+    first_span = lax.rem(span_here[0], slot_total)
+    half_states(
+        1, wide, chunk // wide, slot_total, meta, first_span, fetch, held_rows, rates_ref, states
+    )
     weight_copy.wait()
 
 
-def history_states(meta, cache, rates, resid, weight, slot_total):
+def history_states(meta, first, cache, rates, resid, weight, held_weight, slot_total):
     slots, rows, width = cache.shape
     modes = rates.shape[0]
     half = weight.shape[1]
-    chunk = 512 if half % 512 == 0 else LANES
-    wide = 2 * LANES if chunk % (2 * LANES) == 0 else LANES
-    vmem = pl.BlockSpec(memory_space=pltpu.VMEM)
+    sizes = tile_sizes(half)
+    vmem, anywhere = pl.BlockSpec(memory_space=pltpu.VMEM), pl.BlockSpec(memory_space=pl.ANY)
     return pl.pallas_call(
-        functools.partial(history_body, chunk, wide, slot_total),
+        functools.partial(history_body, sizes, slot_total),
         out_shape=(
-            jax.ShapeDtypeStruct((2, 2, modes, half), f32),
+            jax.ShapeDtypeStruct((2, modes, half), f32),
             jax.ShapeDtypeStruct((rows, half), f32),
             jax.ShapeDtypeStruct((modes, half), f32),
             jax.ShapeDtypeStruct((modes, half), f32),
             pltpu.VMEM(weight.shape, weight.dtype),
         ),
-        in_specs=[pl.BlockSpec(memory_space=pltpu.SMEM)] + [pl.BlockSpec(memory_space=pl.ANY)] * 4,
-        out_specs=(vmem, vmem, vmem, vmem, vmem),
+        in_specs=[pl.BlockSpec(memory_space=pltpu.SMEM)] + [anywhere] * 6,
+        out_specs=(vmem,) * 5,
         scratch_shapes=[
-            pltpu.VMEM((slots, rows, width), f32),
+            pltpu.SMEM((1,), jnp.int32),
+            pltpu.VMEM((slots, rows, half), f32),
             pltpu.VMEM((modes, width), f32),
             pltpu.VMEM((modes, width), f32),
-            pltpu.SemaphoreType.DMA((width // chunk,)),
-            pltpu.SemaphoreType.DMA((3,)),
+            pltpu.SemaphoreType.DMA((4,)),
+            pltpu.SemaphoreType.DMA((half // sizes[0],)),
         ],
+        input_output_aliases={6: 4},
         compiler_params=params(6),
-        cost_estimate=cost(2 * slots * rows * modes * width, 4 * slots * rows * width),
+        cost_estimate=cost(2 * slots * rows * modes * half, 4 * slots * rows * half),
         name="history_states",
-    )(meta, in_hbm(cache), in_hbm(rates), in_hbm(resid), in_hbm(weight))
+    )(
+        meta, first, in_hbm(cache), in_hbm(rates), in_hbm(resid), in_hbm(weight),
+        in_vmem(held_weight),
+    )
 
 
 def gate_body(channels, span, counts, meta, base, *rest):
@@ -263,7 +316,7 @@
     rows, half = gated.shape
     modes = rates_ref.shape[0]
     blocks = rows // SUB
-    is_first = meta[2] == 1
+    is_first = meta[1] == 1
     wide = 4 * LANES if half % (4 * LANES) == 0 else LANES
 
     if n_before:
@@ -277,21 +330,21 @@
                 row = row_spread(before[0], r, at)
                 held = [h * d + row for h, d in zip(held, groups)]
             state_buf[:, at] = jnp.concatenate(held, axis=0) * decay + (
-                mine[1, span, :, at] + theirs[span, :, at]
+                mine[span, :, at] + theirs[span, :, at]
             )
             return carry
 
         lax.fori_loop(0, half // wide, chain, 0)
     else:
-        state_buf[...] = mine[1, span] + theirs[span]
+        state_buf[...] = mine[span] + theirs[span]
 
     sums = first_sums[0][span, 0:1, :]
     for ref in first_sums[1:]:
         sums = sums + ref[span, 0:1, :]
     if n_later:
-        later = later_sums[0][0:1, :]
+        later = later_sums[0][span, 0:1, :]
         for ref in later_sums[1:]:
-            later = later + ref[0:1, :]
+            later = later + ref[span, 0:1, :]
         sums = jnp.where(is_first, sums, later)
     here = lax.broadcasted_iota(jnp.int32, (rows, rows), 0)
     there = lax.broadcasted_iota(jnp.int32, (rows, rows), 1)
@@ -303,7 +356,7 @@
 
     def tile(t, carry):
         at = pl.ds(pl.multiple_of(t * LANES, LANES), LANES)
-        own = pl.ds(pl.multiple_of(meta[1] * half + t * LANES, LANES), LANES)
+        own = pl.ds(pl.multiple_of(meta[0] * half + t * LANES, LANES), LANES)
         current = base[span, :, at]
         if n_delta:
             current = current + jnp.where(is_first, 0.0, delta[0][:, at].astype(f32))
@@ -371,7 +424,7 @@
     return jnp.where(came <= count // 2, jnp.maximum(2 * came - 1, 0), 2 * (count - came))
 
 
-def mix_body(kind, chosen, counts, out_tile, step, meta, *refs):
+def mix_body(kind, chosen, counts, out_tile, step, own, meta, *refs):
     parts, n_acc, n_base, n_delta, n_done, seqs, tensors = counts
     refs = list(refs)
 
@@ -386,13 +439,19 @@
     if step is None:
         starts = [0] * parts
     else:
-        source = source_of(step, meta[3], tensors) * seqs
+        source = source_of(step, meta[2], tensors) * seqs
         starts = [
-            pl.multiple_of((source + jnp.where(p == 0, meta[1], seqs - 1 - meta[1])) * depth, depth)
-            for p in range(parts)
+            pl.multiple_of((source + (meta[0] if mine else seqs - 1 - meta[0])) * depth, depth)
+            for mine in own
         ]
     span = chosen[0]
     squares = jnp.zeros((rows, LANES), f32)
+    leaving = []
+    if kind == "out":
+        fresh_buf, sems = refs[1:]
+        for i, ref in enumerate(done):
+            leaving.append(pltpu.make_async_copy(ref, refs[0].at[0, i], sems.at[i]))
+            leaving[-1].start()
     for n in range(out // out_tile):
         at = slice(n * out_tile, (n + 1) * out_tile)
         total = None
@@ -408,7 +467,7 @@
             refs[0][:, at] = total
             continue
         if n_delta:
-            total = total + jnp.where(meta[2] == 1, 0.0, delta[0][:, at].astype(f32))
+            total = total + jnp.where(meta[1] == 1, 0.0, delta[0][:, at].astype(f32))
         fresh = base[0][span, :, at] + total
         if kind == "hop":
             refs[0][:, at] = total.astype(refs[0].dtype)
@@ -416,14 +475,22 @@
         elif kind == "done":
             refs[0][:, at] = fresh
         else:
-            refs[0][0, span, :, at] = fresh
-            for i, ref in enumerate(done):
-                refs[0][0, i, :, at] = ref[:, at]
+            fresh_buf[:, at] = fresh
+            leaving.append(
+                pltpu.make_async_copy(
+                    fresh_buf.at[:, at], refs[0].at[0, span, :, at], sems.at[len(done) + n]
+                )
+            )
+            leaving[-1].start()
+    for copy in leaving:
+        copy.wait()
     if kind == "hop":
-        refs[1][...] = row_sums(squares)
-
-
-def mix(kind, meta, step, pieces, chosen, weight, acc, base, delta, seqs, tensors, done=()):
+        for ref in done:
+            refs[1][0:span] = ref[0:span]
+        refs[1][span] = row_sums(squares)
+
+
+def mix(kind, meta, step, own, pieces, chosen, weight, acc, base, delta, seqs, tensors, done=()):
     rows, depth = pieces[0][0].shape
     out = weight.shape[1]
     vmem = pl.BlockSpec(memory_space=pltpu.VMEM)
@@ -438,17 +505,25 @@
     if kind == "hop":
         out_shape = (
             jax.ShapeDtypeStruct((rows, out), jnp.bfloat16),
-            jax.ShapeDtypeStruct((SUB, rows), f32),
+            jax.ShapeDtypeStruct((base.shape[0], SUB, rows), f32),
         )
         out_specs = (vmem, vmem)
     elif kind == "out":
         out_shape = jax.ShapeDtypeStruct((1, len(done) + 1, rows, out), f32)
+        out_specs = pl.BlockSpec(memory_space=pl.ANY)
     out_tile = 4 * LANES if out % (4 * LANES) == 0 else LANES
+    scratch = []
+    if kind == "out":
+        scratch = [
+            pltpu.VMEM((rows, out), f32),
+            pltpu.SemaphoreType.DMA((len(done) + out // out_tile,)),
+        ]
     return pl.pallas_call(
-        functools.partial(mix_body, kind, chosen, counts, out_tile, step),
+        functools.partial(mix_body, kind, chosen, counts, out_tile, step, own),
         out_shape=out_shape,
         in_specs=[pl.BlockSpec(memory_space=pltpu.SMEM)] + [vmem] * len(operands),
         out_specs=out_specs,
+        scratch_shapes=scratch,
         compiler_params=params(8),
         cost_estimate=cost(
             2 * rows * len(chosen) * depth * out * len(pieces), 2 * depth * out * len(pieces)
@@ -474,7 +549,6 @@
     rates, resid, cache, weight = decay_rates[0], residues[0], history[0], mix_weight[0]
     spans, _ = token_ids.shape
     slots, _, _ = cache.shape
-    half = weight.shape[1]
     slot_total = slots * seqs
     order = ring_order(tensors)
 
@@ -499,11 +573,12 @@
                 route.append((i * sections + s, (i ^ flip) * sections + (s + 1) % sections))
         return lax.ppermute(value, ("tensor", "section"), route)
 
-    first_span = lax.rem(leading_span_index[0], slot_total)
     is_first = (section_rank == 0).astype(jnp.int32)
-    meta = jnp.stack([first_span, seq_rank, is_first, tensor_rank]).astype(jnp.int32)
-
-    base, sums = embed_rows(token_ids, meta, embed_table, half)
+    meta = jnp.stack([seq_rank, is_first, tensor_rank]).astype(jnp.int32)
+
+    base, sums, for_partner, held_weight = open_step(
+        meta, leading_span_index, token_ids, embed_table, cache, rates, weight, slot_total
+    )
     small_ring = ring_fits(tensors)
     first_sums = [sums]
     if small_ring:
@@ -511,13 +586,14 @@
             first_sums.append(along_ring(sums, k))
     else:
         first_sums = [lax.psum(sums, "tensor")]
-    states, taps, *modes_here = history_states(meta, cache, rates, resid, weight, slot_total)
-    weight = modes_here.pop()
-    partner = swapped(states[0])
+    partner = swapped(for_partner)
+    states, taps, *modes_here, weight = history_states(
+        meta, leading_span_index, cache, rates, resid, weight, held_weight, slot_total
+    )
 
     every = tuple(range(spans))
     deltas = [None] * spans
-    later_sums = [[]] * spans
+    later_sums = []
     for stage in range(sections):
         last_stage = stage + 1 == sections
         gates = []
@@ -525,7 +601,7 @@
         for span in every:
             got = gate(
                 meta, base, deltas[span], norm_gain, modes_here, taps, weight, first_sums,
-                later_sums[span], [states, partner], before, span,
+                later_sums, [states, partner], before, span,
             )
             gates.append(got[0])
             before = list(got[1:])
@@ -548,34 +624,46 @@
                 step = None
                 pairs = [[lax.all_gather(g, ("tensor", "seq"), axis=1, tiled=True) for g in gates]]
             if not final:
-                acc = mix("part", meta, step, pairs, every, weight, acc, None, None, seqs, tensors)
+                acc = mix(
+                    "part", meta, step, (True, False), pairs, every, weight, acc, None, None,
+                    seqs, tensors,
+                )
                 continue
             for span in every:
                 kind = "hop" if not last_stage else "out" if span + 1 == spans else "done"
-                done = tuple(results) if kind == "out" else ()
+                done = ()
+                if kind == "out":
+                    done = tuple(results)
+                elif kind == "hop" and span > 0:
+                    done = (results[-1][1],)
+                acc_here, rest = acc, [[part[span]] for part in pairs]
+                own = (True, False)[: len(rest)]
+                if small_ring:
+                    acc_here = mix(
+                        "part", meta, step, own[:1], rest[:1], (span,), weight, acc, None, None,
+                        seqs, tensors,
+                    )
+                    own, rest = own[1:], rest[1:]
                 results.append(
                     mix(
-                        kind, meta, step, [[part[span]] for part in pairs], (span,), weight,
-                        acc, base, deltas[span], seqs, tensors, done,
+                        kind, meta, step, own, rest, (span,), weight, acc_here, base,
+                        deltas[span], seqs, tensors, done,
                     )
                 )
         if not last_stage:
-            new_deltas, new_sums = [], []
+            deltas = []
             for span in every:
-                moved, partial = results[span]
-                new_deltas.append(to_next(moved))
-                both = partial + swapped(partial)
-                if small_ring:
-                    bits = tensors.bit_length() - 1
-                    for bit in range(bits - 1):
-                        both = both + across(both, 1 << bit)
-                    got = []
-                    for k in range(2):
-                        got.append(to_next_across(both, k * tensors // 2))
-                    new_sums.append(got)
-                else:
-                    new_sums.append([to_next(lax.psum(both, "tensor"))])
-            deltas, later_sums = new_deltas, new_sums
+                deltas.append(to_next(results[span][0]))
+            both = results[-1][1]
+            both = both + swapped(both)
+            if small_ring:
+                for bit in range(tensors.bit_length() - 2):
+                    both = both + across(both, 1 << bit)
+                later_sums = []
+                for k in range(2):
+                    later_sums.append(to_next_across(both, k * tensors // 2))
+            else:
+                later_sums = [to_next(lax.psum(both, "tensor"))]
     return results[-1]
 
 

time: 114 us -> 111 us (0.974)
  starting transfers between devices: 59 us -> 38.8 us
  waiting for transfers between devices: 13.7 us -> 28.9 us
  Pallas kernels: 40 us -> 42 us
    ppermute x15, waiting for transfers between devices: 11.3 us -> 21.3 us  [along_ring(): lax.ppermute(value, 'tensor', [(order[i], order[(i + shift) % tensors]) f...]
    ppermute x19 -> x18, starting transfers between devices: 34.6 us -> 25 us  [swapped(): return lax.ppermute(value, 'seq', [(i, seqs - 1 - i) for i in range(seqs)])]
    ppermute x15, starting transfers between devices: 16.3 us -> 10.7 us  [along_ring(): lax.ppermute(value, 'tensor', [(order[i], order[(i + shift) % tensors]) f...]
    ppermute x4 -> x2, waiting for transfers between devices: 0.11 us -> 3.89 us  [to_next_across(): return lax.ppermute(value, ('tensor', 'section'), route)]
    ppermute x4 -> x2, starting transfers between devices: 5.35 us -> 1.62 us  [to_next_across(): return lax.ppermute(value, ('tensor', 'section'), route)]
    pallas_call x10 -> x14, Pallas kernels: 16.4 us -> 19 us  [mix(): pl.pallas_call(functools.partial(mix_body, kind, chosen, counts, out_tile...]
    ppermute x2 -> x1, waiting for transfers between devices: 1.28 us -> 2.79 us  [across(): lax.ppermute(value, 'tensor', [(i, i ^ flip) for i in range(tensors)])]
    ppermute x2 -> x1, starting transfers between devices: 1.32 us -> 0.01 us  [across(): lax.ppermute(value, 'tensor', [(i, i ^ flip) for i in range(tensors)])]
  transfers between devices with their start and end apart: 42 -> 38, of which waited for: 11 -> 12; matrix products, arithmetic and copies ran while one was open for 0% -> 0% of each run, Pallas kernels for 24% -> 28%
where the time goes in v2:
time: 111 us
  Pallas kernels  42 us (38%)
  starting transfers between devices  38.8 us (35%)
  waiting for transfers between devices  28.9 us (26%)
    ppermute x18, starting transfers between devices, swapped(): return lax.ppermute(value, 'seq', [(i, seqs - 1 - i) for i in range(seqs)])  25 us
    ppermute x15, waiting for transfers between devices, along_ring(): lax.ppermute(value, 'tensor', [(order[i], order[(i + shift) % tensors]) f...  21.3 us
    pallas_call x14, Pallas kernels, mix(): pl.pallas_call(functools.partial(mix_body, kind, chosen, counts, out_tile...  19 us
    pallas_call x4, Pallas kernels, gate(): pl.pallas_call(functools.partial(gate_body, weight.shape[0], span, counts...  11.7 us
    ppermute x15, starting transfers between devices, along_ring(): lax.ppermute(value, 'tensor', [(order[i], order[(i + shift) % tensors]) f...  10.7 us
    pallas_call x1, Pallas kernels, open_step(): pl.pallas_call(functools.partial(open_body, pieces, sizes, slot_total), o...  6.67 us
    pallas_call x1, Pallas kernels, history_states(): pl.pallas_call(functools.partial(history_body, sizes, slot_total), out_sh...  4.61 us
    ppermute x2, waiting for transfers between devices, to_next_across(): return lax.ppermute(value, ('tensor', 'section'), route)  3.89 us
  transfers between devices with their start and end apart: 38, of which 12 were waited for; matrix products, arithmetic and copies ran while one was open for 0% of the time, Pallas kernels for 28%

profile of v2, /device:TPU:1, one launch (start us, length us, event | category | flops | bytes accessed | tf_op | source)
XLA Modules:
  0.0 110.9 jit_solution(671620970212687772)
XLA Ops:
  0.7 6.7 %open_step.1 = (f32[2,96,1024]{2,1,0:T(8,128)S(1)}, f32[2,8,96]{2,1,0:T(8,128)S(1)}, f32[2,16,1024]{2,1,0:T(8,128)S(1)}, bf16[8192,1024]{1,0:T(8,128)(2,1)S(1)}) custom-call(s32[3]{0:T(128)S(1)} %pad_add_fusion.meta, s32[1]{0:T(128)S(6)} %copy.11.span_any, s32[2,96]{1,0:T(2,128)} %ids_any.1, f32[512,2048]{1,0:T(8,128)} %table.1, f32[4,96,2048]{2,1,0:T(8,128)} %bitcast.9, ...), custom_call_target="tpu_custom_call" | custom-call | flops 12582912 | bytes 4194304 | tf_op jit(solution)/shard_map/open_step/pallas_call | solution.py:190
  7.5 2.7 %collective-permute-start.1 = (f32[2,8,96]{2,1,0:T(8,128)S(1)}, f32[2,8,96]{2,1,0:T(8,128)S(1)}, u32[]{:S(2)}, u32[]{:S(2)}) collective-permute-start(f32[2,8,96]{2,1,0:T(8,128)S(1)} %get-tuple-element.30.rest_7_.rest_8_), channel_id=1, source_target_pairs={{0,4},{4,12},{12,8},{8,0},{1,5},{5,13},{13,9},{9,1},{2,6},{6,14},{... | collective-permute-start | bytes 18440 | tf_op jit(solution)/shard_map/ppermute | solution.py:556
  10.2 2.2 %collective-permute-start.2 = (f32[2,8,96]{2,1,0:T(8,128)S(1)}, f32[2,8,96]{2,1,0:T(8,128)S(1)}, u32[]{:S(2)}, u32[]{:S(2)}) collective-permute-start(f32[2,8,96]{2,1,0:T(8,128)S(1)} %get-tuple-element.30.rest_7_.rest_8_), channel_id=1, source_target_pairs={{0,12},{4,8},{12,0},{8,4},{1,13},{5,9},{13,1},{9,5},{2,14},{6,10},... | collective-permute-start | bytes 18440 | tf_op jit(solution)/shard_map/ppermute | solution.py:556
  12.4 1.3 %collective-permute-start.3 = (f32[2,8,96]{2,1,0:T(8,128)S(1)}, f32[2,8,96]{2,1,0:T(8,128)S(1)}, u32[]{:S(2)}, u32[]{:S(2)}) collective-permute-start(f32[2,8,96]{2,1,0:T(8,128)S(1)} %get-tuple-element.30.rest_7_.rest_8_), channel_id=1, source_target_pairs={{0,8},{4,0},{12,4},{8,12},{1,9},{5,1},{13,5},{9,13},{2,10},{6,2},{... | collective-permute-start | bytes 18440 | tf_op jit(solution)/shard_map/ppermute | solution.py:556
  13.7 4.6 %history_states.1 = (f32[2,16,1024]{2,1,0:T(8,128)S(1)}, f32[96,1024]{1,0:T(8,128)S(1)}, f32[16,1024]{1,0:T(8,128)S(1)}, f32[16,1024]{1,0:T(8,128)S(1)}, bf16[8192,1024]{1,0:T(8,128)(2,1)S(1)}) custom-call(s32[3]{0:T(128)S(1)} %pad_add_fusion.meta, s32[1]{0:T(128)S(6)} %copy.11.span_any, f32[4,96,2048]{2,1,0:T(8,128)} %bitcast.10, ...), custom_call_target="tpu_custom_call", output_to_operand_aliasing={{4}: (6, {})} | custom-call | flops 12582912 | bytes 1572864 | tf_op jit(solution)/shard_map/history_states/pallas_call | solution.py:273
  18.3 2.7 %gate.4 = (bf16[96,1024]{1,0:T(8,128)(2,1)S(1)}, f32[96,1024]{1,0:T(8,128)S(1)}) custom-call(s32[3]{0:T(128)S(1)} %pad_add_fusion.meta, f32[2,96,1024]{2,1,0:T(8,128)S(1)} %get-tuple-element.22.base.refs_3_, f32[1,2048]{1,0:T(1,128)S(1)} %copy-done, f32[16,1024]{1,0:T(8,128)S(1)} %get-tuple-element.24.rest_1_.rest_2_, ...), custom_call_target="tpu_custom_call" | custom-call | flops 15728640 | bytes 1179648 | tf_op jit(solution)/shard_map/gate/pallas_call | solution.py:409
  21.2 3.1 %gate.5.refs_1_ = bf16[96,1024]{1,0:T(8,128)(2,1)S(1)} custom-call(s32[3]{0:T(128)S(1)} %pad_add_fusion.meta, f32[2,96,1024]{2,1,0:T(8,128)S(1)} %get-tuple-element.22.base.refs_3_, f32[1,2048]{1,0:T(1,128)S(1)} %copy-done, f32[16,1024]{1,0:T(8,128)S(1)} %get-tuple-element.24.rest_1_.rest_2_, f32[16,1024]{1,0:T(8,128)S(1)} %get-tuple-element.25.rest_2_.rest_3_, ...), custom_call_target="tpu_custom_call" | custom-call | flops 15728640 | bytes 1179648 | tf_op jit(solution)/shard_map/gate/pallas_call | solution.py:409
  24.4 1.1 collective-permute-start.4
  25.4 2.1 %collective-permute-done.8.refs_0_ = bf16[96,1024]{1,0:T(8,128)(2,1)S(1)} collective-permute-done((bf16[96,1024]{1,0:T(8,128)(2,1)S(1)}, bf16[96,1024]{1,0:T(8,128)(2,1)S(1)}, u32[]{:S(2)}, u32[]{:S(2)}) %collective-permute-start.8) | collective-permute-done | bytes 196640 | tf_op jit(solution)/shard_map/ppermute | solution.py:556
  27.5 4.7 %collective-permute-done.4.refs_1_ = bf16[96,1024]{1,0:T(8,128)(2,1)S(1)} collective-permute-done((bf16[96,1024]{1,0:T(8,128)(2,1)S(1)}, bf16[96,1024]{1,0:T(8,128)(2,1)S(1)}, u32[]{:S(2)}, u32[]{:S(2)}) %collective-permute-start.4) | collective-permute-done | bytes 196640 | tf_op jit(solution)/shard_map/ppermute | solution.py:556
  32.3 2.2 %collective-permute-start.15 = (bf16[96,1024]{1,0:T(8,128)(2,1)S(1)}, bf16[96,1024]{1,0:T(8,128)(2,1)S(1)}, u32[]{:S(2)}, u32[]{:S(2)}) collective-permute-start(bf16[96,1024]{1,0:T(8,128)(2,1)S(1)} %gate.5.refs_1_), channel_id=1, source_target_pairs={{0,1},{1,0},{2,3},{3,2},{4,5},{5,4},{6,7},{7,6},{8,9},{9,8},{10,11... | collective-permute-start | bytes 589832 | tf_op jit(solution)/shard_map/ppermute | solution.py:561
  34.9 1.3 %collective-permute-done.9.refs_0_ = bf16[96,1024]{1,0:T(8,128)(2,1)S(1)} collective-permute-done((bf16[96,1024]{1,0:T(8,128)(2,1)S(1)}, bf16[96,1024]{1,0:T(8,128)(2,1)S(1)}, u32[]{:S(2)}, u32[]{:S(2)}) %collective-permute-start.9) | collective-permute-done | bytes 196640 | tf_op jit(solution)/shard_map/ppermute | solution.py:556
  36.4 4.0 %collective-permute-done.5.refs_1_ = bf16[96,1024]{1,0:T(8,128)(2,1)S(1)} collective-permute-done((bf16[96,1024]{1,0:T(8,128)(2,1)S(1)}, bf16[96,1024]{1,0:T(8,128)(2,1)S(1)}, u32[]{:S(2)}, u32[]{:S(2)}) %collective-permute-start.5) | collective-permute-done | bytes 196640 | tf_op jit(solution)/shard_map/ppermute | solution.py:556
  40.4 2.6 %collective-permute-start.12 = (bf16[96,1024]{1,0:T(8,128)(2,1)S(1)}, bf16[96,1024]{1,0:T(8,128)(2,1)S(1)}, u32[]{:S(2)}, u32[]{:S(2)}) collective-permute-start(bf16[96,1024]{1,0:T(8,128)(2,1)S(1)} %collective-permute-done.8.refs_0_), channel_id=1, source_target_pairs={{0,1},{1,0},{2,3},{3,2},{4,5},{5,4},{6,7},{7,6},{8,9},{9,8},{10,11... | collective-permute-start | bytes 589832 | tf_op jit(solution)/shard_map/ppermute | solution.py:561
  43.6 0.8 collective-permute-done.16.refs_0_
  44.4 3.1 %collective-permute-start.17 = (bf16[96,1024]{1,0:T(8,128)(2,1)S(1)}, bf16[96,1024]{1,0:T(8,128)(2,1)S(1)}, u32[]{:S(2)}, u32[]{:S(2)}) collective-permute-start(bf16[96,1024]{1,0:T(8,128)(2,1)S(1)} %collective-permute-done.16.refs_0_), channel_id=1, source_target_pairs={{0,1},{1,0},{2,3},{3,2},{4,5},{5,4},{6,7},{7,6},{8,9},{9,8},{10,11... | collective-permute-start | bytes 589832 | tf_op jit(solution)/shard_map/ppermute | solution.py:561
  47.5 1.6 %shard_map.82.refs_5_ = f32[192,1024]{1,0:T(8,128)S(1)} custom-call(s32[3]{0:T(128)S(1)} %pad_add_fusion.meta, bf16[96,1024]{1,0:T(8,128)(2,1)S(1)} %get-tuple-element.32.refs_0_, bf16[96,1024]{1,0:T(8,128)(2,1)S(1)} %gate.5.refs_1_, bf16[96,1024]{1,0:T(8,128)(2,1)S(1)} %collective-permute-done.14.refs_2_, ...), custom_call_target="tpu_custom_call" | custom-call | flops 805306368 | bytes 4194304 | tf_op jit(solution)/shard_map/pallas_call | solution.py:521
  49.1 1.3 %collective-permute-start.7 = (bf16[96,1024]{1,0:T(8,128)(2,1)S(1)}, bf16[96,1024]{1,0:T(8,128)(2,1)S(1)}, u32[]{:S(2)}, u32[]{:S(2)}) collective-permute-start(bf16[96,1024]{1,0:T(8,128)(2,1)S(1)} %collective-permute-done.6.refs_0_), channel_id=1, source_target_pairs={{0,1},{1,0},{2,3},{3,2},{4,5},{5,4},{6,7},{7,6},{8,9},{9,8},{10,11... | collective-permute-start | bytes 589832 | tf_op jit(solution)/shard_map/ppermute | solution.py:561
  50.4 1.6 %shard_map.83.refs_5_ = f32[192,1024]{1,0:T(8,128)S(1)} custom-call(s32[3]{0:T(128)S(1)} %pad_add_fusion.meta, bf16[96,1024]{1,0:T(8,128)(2,1)S(1)} %collective-permute-done.8.refs_0_, bf16[96,1024]{1,0:T(8,128)(2,1)S(1)} %collective-permute-done.4.refs_1_, bf16[96,1024]{1,0:T(8,128)(2,1)S(1)} %collective-permute-done.12.refs_2_, ...), custom_call_target="tpu_custom_call" | custom-call | flops 805306368 | bytes 4194304 | tf_op jit(solution)/shard_map/pallas_call | solution.py:521
  52.0 1.6 %shard_map.84.refs_2_ = f32[192,1024]{1,0:T(8,128)S(1)} custom-call(s32[3]{0:T(128)S(1)} %pad_add_fusion.meta, bf16[96,1024]{1,0:T(8,128)(2,1)S(1)} %collective-permute-done.9.refs_0_, bf16[96,1024]{1,0:T(8,128)(2,1)S(1)} %collective-permute-done.5.refs_1_, bf16[96,1024]{1,0:T(8,128)(2,1)S(1)} %collective-permute-done.10.refs_2_, ...), custom_call_target="tpu_custom_call" | custom-call | flops 805306368 | bytes 4194304 | tf_op jit(solution)/shard_map/pallas_call | solution.py:521
  53.5 1.0 shard_map.86.refs_2_
  54.6 1.3 %shard_map.87 = (bf16[96,1024]{1,0:T(8,128)(2,1)S(1)}, f32[2,8,96]{2,1,0:T(8,128)S(1)}) custom-call(s32[3]{0:T(128)S(1)} %pad_add_fusion.meta, bf16[96,1024]{1,0:T(8,128)(2,1)S(1)} %collective-permute-done.17.refs_0_, bf16[8192,1024]{1,0:T(8,128)(2,1)S(1)} %get-tuple-element.29.rest_6_.refs_4_.refs_1_.rest_7_, f32[96,1024]{1,0:T(8,128)S(1)} %shard_map.86.refs_2_, ...), custom_call_target="tpu_custom_call" | custom-call | flops 201326592 | bytes 2097152 | tf_op jit(solution)/shard_map/pallas_call | solution.py:521
  55.9 1.2 %collective-permute-start.23 = (bf16[96,1024]{1,0:T(8,128)(2,1)S(1)}, bf16[96,1024]{1,0:T(8,128)(2,1)S(1)}, u32[]{:S(2)}, u32[]{:S(2)}) collective-permute-start(bf16[96,1024]{1,0:T(8,128)(2,1)S(1)} %get-tuple-element.36), channel_id=1, source_target_pairs={{0,2},{2,0},{1,3},{3,1},{4,6},{6,4},{5,7},{7,5},{8,10},{10,8},{9,1... | collective-permute-start | bytes 589832 | tf_op jit(solution)/shard_map/ppermute | solution.py:564
  57.2 1.0 shard_map.85.refs_2_
  58.2 1.3 %shard_map.88 = (bf16[96,1024]{1,0:T(8,128)(2,1)S(1)}, f32[2,8,96]{2,1,0:T(8,128)S(1)}) custom-call(s32[3]{0:T(128)S(1)} %pad_add_fusion.meta, bf16[96,1024]{1,0:T(8,128)(2,1)S(1)} %collective-permute-done.7.refs_0_, bf16[8192,1024]{1,0:T(8,128)(2,1)S(1)} %get-tuple-element.29.rest_6_.refs_4_.refs_1_.rest_7_, f32[96,1024]{1,0:T(8,128)S(1)} %shard_map.85.refs_2_, ...), custom_call_target="tpu_custom_call" | custom-call | flops 201326592 | bytes 2097152 | tf_op jit(solution)/shard_map/pallas_call | solution.py:521
  59.8 0.6 collective-permute-start.19
  60.4 0.8 collective-permute-done.19
  61.2 2.8 %collective-permute-done.20 = f32[2,8,96]{2,1,0:T(8,128)S(1)} collective-permute-done((f32[2,8,96]{2,1,0:T(8,128)S(1)}, f32[2,8,96]{2,1,0:T(8,128)S(1)}, u32[]{:S(2)}, u32[]{:S(2)}) %collective-permute-start.20) | collective-permute-done | bytes 6176 | tf_op jit(solution)/shard_map/ppermute | solution.py:567
  64.0 1.2 %collective-permute-start.21 = (f32[2,8,96]{2,1,0:T(8,128)S(1)}, f32[2,8,96]{2,1,0:T(8,128)S(1)}, u32[]{:S(2)}, u32[]{:S(2)}) collective-permute-start(f32[2,8,96]{2,1,0:T(8,128)S(1)} %add.7), channel_id=1, source_target_pairs={{0,2},{2,0},{4,6},{6,4},{8,10},{10,8},{12,14},{14,12},{1,3},{3,1},... | collective-permute-start | bytes 18440 | tf_op jit(solution)/shard_map/ppermute | solution.py:574
  65.7 1.3 %collective-permute-done.21.rest_12_ = f32[2,8,96]{2,1,0:T(8,128)S(1)} collective-permute-done((f32[2,8,96]{2,1,0:T(8,128)S(1)}, f32[2,8,96]{2,1,0:T(8,128)S(1)}, u32[]{:S(2)}, u32[]{:S(2)}) %collective-permute-start.21) | collective-permute-done | bytes 6176 | tf_op jit(solution)/shard_map/ppermute | solution.py:574
  66.9 2.6 %collective-permute-done.22.rest_13_ = f32[2,8,96]{2,1,0:T(8,128)S(1)} collective-permute-done((f32[2,8,96]{2,1,0:T(8,128)S(1)}, f32[2,8,96]{2,1,0:T(8,128)S(1)}, u32[]{:S(2)}, u32[]{:S(2)}) %collective-permute-start.22) | collective-permute-done | bytes 6176 | tf_op jit(solution)/shard_map/ppermute | solution.py:574
  69.6 2.7 %gate.6 = (bf16[96,1024]{1,0:T(8,128)(2,1)S(1)}, f32[96,1024]{1,0:T(8,128)S(1)}) custom-call(s32[3]{0:T(128)S(1)} %pad_add_fusion.meta, f32[2,96,1024]{2,1,0:T(8,128)S(1)} %get-tuple-element.22.base.refs_3_, bf16[96,1024]{1,0:T(8,128)(2,1)S(1)} %collective-permute-done.23.rest_0_.refs_4_, f32[1,2048]{1,0:T(1,128)S(1)} %copy-done, ...), custom_call_target="tpu_custom_call" | custom-call | flops 15728640 | bytes 1179648 | tf_op jit(solution)/shard_map/gate/pallas_call | solution.py:409
  72.4 3.2 %gate.7.refs_1_ = bf16[96,1024]{1,0:T(8,128)(2,1)S(1)} custom-call(s32[3]{0:T(128)S(1)} %pad_add_fusion.meta, f32[2,96,1024]{2,1,0:T(8,128)S(1)} %get-tuple-element.22.base.refs_3_, bf16[96,1024]{1,0:T(8,128)(2,1)S(1)} %collective-permute-done.18.rest_0_.refs_4_, f32[1,2048]{1,0:T(1,128)S(1)} %copy-done, f32[16,1024]{1,0:T(8,128)S(1)} %get-tuple-element.24.rest_1_.rest_2_, ...), custom_call_target="tpu_custom_call" | custom-call | flops 15728640 | bytes 1179648 | tf_op jit(solution)/shard_map/gate/pallas_call | solution.py:409
  75.6 1.2 %collective-permute-start.24 = (bf16[96,1024]{1,0:T(8,128)(2,1)S(1)}, bf16[96,1024]{1,0:T(8,128)(2,1)S(1)}, u32[]{:S(2)}, u32[]{:S(2)}) collective-permute-start(bf16[96,1024]{1,0:T(8,128)(2,1)S(1)} %gate.7.refs_1_), channel_id=1, source_target_pairs={{0,4},{4,12},{12,8},{8,0},{1,5},{5,13},{13,9},{9,1},{2,6},{6,14},{... | collective-permute-start | bytes 589832 | tf_op jit(solution)/shard_map/ppermute | solution.py:556
  76.8 1.0 collective-permute-done.28.refs_0_
  77.8 5.7 %collective-permute-done.24.refs_1_ = bf16[96,1024]{1,0:T(8,128)(2,1)S(1)} collective-permute-done((bf16[96,1024]{1,0:T(8,128)(2,1)S(1)}, bf16[96,1024]{1,0:T(8,128)(2,1)S(1)}, u32[]{:S(2)}, u32[]{:S(2)}) %collective-permute-start.24) | collective-permute-done | bytes 196640 | tf_op jit(solution)/shard_map/ppermute | solution.py:556
  83.4 4.2 %collective-permute-start.35 = (bf16[96,1024]{1,0:T(8,128)(2,1)S(1)}, bf16[96,1024]{1,0:T(8,128)(2,1)S(1)}, u32[]{:S(2)}, u32[]{:S(2)}) collective-permute-start(bf16[96,1024]{1,0:T(8,128)(2,1)S(1)} %gate.7.refs_1_), channel_id=1, source_target_pairs={{0,1},{1,0},{2,3},{3,2},{4,5},{5,4},{6,7},{7,6},{8,9},{9,8},{10,11... | collective-permute-start | bytes 589832 | tf_op jit(solution)/shard_map/ppermute | solution.py:561
  88.2 1.7 %collective-permute-start.36 = (bf16[96,1024]{1,0:T(8,128)(2,1)S(1)}, bf16[96,1024]{1,0:T(8,128)(2,1)S(1)}, u32[]{:S(2)}, u32[]{:S(2)}) collective-permute-start(bf16[96,1024]{1,0:T(8,128)(2,1)S(1)} %collective-permute-done.29.refs_0_), channel_id=1, source_target_pairs={{0,4},{4,12},{12,8},{8,0},{1,5},{5,13},{13,9},{9,1},{2,6},{6,14},{... | collective-permute-start | bytes 589832 | tf_op jit(solution)/shard_map/ppermute | solution.py:556
  89.9 1.7 %collective-permute-done.25.refs_1_ = bf16[96,1024]{1,0:T(8,128)(2,1)S(1)} collective-permute-done((bf16[96,1024]{1,0:T(8,128)(2,1)S(1)}, bf16[96,1024]{1,0:T(8,128)(2,1)S(1)}, u32[]{:S(2)}, u32[]{:S(2)}) %collective-permute-start.25) | collective-permute-done | bytes 196640 | tf_op jit(solution)/shard_map/ppermute | solution.py:556
  91.6 4.4 %collective-permute-start.32 = (bf16[96,1024]{1,0:T(8,128)(2,1)S(1)}, bf16[96,1024]{1,0:T(8,128)(2,1)S(1)}, u32[]{:S(2)}, u32[]{:S(2)}) collective-permute-start(bf16[96,1024]{1,0:T(8,128)(2,1)S(1)} %collective-permute-done.28.refs_0_), channel_id=1, source_target_pairs={{0,1},{1,0},{2,3},{3,2},{4,5},{5,4},{6,7},{7,6},{8,9},{9,8},{10,11... | collective-permute-start | bytes 589832 | tf_op jit(solution)/shard_map/ppermute | solution.py:561
  96.5 4.0 %collective-permute-start.37 = (bf16[96,1024]{1,0:T(8,128)(2,1)S(1)}, bf16[96,1024]{1,0:T(8,128)(2,1)S(1)}, u32[]{:S(2)}, u32[]{:S(2)}) collective-permute-start(bf16[96,1024]{1,0:T(8,128)(2,1)S(1)} %collective-permute-done.36.refs_0_), channel_id=1, source_target_pairs={{0,1},{1,0},{2,3},{3,2},{4,5},{5,4},{6,7},{7,6},{8,9},{9,8},{10,11... | collective-permute-start | bytes 589832 | tf_op jit(solution)/shard_map/ppermute | solution.py:561
  100.5 1.6 %shard_map.89.refs_5_ = f32[192,1024]{1,0:T(8,128)S(1)} custom-call(s32[3]{0:T(128)S(1)} %pad_add_fusion.meta, bf16[96,1024]{1,0:T(8,128)(2,1)S(1)} %get-tuple-element.38.refs_0_, bf16[96,1024]{1,0:T(8,128)(2,1)S(1)} %gate.7.refs_1_, bf16[96,1024]{1,0:T(8,128)(2,1)S(1)} %collective-permute-done.34.refs_2_, ...), custom_call_target="tpu_custom_call" | custom-call | flops 805306368 | bytes 4194304 | tf_op jit(solution)/shard_map/pallas_call | solution.py:521
  102.7 1.6 %shard_map.90.refs_5_ = f32[192,1024]{1,0:T(8,128)S(1)} custom-call(s32[3]{0:T(128)S(1)} %pad_add_fusion.meta, bf16[96,1024]{1,0:T(8,128)(2,1)S(1)} %collective-permute-done.28.refs_0_, bf16[96,1024]{1,0:T(8,128)(2,1)S(1)} %collective-permute-done.24.refs_1_, bf16[96,1024]{1,0:T(8,128)(2,1)S(1)} %collective-permute-done.32.refs_2_, ...), custom_call_target="tpu_custom_call" | custom-call | flops 805306368 | bytes 4194304 | tf_op jit(solution)/shard_map/pallas_call | solution.py:521
  104.2 1.6 %shard_map.91.refs_2_ = f32[192,1024]{1,0:T(8,128)S(1)} custom-call(s32[3]{0:T(128)S(1)} %pad_add_fusion.meta, bf16[96,1024]{1,0:T(8,128)(2,1)S(1)} %collective-permute-done.29.refs_0_, bf16[96,1024]{1,0:T(8,128)(2,1)S(1)} %collective-permute-done.25.refs_1_, bf16[96,1024]{1,0:T(8,128)(2,1)S(1)} %collective-permute-done.30.refs_2_, ...), custom_call_target="tpu_custom_call" | custom-call | flops 805306368 | bytes 4194304 | tf_op jit(solution)/shard_map/pallas_call | solution.py:521
  105.8 1.0 shard_map.93.refs_2_
  106.9 1.0 shard_map.92.refs_2_
  107.9 1.1 shard_map.94.refs_5_
  109.0 1.8 %shard_map.95 = f32[1,2,96,1024]{3,2,1,0:T(8,128)} custom-call(s32[3]{0:T(128)S(1)} %pad_add_fusion.meta, bf16[96,1024]{1,0:T(8,128)(2,1)S(1)} %collective-permute-done.27.refs_0_, bf16[8192,1024]{1,0:T(8,128)(2,1)S(1)} %get-tuple-element.29.rest_6_.refs_4_.refs_1_.rest_7_, f32[96,1024]{1,0:T(8,128)S(1)} %shard_map.92.refs_2_, ...), custom_call_target="tpu_custom_call" | custom-call | flops 201326592 | bytes 2097152 | tf_op jit(solution)/shard_map/pallas_call | solution.py:521
  (53 shorter events, 4.0 us)
Async XLA Ops:
  7.4 10.9 %collective-permute-start = (f32[2,16,1024]{2,1,0:T(8,128)S(1)}, f32[2,16,1024]{2,1,0:T(8,128)S(1)}, u32[]{:S(2)}, u32[]{:S(2)}) collective-permute-start(f32[2,16,1024]{2,1,0:T(8,128)S(1)} %get-tuple-element.28), channel_id=1, source_target_pairs={{0,1},{1,0},{2,3},{3,2},{4,5},{5,4},{6,7},{7,6},{8,9},{9,8},{10,11... | collective-permute-start | bytes 393224 | tf_op jit(solution)/shard_map/ppermute | solution.py:561
  7.5 10.8 %collective-permute-start.1 = (f32[2,8,96]{2,1,0:T(8,128)S(1)}, f32[2,8,96]{2,1,0:T(8,128)S(1)}, u32[]{:S(2)}, u32[]{:S(2)}) collective-permute-start(f32[2,8,96]{2,1,0:T(8,128)S(1)} %get-tuple-element.30.rest_7_.rest_8_), channel_id=1, source_target_pairs={{0,4},{4,12},{12,8},{8,0},{1,5},{5,13},{13,9},{9,1},{2,6},{6,14},{... | collective-permute-start | bytes 18440 | tf_op jit(solution)/shard_map/ppermute | solution.py:556
  10.2 8.1 %collective-permute-start.2 = (f32[2,8,96]{2,1,0:T(8,128)S(1)}, f32[2,8,96]{2,1,0:T(8,128)S(1)}, u32[]{:S(2)}, u32[]{:S(2)}) collective-permute-start(f32[2,8,96]{2,1,0:T(8,128)S(1)} %get-tuple-element.30.rest_7_.rest_8_), channel_id=1, source_target_pairs={{0,12},{4,8},{12,0},{8,4},{1,13},{5,9},{13,1},{9,5},{2,14},{6,10},... | collective-permute-start | bytes 18440 | tf_op jit(solution)/shard_map/ppermute | solution.py:556
  12.4 5.9 %collective-permute-start.3 = (f32[2,8,96]{2,1,0:T(8,128)S(1)}, f32[2,8,96]{2,1,0:T(8,128)S(1)}, u32[]{:S(2)}, u32[]{:S(2)}) collective-permute-start(f32[2,8,96]{2,1,0:T(8,128)S(1)} %get-tuple-element.30.rest_7_.rest_8_), channel_id=1, source_target_pairs={{0,8},{4,0},{12,4},{8,12},{1,9},{5,1},{13,5},{9,13},{2,10},{6,2},{... | collective-permute-start | bytes 18440 | tf_op jit(solution)/shard_map/ppermute | solution.py:556
  13.7 4.7 %copy-start = (f32[1,2048]{1,0:T(1,128)S(1)}, f32[1,2048]{1,0:T(1,128)}, u32[]{:S(2)}) copy-start(f32[1,2048]{1,0:T(1,128)} %rest_1_.3) | copy-start | bytes 24580
  21.0 6.5 %collective-permute-start.8 = (bf16[96,1024]{1,0:T(8,128)(2,1)S(1)}, bf16[96,1024]{1,0:T(8,128)(2,1)S(1)}, u32[]{:S(2)}, u32[]{:S(2)}) collective-permute-start(bf16[96,1024]{1,0:T(8,128)(2,1)S(1)} %get-tuple-element.32.refs_0_), channel_id=1, source_target_pairs={{0,4},{4,12},{12,8},{8,0},{1,5},{5,13},{13,9},{9,1},{2,6},{6,14},{... | collective-permute-start | bytes 589832 | tf_op jit(solution)/shard_map/ppermute | solution.py:556
  24.4 7.9 %collective-permute-start.4 = (bf16[96,1024]{1,0:T(8,128)(2,1)S(1)}, bf16[96,1024]{1,0:T(8,128)(2,1)S(1)}, u32[]{:S(2)}, u32[]{:S(2)}) collective-permute-start(bf16[96,1024]{1,0:T(8,128)(2,1)S(1)} %gate.5.refs_1_), channel_id=1, source_target_pairs={{0,4},{4,12},{12,8},{8,0},{1,5},{5,13},{13,9},{9,1},{2,6},{6,14},{... | collective-permute-start | bytes 589832 | tf_op jit(solution)/shard_map/ppermute | solution.py:556
  27.5 8.7 %collective-permute-start.9 = (bf16[96,1024]{1,0:T(8,128)(2,1)S(1)}, bf16[96,1024]{1,0:T(8,128)(2,1)S(1)}, u32[]{:S(2)}, u32[]{:S(2)}) collective-permute-start(bf16[96,1024]{1,0:T(8,128)(2,1)S(1)} %collective-permute-done.8.refs_0_), channel_id=1, source_target_pairs={{0,4},{4,12},{12,8},{8,0},{1,5},{5,13},{13,9},{9,1},{2,6},{6,14},{... | collective-permute-start | bytes 589832 | tf_op jit(solution)/shard_map/ppermute | solution.py:556
  32.2 8.2 %collective-permute-start.5 = (bf16[96,1024]{1,0:T(8,128)(2,1)S(1)}, bf16[96,1024]{1,0:T(8,128)(2,1)S(1)}, u32[]{:S(2)}, u32[]{:S(2)}) collective-permute-start(bf16[96,1024]{1,0:T(8,128)(2,1)S(1)} %collective-permute-done.4.refs_1_), channel_id=1, source_target_pairs={{0,4},{4,12},{12,8},{8,0},{1,5},{5,13},{13,9},{9,1},{2,6},{6,14},{... | collective-permute-start | bytes 589832 | tf_op jit(solution)/shard_map/ppermute | solution.py:556
  32.3 8.2 %collective-permute-start.15 = (bf16[96,1024]{1,0:T(8,128)(2,1)S(1)}, bf16[96,1024]{1,0:T(8,128)(2,1)S(1)}, u32[]{:S(2)}, u32[]{:S(2)}) collective-permute-start(bf16[96,1024]{1,0:T(8,128)(2,1)S(1)} %gate.5.refs_1_), channel_id=1, source_target_pairs={{0,1},{1,0},{2,3},{3,2},{4,5},{5,4},{6,7},{7,6},{8,9},{9,8},{10,11... | collective-permute-start | bytes 589832 | tf_op jit(solution)/shard_map/ppermute | solution.py:561
  34.4 8.6 %collective-permute-start.14 = (bf16[96,1024]{1,0:T(8,128)(2,1)S(1)}, bf16[96,1024]{1,0:T(8,128)(2,1)S(1)}, u32[]{:S(2)}, u32[]{:S(2)}) collective-permute-start(bf16[96,1024]{1,0:T(8,128)(2,1)S(1)} %get-tuple-element.32.refs_0_), channel_id=1, source_target_pairs={{0,1},{1,0},{2,3},{3,2},{4,5},{5,4},{6,7},{7,6},{8,9},{9,8},{10,11... | collective-permute-start | bytes 589832 | tf_op jit(solution)/shard_map/ppermute | solution.py:561
  34.4 8.7 %collective-permute-start.13 = (bf16[96,1024]{1,0:T(8,128)(2,1)S(1)}, bf16[96,1024]{1,0:T(8,128)(2,1)S(1)}, u32[]{:S(2)}, u32[]{:S(2)}) collective-permute-start(bf16[96,1024]{1,0:T(8,128)(2,1)S(1)} %collective-permute-done.4.refs_1_), channel_id=1, source_target_pairs={{0,1},{1,0},{2,3},{3,2},{4,5},{5,4},{6,7},{7,6},{8,9},{9,8},{10,11... | collective-permute-start | bytes 589832 | tf_op jit(solution)/shard_map/ppermute | solution.py:561
  36.2 8.2 %collective-permute-start.16 = (bf16[96,1024]{1,0:T(8,128)(2,1)S(1)}, bf16[96,1024]{1,0:T(8,128)(2,1)S(1)}, u32[]{:S(2)}, u32[]{:S(2)}) collective-permute-start(bf16[96,1024]{1,0:T(8,128)(2,1)S(1)} %collective-permute-done.9.refs_0_), channel_id=1, source_target_pairs={{0,4},{4,12},{12,8},{8,0},{1,5},{5,13},{13,9},{9,1},{2,6},{6,14},{... | collective-permute-start | bytes 589832 | tf_op jit(solution)/shard_map/ppermute | solution.py:556
  40.4 8.6 %collective-permute-start.6 = (bf16[96,1024]{1,0:T(8,128)(2,1)S(1)}, bf16[96,1024]{1,0:T(8,128)(2,1)S(1)}, u32[]{:S(2)}, u32[]{:S(2)}) collective-permute-start(bf16[96,1024]{1,0:T(8,128)(2,1)S(1)} %collective-permute-done.5.refs_1_), channel_id=1, source_target_pairs={{0,4},{4,12},{12,8},{8,0},{1,5},{5,13},{13,9},{9,1},{2,6},{6,14},{... | collective-permute-start | bytes 589832 | tf_op jit(solution)/shard_map/ppermute | solution.py:556
  40.4 9.9 %collective-permute-start.12 = (bf16[96,1024]{1,0:T(8,128)(2,1)S(1)}, bf16[96,1024]{1,0:T(8,128)(2,1)S(1)}, u32[]{:S(2)}, u32[]{:S(2)}) collective-permute-start(bf16[96,1024]{1,0:T(8,128)(2,1)S(1)} %collective-permute-done.8.refs_0_), channel_id=1, source_target_pairs={{0,1},{1,0},{2,3},{3,2},{4,5},{5,4},{6,7},{7,6},{8,9},{9,8},{10,11... | collective-permute-start | bytes 589832 | tf_op jit(solution)/shard_map/ppermute | solution.py:561
  43.0 8.9 %collective-permute-start.11 = (bf16[96,1024]{1,0:T(8,128)(2,1)S(1)}, bf16[96,1024]{1,0:T(8,128)(2,1)S(1)}, u32[]{:S(2)}, u32[]{:S(2)}) collective-permute-start(bf16[96,1024]{1,0:T(8,128)(2,1)S(1)} %collective-permute-done.5.refs_1_), channel_id=1, source_target_pairs={{0,1},{1,0},{2,3},{3,2},{4,5},{5,4},{6,7},{7,6},{8,9},{9,8},{10,11... | collective-permute-start | bytes 589832 | tf_op jit(solution)/shard_map/ppermute | solution.py:561
  43.1 8.8 %collective-permute-start.10 = (bf16[96,1024]{1,0:T(8,128)(2,1)S(1)}, bf16[96,1024]{1,0:T(8,128)(2,1)S(1)}, u32[]{:S(2)}, u32[]{:S(2)}) collective-permute-start(bf16[96,1024]{1,0:T(8,128)(2,1)S(1)} %collective-permute-done.9.refs_0_), channel_id=1, source_target_pairs={{0,1},{1,0},{2,3},{3,2},{4,5},{5,4},{6,7},{7,6},{8,9},{9,8},{10,11... | collective-permute-start | bytes 589832 | tf_op jit(solution)/shard_map/ppermute | solution.py:561
  44.4 10.2 %collective-permute-start.17 = (bf16[96,1024]{1,0:T(8,128)(2,1)S(1)}, bf16[96,1024]{1,0:T(8,128)(2,1)S(1)}, u32[]{:S(2)}, u32[]{:S(2)}) collective-permute-start(bf16[96,1024]{1,0:T(8,128)(2,1)S(1)} %collective-permute-done.16.refs_0_), channel_id=1, source_target_pairs={{0,1},{1,0},{2,3},{3,2},{4,5},{5,4},{6,7},{7,6},{8,9},{9,8},{10,11... | collective-permute-start | bytes 589832 | tf_op jit(solution)/shard_map/ppermute | solution.py:561
  49.1 9.1 %collective-permute-start.7 = (bf16[96,1024]{1,0:T(8,128)(2,1)S(1)}, bf16[96,1024]{1,0:T(8,128)(2,1)S(1)}, u32[]{:S(2)}, u32[]{:S(2)}) collective-permute-start(bf16[96,1024]{1,0:T(8,128)(2,1)S(1)} %collective-permute-done.6.refs_0_), channel_id=1, source_target_pairs={{0,1},{1,0},{2,3},{3,2},{4,5},{5,4},{6,7},{7,6},{8,9},{9,8},{10,11... | collective-permute-start | bytes 589832 | tf_op jit(solution)/shard_map/ppermute | solution.py:561
  55.9 13.6 %collective-permute-start.23 = (bf16[96,1024]{1,0:T(8,128)(2,1)S(1)}, bf16[96,1024]{1,0:T(8,128)(2,1)S(1)}, u32[]{:S(2)}, u32[]{:S(2)}) collective-permute-start(bf16[96,1024]{1,0:T(8,128)(2,1)S(1)} %get-tuple-element.36), channel_id=1, source_target_pairs={{0,2},{2,0},{1,3},{3,1},{4,6},{6,4},{5,7},{7,5},{8,10},{10,8},{9,1... | collective-permute-start | bytes 589832 | tf_op jit(solution)/shard_map/ppermute | solution.py:564
  59.6 12.8 %collective-permute-start.18 = (bf16[96,1024]{1,0:T(8,128)(2,1)S(1)}, bf16[96,1024]{1,0:T(8,128)(2,1)S(1)}, u32[]{:S(2)}, u32[]{:S(2)}) collective-permute-start(bf16[96,1024]{1,0:T(8,128)(2,1)S(1)} %get-tuple-element.34), channel_id=1, source_target_pairs={{0,2},{2,0},{1,3},{3,1},{4,6},{6,4},{5,7},{7,5},{8,10},{10,8},{9,1... | collective-permute-start | bytes 589832 | tf_op jit(solution)/shard_map/ppermute | solution.py:564
  59.8 1.4 %collective-permute-start.19 = (f32[2,8,96]{2,1,0:T(8,128)S(1)}, f32[2,8,96]{2,1,0:T(8,128)S(1)}, u32[]{:S(2)}, u32[]{:S(2)}) collective-permute-start(f32[2,8,96]{2,1,0:T(8,128)S(1)} %get-tuple-element.35), channel_id=1, source_target_pairs={{0,1},{1,0},{2,3},{3,2},{4,5},{5,4},{6,7},{7,6},{8,9},{9,8},{10,11... | collective-permute-start | bytes 18440 | tf_op jit(solution)/shard_map/ppermute | solution.py:561
  61.2 2.8 %collective-permute-start.20 = (f32[2,8,96]{2,1,0:T(8,128)S(1)}, f32[2,8,96]{2,1,0:T(8,128)S(1)}, u32[]{:S(2)}, u32[]{:S(2)}) collective-permute-start(f32[2,8,96]{2,1,0:T(8,128)S(1)} %add.6), channel_id=1, source_target_pairs={{0,4},{4,0},{8,12},{12,8},{1,5},{5,1},{9,13},{13,9},{2,6},{6,2},{1... | collective-permute-start | bytes 18440 | tf_op jit(solution)/shard_map/ppermute | solution.py:567
  64.0 2.9 %collective-permute-start.21 = (f32[2,8,96]{2,1,0:T(8,128)S(1)}, f32[2,8,96]{2,1,0:T(8,128)S(1)}, u32[]{:S(2)}, u32[]{:S(2)}) collective-permute-start(f32[2,8,96]{2,1,0:T(8,128)S(1)} %add.7), channel_id=1, source_target_pairs={{0,2},{2,0},{4,6},{6,4},{8,10},{10,8},{12,14},{14,12},{1,3},{3,1},... | collective-permute-start | bytes 18440 | tf_op jit(solution)/shard_map/ppermute | solution.py:574
  65.3 4.3 %collective-permute-start.22 = (f32[2,8,96]{2,1,0:T(8,128)S(1)}, f32[2,8,96]{2,1,0:T(8,128)S(1)}, u32[]{:S(2)}, u32[]{:S(2)}) collective-permute-start(f32[2,8,96]{2,1,0:T(8,128)S(1)} %add.7), channel_id=1, source_target_pairs={{0,10},{2,8},{4,14},{6,12},{8,2},{10,0},{12,6},{14,4},{1,11},{3,9}... | collective-permute-start | bytes 18440 | tf_op jit(solution)/shard_map/ppermute | solution.py:574
  72.3 5.5 %collective-permute-start.28 = (bf16[96,1024]{1,0:T(8,128)(2,1)S(1)}, bf16[96,1024]{1,0:T(8,128)(2,1)S(1)}, u32[]{:S(2)}, u32[]{:S(2)}) collective-permute-start(bf16[96,1024]{1,0:T(8,128)(2,1)S(1)} %get-tuple-element.38.refs_0_), channel_id=1, source_target_pairs={{0,4},{4,12},{12,8},{8,0},{1,5},{5,13},{13,9},{9,1},{2,6},{6,14},{... | collective-permute-start | bytes 589832 | tf_op jit(solution)/shard_map/ppermute | solution.py:556
  75.6 7.9 %collective-permute-start.24 = (bf16[96,1024]{1,0:T(8,128)(2,1)S(1)}, bf16[96,1024]{1,0:T(8,128)(2,1)S(1)}, u32[]{:S(2)}, u32[]{:S(2)}) collective-permute-start(bf16[96,1024]{1,0:T(8,128)(2,1)S(1)} %gate.7.refs_1_), channel_id=1, source_target_pairs={{0,4},{4,12},{12,8},{8,0},{1,5},{5,13},{13,9},{9,1},{2,6},{6,14},{... | collective-permute-start | bytes 589832 | tf_op jit(solution)/shard_map/ppermute | solution.py:556
  77.8 10.4 %collective-permute-start.29 = (bf16[96,1024]{1,0:T(8,128)(2,1)S(1)}, bf16[96,1024]{1,0:T(8,128)(2,1)S(1)}, u32[]{:S(2)}, u32[]{:S(2)}) collective-permute-start(bf16[96,1024]{1,0:T(8,128)(2,1)S(1)} %collective-permute-done.28.refs_0_), channel_id=1, source_target_pairs={{0,4},{4,12},{12,8},{8,0},{1,5},{5,13},{13,9},{9,1},{2,6},{6,14},{... | collective-permute-start | bytes 589832 | tf_op jit(solution)/shard_map/ppermute | solution.py:556
  83.4 8.2 %collective-permute-start.25 = (bf16[96,1024]{1,0:T(8,128)(2,1)S(1)}, bf16[96,1024]{1,0:T(8,128)(2,1)S(1)}, u32[]{:S(2)}, u32[]{:S(2)}) collective-permute-start(bf16[96,1024]{1,0:T(8,128)(2,1)S(1)} %collective-permute-done.24.refs_1_), channel_id=1, source_target_pairs={{0,4},{4,12},{12,8},{8,0},{1,5},{5,13},{13,9},{9,1},{2,6},{6,14},{... | collective-permute-start | bytes 589832 | tf_op jit(solution)/shard_map/ppermute | solution.py:556
  83.4 8.2 %collective-permute-start.35 = (bf16[96,1024]{1,0:T(8,128)(2,1)S(1)}, bf16[96,1024]{1,0:T(8,128)(2,1)S(1)}, u32[]{:S(2)}, u32[]{:S(2)}) collective-permute-start(bf16[96,1024]{1,0:T(8,128)(2,1)S(1)} %gate.7.refs_1_), channel_id=1, source_target_pairs={{0,1},{1,0},{2,3},{3,2},{4,5},{5,4},{6,7},{7,6},{8,9},{9,8},{10,11... | collective-permute-start | bytes 589832 | tf_op jit(solution)/shard_map/ppermute | solution.py:561
  87.7 8.3 %collective-permute-start.34 = (bf16[96,1024]{1,0:T(8,128)(2,1)S(1)}, bf16[96,1024]{1,0:T(8,128)(2,1)S(1)}, u32[]{:S(2)}, u32[]{:S(2)}) collective-permute-start(bf16[96,1024]{1,0:T(8,128)(2,1)S(1)} %get-tuple-element.38.refs_0_), channel_id=1, source_target_pairs={{0,1},{1,0},{2,3},{3,2},{4,5},{5,4},{6,7},{7,6},{8,9},{9,8},{10,11... | collective-permute-start | bytes 589832 | tf_op jit(solution)/shard_map/ppermute | solution.py:561
  87.7 8.4 %collective-permute-start.33 = (bf16[96,1024]{1,0:T(8,128)(2,1)S(1)}, bf16[96,1024]{1,0:T(8,128)(2,1)S(1)}, u32[]{:S(2)}, u32[]{:S(2)}) collective-permute-start(bf16[96,1024]{1,0:T(8,128)(2,1)S(1)} %collective-permute-done.24.refs_1_), channel_id=1, source_target_pairs={{0,1},{1,0},{2,3},{3,2},{4,5},{5,4},{6,7},{7,6},{8,9},{9,8},{10,11... | collective-permute-start | bytes 589832 | tf_op jit(solution)/shard_map/ppermute | solution.py:561
  88.2 8.3 %collective-permute-start.36 = (bf16[96,1024]{1,0:T(8,128)(2,1)S(1)}, bf16[96,1024]{1,0:T(8,128)(2,1)S(1)}, u32[]{:S(2)}, u32[]{:S(2)}) collective-permute-start(bf16[96,1024]{1,0:T(8,128)(2,1)S(1)} %collective-permute-done.29.refs_0_), channel_id=1, source_target_pairs={{0,4},{4,12},{12,8},{8,0},{1,5},{5,13},{13,9},{9,1},{2,6},{6,14},{... | collective-permute-start | bytes 589832 | tf_op jit(solution)/shard_map/ppermute | solution.py:556
  91.6 10.5 %collective-permute-start.26 = (bf16[96,1024]{1,0:T(8,128)(2,1)S(1)}, bf16[96,1024]{1,0:T(8,128)(2,1)S(1)}, u32[]{:S(2)}, u32[]{:S(2)}) collective-permute-start(bf16[96,1024]{1,0:T(8,128)(2,1)S(1)} %collective-permute-done.25.refs_1_), channel_id=1, source_target_pairs={{0,4},{4,12},{12,8},{8,0},{1,5},{5,13},{13,9},{9,1},{2,6},{6,14},{... | collective-permute-start | bytes 589832 | tf_op jit(solution)/shard_map/ppermute | solution.py:556
  91.6 11.0 %collective-permute-start.32 = (bf16[96,1024]{1,0:T(8,128)(2,1)S(1)}, bf16[96,1024]{1,0:T(8,128)(2,1)S(1)}, u32[]{:S(2)}, u32[]{:S(2)}) collective-permute-start(bf16[96,1024]{1,0:T(8,128)(2,1)S(1)} %collective-permute-done.28.refs_0_), channel_id=1, source_target_pairs={{0,1},{1,0},{2,3},{3,2},{4,5},{5,4},{6,7},{7,6},{8,9},{9,8},{10,11... | collective-permute-start | bytes 589832 | tf_op jit(solution)/shard_map/ppermute | solution.py:561
  96.0 8.2 %collective-permute-start.31 = (bf16[96,1024]{1,0:T(8,128)(2,1)S(1)}, bf16[96,1024]{1,0:T(8,128)(2,1)S(1)}, u32[]{:S(2)}, u32[]{:S(2)}) collective-permute-start(bf16[96,1024]{1,0:T(8,128)(2,1)S(1)} %collective-permute-done.25.refs_1_), channel_id=1, source_target_pairs={{0,1},{1,0},{2,3},{3,2},{4,5},{5,4},{6,7},{7,6},{8,9},{9,8},{10,11... | collective-permute-start | bytes 589832 | tf_op jit(solution)/shard_map/ppermute | solution.py:561
  96.1 8.1 %collective-permute-start.30 = (bf16[96,1024]{1,0:T(8,128)(2,1)S(1)}, bf16[96,1024]{1,0:T(8,128)(2,1)S(1)}, u32[]{:S(2)}, u32[]{:S(2)}) collective-permute-start(bf16[96,1024]{1,0:T(8,128)(2,1)S(1)} %collective-permute-done.29.refs_0_), channel_id=1, source_target_pairs={{0,1},{1,0},{2,3},{3,2},{4,5},{5,4},{6,7},{7,6},{8,9},{9,8},{10,11... | collective-permute-start | bytes 589832 | tf_op jit(solution)/shard_map/ppermute | solution.py:561
  96.5 11.4 %collective-permute-start.37 = (bf16[96,1024]{1,0:T(8,128)(2,1)S(1)}, bf16[96,1024]{1,0:T(8,128)(2,1)S(1)}, u32[]{:S(2)}, u32[]{:S(2)}) collective-permute-start(bf16[96,1024]{1,0:T(8,128)(2,1)S(1)} %collective-permute-done.36.refs_0_), channel_id=1, source_target_pairs={{0,1},{1,0},{2,3},{3,2},{4,5},{5,4},{6,7},{7,6},{8,9},{9,8},{10,11... | collective-permute-start | bytes 589832 | tf_op jit(solution)/shard_map/ppermute | solution.py:561
  102.1 6.9 %collective-permute-start.27 = (bf16[96,1024]{1,0:T(8,128)(2,1)S(1)}, bf16[96,1024]{1,0:T(8,128)(2,1)S(1)}, u32[]{:S(2)}, u32[]{:S(2)}) collective-permute-start(bf16[96,1024]{1,0:T(8,128)(2,1)S(1)} %collective-permute-done.26.refs_0_), channel_id=1, source_target_pairs={{0,1},{1,0},{2,3},{3,2},{4,5},{5,4},{6,7},{7,6},{8,9},{9,8},{10,11... | collective-permute-start | bytes 589832 | tf_op jit(solution)/shard_map/ppermute | solution.py:561

commit v3 on v2

--- a/solution.py
+++ b/solution.py
@@ -300,7 +300,7 @@
 
 
 def gate_body(channels, span, counts, meta, base, *rest):
-    n_delta, n_first, n_later, n_before, n_out = counts
+    n_delta, n_first, n_later, n_before, n_past, n_out, n_keep = counts
     rest = list(rest)
 
     def take(n):
@@ -310,8 +310,9 @@
     gain, rates_ref, resid_ref, taps, mine, theirs = take(6)
     take(1)
     first_sums, later_sums, before = take(n_first), take(n_later), take(n_before)
+    past = take(n_past)
     gated = rest.pop(0)
-    normed_out = take(n_out)
+    normed_out, past_out = take(n_out), take(n_keep)
     padded, state_buf = rest
     rows, half = gated.shape
     modes = rates_ref.shape[0]
@@ -335,7 +336,7 @@
             return carry
 
         lax.fori_loop(0, half // wide, chain, 0)
-    else:
+    elif not n_past:
         state_buf[...] = mine[span] + theirs[span]
 
     sums = first_sums[0][span, 0:1, :]
@@ -365,46 +366,54 @@
         if n_out:
             normed_out[0][:, at] = normed
         rates = rates_ref[:, at]
-        weighted = resid_ref[:, at] * state_buf[:, at]
-        step8 = jnp.exp(-rates * float(SUB))
-        place = lax.broadcasted_iota(jnp.int32, (SUB, LANES), 0).astype(f32)
-        first = [spread(weighted, m) * jnp.exp(-spread(rates, m) * place) for m in range(modes)]
         total = [None] * blocks
 
         def store(k, value):
             total[k] = value
 
-        mode_rows(first, [spread(step8, m) for m in range(modes)], rows, store)
+        if n_past:
+            for k in range(blocks):
+                total[k] = past[0][k * SUB : (k + 1) * SUB, at]
+        else:
+            weighted = resid_ref[:, at] * state_buf[:, at]
+            step8 = jnp.exp(-rates * float(SUB))
+            place = lax.broadcasted_iota(jnp.int32, (SUB, LANES), 0).astype(f32)
+            first = [spread(weighted, m) * jnp.exp(-spread(rates, m) * place) for m in range(modes)]
+            mode_rows(first, [spread(step8, m) for m in range(modes)], rows, store)
+            if n_keep:
+                for k in range(blocks):
+                    past_out[0][k * SUB : (k + 1) * SUB, at] = total[k]
         for b in range(SUB):
             shifted = [
                 padded[SUB + k * SUB - b : 2 * SUB + k * SUB - b, :] for k in range(blocks)
             ]
             for a in range(blocks):
-                j = a * SUB + b
-                tap = row_spread(taps, j, at)
+                tap = row_spread(taps, a * SUB + b, at)
                 for k in range(a, blocks):
                     total[k] = total[k] + tap * shifted[k - a]
         for k in range(blocks):
-            rows_at = pl.ds(SUB + k * SUB, SUB)
-            gated[k * SUB : (k + 1) * SUB, at] = (padded[rows_at, :] * total[k]).astype(gated.dtype)
+            block = padded[pl.ds(SUB + k * SUB, SUB), :]
+            gated[k * SUB : (k + 1) * SUB, at] = (block * total[k]).astype(gated.dtype)
         return carry
 
     lax.fori_loop(0, half // LANES, tile, 0)
 
 
-def gate(meta, base, delta, gain, modes_here, taps, weight, first_sums, later_sums, states, before, span):
+def gate(meta, base, delta, gain, modes_here, taps, weight, first_sums, later_sums, states, before, past, keep, span):
     spans, rows, half = base.shape
     modes = modes_here[0].shape[0]
     vmem = pl.BlockSpec(memory_space=pltpu.VMEM)
     deltas = [] if delta is None else [delta]
     want = int(span + 1 < spans)
     head = [base, *deltas, gain, *modes_here, taps, *states]
-    operands = [*head, in_vmem(weight), *first_sums, *later_sums, *before]
+    operands = [*head, in_vmem(weight), *first_sums, *later_sums, *before, *past]
     in_specs = [vmem] * len(operands)
     in_specs[len(head)] = pl.BlockSpec(memory_space=pl.ANY)
-    counts = (len(deltas), len(first_sums), len(later_sums), len(before), want)
+    counts = (len(deltas), len(first_sums), len(later_sums), len(before), len(past), want, int(keep))
     out_shape = [jax.ShapeDtypeStruct((rows, half), jnp.bfloat16)]
     if want:
+        out_shape.append(jax.ShapeDtypeStruct((rows, half), f32))
+    if keep:
         out_shape.append(jax.ShapeDtypeStruct((rows, half), f32))
     return pl.pallas_call(
         functools.partial(gate_body, weight.shape[0], span, counts),
@@ -594,6 +603,7 @@
     every = tuple(range(spans))
     deltas = [None] * spans
     later_sums = []
+    past = []
     for stage in range(sections):
         last_stage = stage + 1 == sections
         gates = []
@@ -601,10 +611,13 @@
         for span in every:
             got = gate(
                 meta, base, deltas[span], norm_gain, modes_here, taps, weight, first_sums,
-                later_sums, [states, partner], before, span,
+                later_sums, [states, partner], before, past if span == 0 else [],
+                span == 0 and stage == 0 and not last_stage, span,
             )
             gates.append(got[0])
-            before = list(got[1:])
+            before = list(got[1:2])
+            if len(got) == 3:
+                past = [got[2]]
         acc = None
         moving = list(gates)
         results = []

time: 111 us -> 111 us (level)
  no operation moved by 1% of the time
where the time goes in v3:
time: 111 us; the launch traced here: 110 us
  Pallas kernels  41.5 us (37%)
  starting transfers between devices  38.8 us (35%)
  waiting for transfers between devices  28.9 us (26%)
    ppermute x18, starting transfers between devices, swapped(): return lax.ppermute(value, 'seq', [(i, seqs - 1 - i) for i in range(seqs)])  24.9 us
    ppermute x15, waiting for transfers between devices, along_ring(): lax.ppermute(value, 'tensor', [(order[i], order[(i + shift) % tensors]) f...  21.3 us
    pallas_call x14, Pallas kernels, mix(): pl.pallas_call(functools.partial(mix_body, kind, chosen, counts, out_tile...  19.1 us
    pallas_call x4, Pallas kernels, gate(): pl.pallas_call(functools.partial(gate_body, weight.shape[0], span, counts...  11.2 us
    ppermute x15, starting transfers between devices, along_ring(): lax.ppermute(value, 'tensor', [(order[i], order[(i + shift) % tensors]) f...  10.7 us
    pallas_call x1, Pallas kernels, open_step(): pl.pallas_call(functools.partial(open_body, pieces, sizes, slot_total), o...  6.67 us
    pallas_call x1, Pallas kernels, history_states(): pl.pallas_call(functools.partial(history_body, sizes, slot_total), out_sh...  4.61 us
    ppermute x2, waiting for transfers between devices, to_next_across(): return lax.ppermute(value, ('tensor', 'section'), route)  3.87 us
  transfers between devices with their start and end apart: 38, of which 12 were waited for; matrix products, arithmetic and copies ran while one was open for 0% of the time, Pallas kernels for 28%

profile of v3, /device:TPU:1, one launch (start us, length us, event | category | flops | bytes accessed | tf_op | source)
XLA Modules:
  0.0 110.4 jit_solution(3306270676977495231)
XLA Ops:
  0.7 6.7 %open_step.1 = (f32[2,96,1024]{2,1,0:T(8,128)S(1)}, f32[2,8,96]{2,1,0:T(8,128)S(1)}, f32[2,16,1024]{2,1,0:T(8,128)S(1)}, bf16[8192,1024]{1,0:T(8,128)(2,1)S(1)}) custom-call(s32[3]{0:T(128)S(1)} %pad_add_fusion.meta, s32[1]{0:T(128)S(6)} %copy.11.span_any, s32[2,96]{1,0:T(2,128)} %ids_any.1, f32[512,2048]{1,0:T(8,128)} %table.1, f32[4,96,2048]{2,1,0:T(8,128)} %bitcast.9, ...), custom_call_target="tpu_custom_call" | custom-call | flops 12582912 | bytes 4194304 | tf_op jit(solution)/shard_map/open_step/pallas_call | solution.py:190
  7.5 2.7 %collective-permute-start.1 = (f32[2,8,96]{2,1,0:T(8,128)S(1)}, f32[2,8,96]{2,1,0:T(8,128)S(1)}, u32[]{:S(2)}, u32[]{:S(2)}) collective-permute-start(f32[2,8,96]{2,1,0:T(8,128)S(1)} %get-tuple-element.31.rest_7_.rest_8_), channel_id=1, source_target_pairs={{0,4},{4,12},{12,8},{8,0},{1,5},{5,13},{13,9},{9,1},{2,6},{6,14},{... | collective-permute-start | bytes 18440 | tf_op jit(solution)/shard_map/ppermute | solution.py:565
  10.2 2.2 %collective-permute-start.2 = (f32[2,8,96]{2,1,0:T(8,128)S(1)}, f32[2,8,96]{2,1,0:T(8,128)S(1)}, u32[]{:S(2)}, u32[]{:S(2)}) collective-permute-start(f32[2,8,96]{2,1,0:T(8,128)S(1)} %get-tuple-element.31.rest_7_.rest_8_), channel_id=1, source_target_pairs={{0,12},{4,8},{12,0},{8,4},{1,13},{5,9},{13,1},{9,5},{2,14},{6,10},... | collective-permute-start | bytes 18440 | tf_op jit(solution)/shard_map/ppermute | solution.py:565
  12.4 1.3 %collective-permute-start.3 = (f32[2,8,96]{2,1,0:T(8,128)S(1)}, f32[2,8,96]{2,1,0:T(8,128)S(1)}, u32[]{:S(2)}, u32[]{:S(2)}) collective-permute-start(f32[2,8,96]{2,1,0:T(8,128)S(1)} %get-tuple-element.31.rest_7_.rest_8_), channel_id=1, source_target_pairs={{0,8},{4,0},{12,4},{8,12},{1,9},{5,1},{13,5},{9,13},{2,10},{6,2},{... | collective-permute-start | bytes 18440 | tf_op jit(solution)/shard_map/ppermute | solution.py:565
  13.7 4.6 %history_states.1 = (f32[2,16,1024]{2,1,0:T(8,128)S(1)}, f32[96,1024]{1,0:T(8,128)S(1)}, f32[16,1024]{1,0:T(8,128)S(1)}, f32[16,1024]{1,0:T(8,128)S(1)}, bf16[8192,1024]{1,0:T(8,128)(2,1)S(1)}) custom-call(s32[3]{0:T(128)S(1)} %pad_add_fusion.meta, s32[1]{0:T(128)S(6)} %copy.11.span_any, f32[4,96,2048]{2,1,0:T(8,128)} %bitcast.10, ...), custom_call_target="tpu_custom_call", output_to_operand_aliasing={{4}: (6, {})} | custom-call | flops 12582912 | bytes 1572864 | tf_op jit(solution)/shard_map/history_states/pallas_call | solution.py:273
  18.3 2.7 %gate.4 = (bf16[96,1024]{1,0:T(8,128)(2,1)S(1)}, f32[96,1024]{1,0:T(8,128)S(1)}, f32[96,1024]{1,0:T(8,128)S(1)}) custom-call(s32[3]{0:T(128)S(1)} %pad_add_fusion.meta, f32[2,96,1024]{2,1,0:T(8,128)S(1)} %get-tuple-element.23.base.refs_3_, f32[1,2048]{1,0:T(1,128)S(1)} %copy-done, f32[16,1024]{1,0:T(8,128)S(1)} %get-tuple-element.25.rest_1_.rest_2_, ...), custom_call_target="tpu_custom_call" | custom-call | flops 15728640 | bytes 1179648 | tf_op jit(solution)/shard_map/gate/pallas_call | solution.py:418
  21.2 3.1 %gate.5.refs_1_ = bf16[96,1024]{1,0:T(8,128)(2,1)S(1)} custom-call(s32[3]{0:T(128)S(1)} %pad_add_fusion.meta, f32[2,96,1024]{2,1,0:T(8,128)S(1)} %get-tuple-element.23.base.refs_3_, f32[1,2048]{1,0:T(1,128)S(1)} %copy-done, f32[16,1024]{1,0:T(8,128)S(1)} %get-tuple-element.25.rest_1_.rest_2_, f32[16,1024]{1,0:T(8,128)S(1)} %get-tuple-element.26.rest_2_.rest_3_, ...), custom_call_target="tpu_custom_call" | custom-call | flops 15728640 | bytes 1179648 | tf_op jit(solution)/shard_map/gate/pallas_call | solution.py:418
  24.4 1.1 collective-permute-start.4
  25.4 2.1 %collective-permute-done.8.refs_0_ = bf16[96,1024]{1,0:T(8,128)(2,1)S(1)} collective-permute-done((bf16[96,1024]{1,0:T(8,128)(2,1)S(1)}, bf16[96,1024]{1,0:T(8,128)(2,1)S(1)}, u32[]{:S(2)}, u32[]{:S(2)}) %collective-permute-start.8) | collective-permute-done | bytes 196640 | tf_op jit(solution)/shard_map/ppermute | solution.py:565
  27.5 4.7 %collective-permute-done.4.refs_1_ = bf16[96,1024]{1,0:T(8,128)(2,1)S(1)} collective-permute-done((bf16[96,1024]{1,0:T(8,128)(2,1)S(1)}, bf16[96,1024]{1,0:T(8,128)(2,1)S(1)}, u32[]{:S(2)}, u32[]{:S(2)}) %collective-permute-start.4) | collective-permute-done | bytes 196640 | tf_op jit(solution)/shard_map/ppermute | solution.py:565
  32.3 2.2 %collective-permute-start.15 = (bf16[96,1024]{1,0:T(8,128)(2,1)S(1)}, bf16[96,1024]{1,0:T(8,128)(2,1)S(1)}, u32[]{:S(2)}, u32[]{:S(2)}) collective-permute-start(bf16[96,1024]{1,0:T(8,128)(2,1)S(1)} %gate.5.refs_1_), channel_id=1, source_target_pairs={{0,1},{1,0},{2,3},{3,2},{4,5},{5,4},{6,7},{7,6},{8,9},{9,8},{10,11... | collective-permute-start | bytes 589832 | tf_op jit(solution)/shard_map/ppermute | solution.py:570
  34.9 1.3 %collective-permute-done.9.refs_0_ = bf16[96,1024]{1,0:T(8,128)(2,1)S(1)} collective-permute-done((bf16[96,1024]{1,0:T(8,128)(2,1)S(1)}, bf16[96,1024]{1,0:T(8,128)(2,1)S(1)}, u32[]{:S(2)}, u32[]{:S(2)}) %collective-permute-start.9) | collective-permute-done | bytes 196640 | tf_op jit(solution)/shard_map/ppermute | solution.py:565
  36.4 4.0 %collective-permute-done.5.refs_1_ = bf16[96,1024]{1,0:T(8,128)(2,1)S(1)} collective-permute-done((bf16[96,1024]{1,0:T(8,128)(2,1)S(1)}, bf16[96,1024]{1,0:T(8,128)(2,1)S(1)}, u32[]{:S(2)}, u32[]{:S(2)}) %collective-permute-start.5) | collective-permute-done | bytes 196640 | tf_op jit(solution)/shard_map/ppermute | solution.py:565
  40.4 2.6 %collective-permute-start.12 = (bf16[96,1024]{1,0:T(8,128)(2,1)S(1)}, bf16[96,1024]{1,0:T(8,128)(2,1)S(1)}, u32[]{:S(2)}, u32[]{:S(2)}) collective-permute-start(bf16[96,1024]{1,0:T(8,128)(2,1)S(1)} %collective-permute-done.8.refs_0_), channel_id=1, source_target_pairs={{0,1},{1,0},{2,3},{3,2},{4,5},{5,4},{6,7},{7,6},{8,9},{9,8},{10,11... | collective-permute-start | bytes 589832 | tf_op jit(solution)/shard_map/ppermute | solution.py:570
  43.6 0.8 collective-permute-done.16.refs_0_
  44.4 3.1 %collective-permute-start.17 = (bf16[96,1024]{1,0:T(8,128)(2,1)S(1)}, bf16[96,1024]{1,0:T(8,128)(2,1)S(1)}, u32[]{:S(2)}, u32[]{:S(2)}) collective-permute-start(bf16[96,1024]{1,0:T(8,128)(2,1)S(1)} %collective-permute-done.16.refs_0_), channel_id=1, source_target_pairs={{0,1},{1,0},{2,3},{3,2},{4,5},{5,4},{6,7},{7,6},{8,9},{9,8},{10,11... | collective-permute-start | bytes 589832 | tf_op jit(solution)/shard_map/ppermute | solution.py:570
  47.5 1.6 %shard_map.82.refs_5_ = f32[192,1024]{1,0:T(8,128)S(1)} custom-call(s32[3]{0:T(128)S(1)} %pad_add_fusion.meta, bf16[96,1024]{1,0:T(8,128)(2,1)S(1)} %get-tuple-element.33.refs_0_, bf16[96,1024]{1,0:T(8,128)(2,1)S(1)} %gate.5.refs_1_, bf16[96,1024]{1,0:T(8,128)(2,1)S(1)} %collective-permute-done.14.refs_2_, ...), custom_call_target="tpu_custom_call" | custom-call | flops 805306368 | bytes 4194304 | tf_op jit(solution)/shard_map/pallas_call | solution.py:530
  49.1 1.3 %collective-permute-start.7 = (bf16[96,1024]{1,0:T(8,128)(2,1)S(1)}, bf16[96,1024]{1,0:T(8,128)(2,1)S(1)}, u32[]{:S(2)}, u32[]{:S(2)}) collective-permute-start(bf16[96,1024]{1,0:T(8,128)(2,1)S(1)} %collective-permute-done.6.refs_0_), channel_id=1, source_target_pairs={{0,1},{1,0},{2,3},{3,2},{4,5},{5,4},{6,7},{7,6},{8,9},{9,8},{10,11... | collective-permute-start | bytes 589832 | tf_op jit(solution)/shard_map/ppermute | solution.py:570
  50.4 1.6 %shard_map.83.refs_5_ = f32[192,1024]{1,0:T(8,128)S(1)} custom-call(s32[3]{0:T(128)S(1)} %pad_add_fusion.meta, bf16[96,1024]{1,0:T(8,128)(2,1)S(1)} %collective-permute-done.8.refs_0_, bf16[96,1024]{1,0:T(8,128)(2,1)S(1)} %collective-permute-done.4.refs_1_, bf16[96,1024]{1,0:T(8,128)(2,1)S(1)} %collective-permute-done.12.refs_2_, ...), custom_call_target="tpu_custom_call" | custom-call | flops 805306368 | bytes 4194304 | tf_op jit(solution)/shard_map/pallas_call | solution.py:530
  52.0 1.6 %shard_map.84.refs_2_ = f32[192,1024]{1,0:T(8,128)S(1)} custom-call(s32[3]{0:T(128)S(1)} %pad_add_fusion.meta, bf16[96,1024]{1,0:T(8,128)(2,1)S(1)} %collective-permute-done.9.refs_0_, bf16[96,1024]{1,0:T(8,128)(2,1)S(1)} %collective-permute-done.5.refs_1_, bf16[96,1024]{1,0:T(8,128)(2,1)S(1)} %collective-permute-done.10.refs_2_, ...), custom_call_target="tpu_custom_call" | custom-call | flops 805306368 | bytes 4194304 | tf_op jit(solution)/shard_map/pallas_call | solution.py:530
  53.5 1.0 shard_map.86.refs_2_
  54.6 1.3 %shard_map.87 = (bf16[96,1024]{1,0:T(8,128)(2,1)S(1)}, f32[2,8,96]{2,1,0:T(8,128)S(1)}) custom-call(s32[3]{0:T(128)S(1)} %pad_add_fusion.meta, bf16[96,1024]{1,0:T(8,128)(2,1)S(1)} %collective-permute-done.17.refs_0_, bf16[8192,1024]{1,0:T(8,128)(2,1)S(1)} %get-tuple-element.30.rest_6_.refs_4_.refs_1_.rest_7_, f32[96,1024]{1,0:T(8,128)S(1)} %shard_map.86.refs_2_, ...), custom_call_target="tpu_custom_call" | custom-call | flops 201326592 | bytes 2097152 | tf_op jit(solution)/shard_map/pallas_call | solution.py:530
  55.9 1.2 %collective-permute-start.23 = (bf16[96,1024]{1,0:T(8,128)(2,1)S(1)}, bf16[96,1024]{1,0:T(8,128)(2,1)S(1)}, u32[]{:S(2)}, u32[]{:S(2)}) collective-permute-start(bf16[96,1024]{1,0:T(8,128)(2,1)S(1)} %get-tuple-element.37), channel_id=1, source_target_pairs={{0,2},{2,0},{1,3},{3,1},{4,6},{6,4},{5,7},{7,5},{8,10},{10,8},{9,1... | collective-permute-start | bytes 589832 | tf_op jit(solution)/shard_map/ppermute | solution.py:573
  57.2 1.0 shard_map.85.refs_2_
  58.2 1.3 %shard_map.88 = (bf16[96,1024]{1,0:T(8,128)(2,1)S(1)}, f32[2,8,96]{2,1,0:T(8,128)S(1)}) custom-call(s32[3]{0:T(128)S(1)} %pad_add_fusion.meta, bf16[96,1024]{1,0:T(8,128)(2,1)S(1)} %collective-permute-done.7.refs_0_, bf16[8192,1024]{1,0:T(8,128)(2,1)S(1)} %get-tuple-element.30.rest_6_.refs_4_.refs_1_.rest_7_, f32[96,1024]{1,0:T(8,128)S(1)} %shard_map.85.refs_2_, ...), custom_call_target="tpu_custom_call" | custom-call | flops 201326592 | bytes 2097152 | tf_op jit(solution)/shard_map/pallas_call | solution.py:530
  59.9 0.6 collective-permute-start.19
  60.4 0.8 collective-permute-done.19
  61.3 2.8 %collective-permute-done.20 = f32[2,8,96]{2,1,0:T(8,128)S(1)} collective-permute-done((f32[2,8,96]{2,1,0:T(8,128)S(1)}, f32[2,8,96]{2,1,0:T(8,128)S(1)}, u32[]{:S(2)}, u32[]{:S(2)}) %collective-permute-start.20) | collective-permute-done | bytes 6176 | tf_op jit(solution)/shard_map/ppermute | solution.py:576
  64.1 1.2 %collective-permute-start.21 = (f32[2,8,96]{2,1,0:T(8,128)S(1)}, f32[2,8,96]{2,1,0:T(8,128)S(1)}, u32[]{:S(2)}, u32[]{:S(2)}) collective-permute-start(f32[2,8,96]{2,1,0:T(8,128)S(1)} %add.7), channel_id=1, source_target_pairs={{0,2},{2,0},{4,6},{6,4},{8,10},{10,8},{12,14},{14,12},{1,3},{3,1},... | collective-permute-start | bytes 18440 | tf_op jit(solution)/shard_map/ppermute | solution.py:583
  65.7 1.3 %collective-permute-done.21.rest_12_ = f32[2,8,96]{2,1,0:T(8,128)S(1)} collective-permute-done((f32[2,8,96]{2,1,0:T(8,128)S(1)}, f32[2,8,96]{2,1,0:T(8,128)S(1)}, u32[]{:S(2)}, u32[]{:S(2)}) %collective-permute-start.21) | collective-permute-done | bytes 6176 | tf_op jit(solution)/shard_map/ppermute | solution.py:583
  66.9 2.6 %collective-permute-done.22.rest_13_ = f32[2,8,96]{2,1,0:T(8,128)S(1)} collective-permute-done((f32[2,8,96]{2,1,0:T(8,128)S(1)}, f32[2,8,96]{2,1,0:T(8,128)S(1)}, u32[]{:S(2)}, u32[]{:S(2)}) %collective-permute-start.22) | collective-permute-done | bytes 6176 | tf_op jit(solution)/shard_map/ppermute | solution.py:583
  69.6 2.2 %gate.6 = (bf16[96,1024]{1,0:T(8,128)(2,1)S(1)}, f32[96,1024]{1,0:T(8,128)S(1)}) custom-call(s32[3]{0:T(128)S(1)} %pad_add_fusion.meta, f32[2,96,1024]{2,1,0:T(8,128)S(1)} %get-tuple-element.23.base.refs_3_, bf16[96,1024]{1,0:T(8,128)(2,1)S(1)} %collective-permute-done.23.rest_0_.refs_4_, f32[1,2048]{1,0:T(1,128)S(1)} %copy-done, ...), custom_call_target="tpu_custom_call" | custom-call | flops 15728640 | bytes 1179648 | tf_op jit(solution)/shard_map/gate/pallas_call | solution.py:418
  71.8 3.2 %gate.7.refs_1_ = bf16[96,1024]{1,0:T(8,128)(2,1)S(1)} custom-call(s32[3]{0:T(128)S(1)} %pad_add_fusion.meta, f32[2,96,1024]{2,1,0:T(8,128)S(1)} %get-tuple-element.23.base.refs_3_, bf16[96,1024]{1,0:T(8,128)(2,1)S(1)} %collective-permute-done.18.rest_0_.refs_4_, f32[1,2048]{1,0:T(1,128)S(1)} %copy-done, f32[16,1024]{1,0:T(8,128)S(1)} %get-tuple-element.25.rest_1_.rest_2_, ...), custom_call_target="tpu_custom_call" | custom-call | flops 15728640 | bytes 1179648 | tf_op jit(solution)/shard_map/gate/pallas_call | solution.py:418
  75.0 1.2 %collective-permute-start.24 = (bf16[96,1024]{1,0:T(8,128)(2,1)S(1)}, bf16[96,1024]{1,0:T(8,128)(2,1)S(1)}, u32[]{:S(2)}, u32[]{:S(2)}) collective-permute-start(bf16[96,1024]{1,0:T(8,128)(2,1)S(1)} %gate.7.refs_1_), channel_id=1, source_target_pairs={{0,4},{4,12},{12,8},{8,0},{1,5},{5,13},{13,9},{9,1},{2,6},{6,14},{... | collective-permute-start | bytes 589832 | tf_op jit(solution)/shard_map/ppermute | solution.py:565
  76.2 1.0 collective-permute-done.28.refs_0_
  77.2 5.7 %collective-permute-done.24.refs_1_ = bf16[96,1024]{1,0:T(8,128)(2,1)S(1)} collective-permute-done((bf16[96,1024]{1,0:T(8,128)(2,1)S(1)}, bf16[96,1024]{1,0:T(8,128)(2,1)S(1)}, u32[]{:S(2)}, u32[]{:S(2)}) %collective-permute-start.24) | collective-permute-done | bytes 196640 | tf_op jit(solution)/shard_map/ppermute | solution.py:565
  82.9 4.2 %collective-permute-start.35 = (bf16[96,1024]{1,0:T(8,128)(2,1)S(1)}, bf16[96,1024]{1,0:T(8,128)(2,1)S(1)}, u32[]{:S(2)}, u32[]{:S(2)}) collective-permute-start(bf16[96,1024]{1,0:T(8,128)(2,1)S(1)} %gate.7.refs_1_), channel_id=1, source_target_pairs={{0,1},{1,0},{2,3},{3,2},{4,5},{5,4},{6,7},{7,6},{8,9},{9,8},{10,11... | collective-permute-start | bytes 589832 | tf_op jit(solution)/shard_map/ppermute | solution.py:570
  87.6 1.7 %collective-permute-start.36 = (bf16[96,1024]{1,0:T(8,128)(2,1)S(1)}, bf16[96,1024]{1,0:T(8,128)(2,1)S(1)}, u32[]{:S(2)}, u32[]{:S(2)}) collective-permute-start(bf16[96,1024]{1,0:T(8,128)(2,1)S(1)} %collective-permute-done.29.refs_0_), channel_id=1, source_target_pairs={{0,4},{4,12},{12,8},{8,0},{1,5},{5,13},{13,9},{9,1},{2,6},{6,14},{... | collective-permute-start | bytes 589832 | tf_op jit(solution)/shard_map/ppermute | solution.py:565
  89.3 1.7 %collective-permute-done.25.refs_1_ = bf16[96,1024]{1,0:T(8,128)(2,1)S(1)} collective-permute-done((bf16[96,1024]{1,0:T(8,128)(2,1)S(1)}, bf16[96,1024]{1,0:T(8,128)(2,1)S(1)}, u32[]{:S(2)}, u32[]{:S(2)}) %collective-permute-start.25) | collective-permute-done | bytes 196640 | tf_op jit(solution)/shard_map/ppermute | solution.py:565
  91.1 4.4 %collective-permute-start.32 = (bf16[96,1024]{1,0:T(8,128)(2,1)S(1)}, bf16[96,1024]{1,0:T(8,128)(2,1)S(1)}, u32[]{:S(2)}, u32[]{:S(2)}) collective-permute-start(bf16[96,1024]{1,0:T(8,128)(2,1)S(1)} %collective-permute-done.28.refs_0_), channel_id=1, source_target_pairs={{0,1},{1,0},{2,3},{3,2},{4,5},{5,4},{6,7},{7,6},{8,9},{9,8},{10,11... | collective-permute-start | bytes 589832 | tf_op jit(solution)/shard_map/ppermute | solution.py:570
  96.0 4.0 %collective-permute-start.37 = (bf16[96,1024]{1,0:T(8,128)(2,1)S(1)}, bf16[96,1024]{1,0:T(8,128)(2,1)S(1)}, u32[]{:S(2)}, u32[]{:S(2)}) collective-permute-start(bf16[96,1024]{1,0:T(8,128)(2,1)S(1)} %collective-permute-done.36.refs_0_), channel_id=1, source_target_pairs={{0,1},{1,0},{2,3},{3,2},{4,5},{5,4},{6,7},{7,6},{8,9},{9,8},{10,11... | collective-permute-start | bytes 589832 | tf_op jit(solution)/shard_map/ppermute | solution.py:570
  100.0 1.6 %shard_map.89.refs_5_ = f32[192,1024]{1,0:T(8,128)S(1)} custom-call(s32[3]{0:T(128)S(1)} %pad_add_fusion.meta, bf16[96,1024]{1,0:T(8,128)(2,1)S(1)} %get-tuple-element.40.refs_0_, bf16[96,1024]{1,0:T(8,128)(2,1)S(1)} %gate.7.refs_1_, bf16[96,1024]{1,0:T(8,128)(2,1)S(1)} %collective-permute-done.34.refs_2_, ...), custom_call_target="tpu_custom_call" | custom-call | flops 805306368 | bytes 4194304 | tf_op jit(solution)/shard_map/pallas_call | solution.py:530
  102.1 1.6 %shard_map.90.refs_5_ = f32[192,1024]{1,0:T(8,128)S(1)} custom-call(s32[3]{0:T(128)S(1)} %pad_add_fusion.meta, bf16[96,1024]{1,0:T(8,128)(2,1)S(1)} %collective-permute-done.28.refs_0_, bf16[96,1024]{1,0:T(8,128)(2,1)S(1)} %collective-permute-done.24.refs_1_, bf16[96,1024]{1,0:T(8,128)(2,1)S(1)} %collective-permute-done.32.refs_2_, ...), custom_call_target="tpu_custom_call" | custom-call | flops 805306368 | bytes 4194304 | tf_op jit(solution)/shard_map/pallas_call | solution.py:530
  103.7 1.6 %shard_map.91.refs_2_ = f32[192,1024]{1,0:T(8,128)S(1)} custom-call(s32[3]{0:T(128)S(1)} %pad_add_fusion.meta, bf16[96,1024]{1,0:T(8,128)(2,1)S(1)} %collective-permute-done.29.refs_0_, bf16[96,1024]{1,0:T(8,128)(2,1)S(1)} %collective-permute-done.25.refs_1_, bf16[96,1024]{1,0:T(8,128)(2,1)S(1)} %collective-permute-done.30.refs_2_, ...), custom_call_target="tpu_custom_call" | custom-call | flops 805306368 | bytes 4194304 | tf_op jit(solution)/shard_map/pallas_call | solution.py:530
  105.3 1.0 shard_map.93.refs_2_
  106.3 1.1 shard_map.92.refs_2_
  107.4 1.1 shard_map.94.refs_5_
  108.5 1.8 %shard_map.95 = f32[1,2,96,1024]{3,2,1,0:T(8,128)} custom-call(s32[3]{0:T(128)S(1)} %pad_add_fusion.meta, bf16[96,1024]{1,0:T(8,128)(2,1)S(1)} %collective-permute-done.27.refs_0_, bf16[8192,1024]{1,0:T(8,128)(2,1)S(1)} %get-tuple-element.30.rest_6_.refs_4_.refs_1_.rest_7_, f32[96,1024]{1,0:T(8,128)S(1)} %shard_map.92.refs_2_, ...), custom_call_target="tpu_custom_call" | custom-call | flops 201326592 | bytes 2097152 | tf_op jit(solution)/shard_map/pallas_call | solution.py:530
  (53 shorter events, 4.0 us)
Async XLA Ops:
  7.4 10.9 %collective-permute-start = (f32[2,16,1024]{2,1,0:T(8,128)S(1)}, f32[2,16,1024]{2,1,0:T(8,128)S(1)}, u32[]{:S(2)}, u32[]{:S(2)}) collective-permute-start(f32[2,16,1024]{2,1,0:T(8,128)S(1)} %get-tuple-element.29), channel_id=1, source_target_pairs={{0,1},{1,0},{2,3},{3,2},{4,5},{5,4},{6,7},{7,6},{8,9},{9,8},{10,11... | collective-permute-start | bytes 393224 | tf_op jit(solution)/shard_map/ppermute | solution.py:570
  7.5 10.8 %collective-permute-start.1 = (f32[2,8,96]{2,1,0:T(8,128)S(1)}, f32[2,8,96]{2,1,0:T(8,128)S(1)}, u32[]{:S(2)}, u32[]{:S(2)}) collective-permute-start(f32[2,8,96]{2,1,0:T(8,128)S(1)} %get-tuple-element.31.rest_7_.rest_8_), channel_id=1, source_target_pairs={{0,4},{4,12},{12,8},{8,0},{1,5},{5,13},{13,9},{9,1},{2,6},{6,14},{... | collective-permute-start | bytes 18440 | tf_op jit(solution)/shard_map/ppermute | solution.py:565
  10.2 8.1 %collective-permute-start.2 = (f32[2,8,96]{2,1,0:T(8,128)S(1)}, f32[2,8,96]{2,1,0:T(8,128)S(1)}, u32[]{:S(2)}, u32[]{:S(2)}) collective-permute-start(f32[2,8,96]{2,1,0:T(8,128)S(1)} %get-tuple-element.31.rest_7_.rest_8_), channel_id=1, source_target_pairs={{0,12},{4,8},{12,0},{8,4},{1,13},{5,9},{13,1},{9,5},{2,14},{6,10},... | collective-permute-start | bytes 18440 | tf_op jit(solution)/shard_map/ppermute | solution.py:565
  12.4 5.9 %collective-permute-start.3 = (f32[2,8,96]{2,1,0:T(8,128)S(1)}, f32[2,8,96]{2,1,0:T(8,128)S(1)}, u32[]{:S(2)}, u32[]{:S(2)}) collective-permute-start(f32[2,8,96]{2,1,0:T(8,128)S(1)} %get-tuple-element.31.rest_7_.rest_8_), channel_id=1, source_target_pairs={{0,8},{4,0},{12,4},{8,12},{1,9},{5,1},{13,5},{9,13},{2,10},{6,2},{... | collective-permute-start | bytes 18440 | tf_op jit(solution)/shard_map/ppermute | solution.py:565
  13.7 4.7 %copy-start = (f32[1,2048]{1,0:T(1,128)S(1)}, f32[1,2048]{1,0:T(1,128)}, u32[]{:S(2)}) copy-start(f32[1,2048]{1,0:T(1,128)} %rest_1_.3) | copy-start | bytes 24580
  21.0 6.5 %collective-permute-start.8 = (bf16[96,1024]{1,0:T(8,128)(2,1)S(1)}, bf16[96,1024]{1,0:T(8,128)(2,1)S(1)}, u32[]{:S(2)}, u32[]{:S(2)}) collective-permute-start(bf16[96,1024]{1,0:T(8,128)(2,1)S(1)} %get-tuple-element.33.refs_0_), channel_id=1, source_target_pairs={{0,4},{4,12},{12,8},{8,0},{1,5},{5,13},{13,9},{9,1},{2,6},{6,14},{... | collective-permute-start | bytes 589832 | tf_op jit(solution)/shard_map/ppermute | solution.py:565
  24.4 7.9 %collective-permute-start.4 = (bf16[96,1024]{1,0:T(8,128)(2,1)S(1)}, bf16[96,1024]{1,0:T(8,128)(2,1)S(1)}, u32[]{:S(2)}, u32[]{:S(2)}) collective-permute-start(bf16[96,1024]{1,0:T(8,128)(2,1)S(1)} %gate.5.refs_1_), channel_id=1, source_target_pairs={{0,4},{4,12},{12,8},{8,0},{1,5},{5,13},{13,9},{9,1},{2,6},{6,14},{... | collective-permute-start | bytes 589832 | tf_op jit(solution)/shard_map/ppermute | solution.py:565
  27.5 8.7 %collective-permute-start.9 = (bf16[96,1024]{1,0:T(8,128)(2,1)S(1)}, bf16[96,1024]{1,0:T(8,128)(2,1)S(1)}, u32[]{:S(2)}, u32[]{:S(2)}) collective-permute-start(bf16[96,1024]{1,0:T(8,128)(2,1)S(1)} %collective-permute-done.8.refs_0_), channel_id=1, source_target_pairs={{0,4},{4,12},{12,8},{8,0},{1,5},{5,13},{13,9},{9,1},{2,6},{6,14},{... | collective-permute-start | bytes 589832 | tf_op jit(solution)/shard_map/ppermute | solution.py:565
  32.3 8.2 %collective-permute-start.5 = (bf16[96,1024]{1,0:T(8,128)(2,1)S(1)}, bf16[96,1024]{1,0:T(8,128)(2,1)S(1)}, u32[]{:S(2)}, u32[]{:S(2)}) collective-permute-start(bf16[96,1024]{1,0:T(8,128)(2,1)S(1)} %collective-permute-done.4.refs_1_), channel_id=1, source_target_pairs={{0,4},{4,12},{12,8},{8,0},{1,5},{5,13},{13,9},{9,1},{2,6},{6,14},{... | collective-permute-start | bytes 589832 | tf_op jit(solution)/shard_map/ppermute | solution.py:565
  32.3 8.2 %collective-permute-start.15 = (bf16[96,1024]{1,0:T(8,128)(2,1)S(1)}, bf16[96,1024]{1,0:T(8,128)(2,1)S(1)}, u32[]{:S(2)}, u32[]{:S(2)}) collective-permute-start(bf16[96,1024]{1,0:T(8,128)(2,1)S(1)} %gate.5.refs_1_), channel_id=1, source_target_pairs={{0,1},{1,0},{2,3},{3,2},{4,5},{5,4},{6,7},{7,6},{8,9},{9,8},{10,11... | collective-permute-start | bytes 589832 | tf_op jit(solution)/shard_map/ppermute | solution.py:570
  34.4 8.6 %collective-permute-start.14 = (bf16[96,1024]{1,0:T(8,128)(2,1)S(1)}, bf16[96,1024]{1,0:T(8,128)(2,1)S(1)}, u32[]{:S(2)}, u32[]{:S(2)}) collective-permute-start(bf16[96,1024]{1,0:T(8,128)(2,1)S(1)} %get-tuple-element.33.refs_0_), channel_id=1, source_target_pairs={{0,1},{1,0},{2,3},{3,2},{4,5},{5,4},{6,7},{7,6},{8,9},{9,8},{10,11... | collective-permute-start | bytes 589832 | tf_op jit(solution)/shard_map/ppermute | solution.py:570
  34.4 8.7 %collective-permute-start.13 = (bf16[96,1024]{1,0:T(8,128)(2,1)S(1)}, bf16[96,1024]{1,0:T(8,128)(2,1)S(1)}, u32[]{:S(2)}, u32[]{:S(2)}) collective-permute-start(bf16[96,1024]{1,0:T(8,128)(2,1)S(1)} %collective-permute-done.4.refs_1_), channel_id=1, source_target_pairs={{0,1},{1,0},{2,3},{3,2},{4,5},{5,4},{6,7},{7,6},{8,9},{9,8},{10,11... | collective-permute-start | bytes 589832 | tf_op jit(solution)/shard_map/ppermute | solution.py:570
  36.2 8.2 %collective-permute-start.16 = (bf16[96,1024]{1,0:T(8,128)(2,1)S(1)}, bf16[96,1024]{1,0:T(8,128)(2,1)S(1)}, u32[]{:S(2)}, u32[]{:S(2)}) collective-permute-start(bf16[96,1024]{1,0:T(8,128)(2,1)S(1)} %collective-permute-done.9.refs_0_), channel_id=1, source_target_pairs={{0,4},{4,12},{12,8},{8,0},{1,5},{5,13},{13,9},{9,1},{2,6},{6,14},{... | collective-permute-start | bytes 589832 | tf_op jit(solution)/shard_map/ppermute | solution.py:565
  40.4 8.6 %collective-permute-start.6 = (bf16[96,1024]{1,0:T(8,128)(2,1)S(1)}, bf16[96,1024]{1,0:T(8,128)(2,1)S(1)}, u32[]{:S(2)}, u32[]{:S(2)}) collective-permute-start(bf16[96,1024]{1,0:T(8,128)(2,1)S(1)} %collective-permute-done.5.refs_1_), channel_id=1, source_target_pairs={{0,4},{4,12},{12,8},{8,0},{1,5},{5,13},{13,9},{9,1},{2,6},{6,14},{... | collective-permute-start | bytes 589832 | tf_op jit(solution)/shard_map/ppermute | solution.py:565
  40.4 9.9 %collective-permute-start.12 = (bf16[96,1024]{1,0:T(8,128)(2,1)S(1)}, bf16[96,1024]{1,0:T(8,128)(2,1)S(1)}, u32[]{:S(2)}, u32[]{:S(2)}) collective-permute-start(bf16[96,1024]{1,0:T(8,128)(2,1)S(1)} %collective-permute-done.8.refs_0_), channel_id=1, source_target_pairs={{0,1},{1,0},{2,3},{3,2},{4,5},{5,4},{6,7},{7,6},{8,9},{9,8},{10,11... | collective-permute-start | bytes 589832 | tf_op jit(solution)/shard_map/ppermute | solution.py:570
  43.0 8.9 %collective-permute-start.11 = (bf16[96,1024]{1,0:T(8,128)(2,1)S(1)}, bf16[96,1024]{1,0:T(8,128)(2,1)S(1)}, u32[]{:S(2)}, u32[]{:S(2)}) collective-permute-start(bf16[96,1024]{1,0:T(8,128)(2,1)S(1)} %collective-permute-done.5.refs_1_), channel_id=1, source_target_pairs={{0,1},{1,0},{2,3},{3,2},{4,5},{5,4},{6,7},{7,6},{8,9},{9,8},{10,11... | collective-permute-start | bytes 589832 | tf_op jit(solution)/shard_map/ppermute | solution.py:570
  43.1 8.8 %collective-permute-start.10 = (bf16[96,1024]{1,0:T(8,128)(2,1)S(1)}, bf16[96,1024]{1,0:T(8,128)(2,1)S(1)}, u32[]{:S(2)}, u32[]{:S(2)}) collective-permute-start(bf16[96,1024]{1,0:T(8,128)(2,1)S(1)} %collective-permute-done.9.refs_0_), channel_id=1, source_target_pairs={{0,1},{1,0},{2,3},{3,2},{4,5},{5,4},{6,7},{7,6},{8,9},{9,8},{10,11... | collective-permute-start | bytes 589832 | tf_op jit(solution)/shard_map/ppermute | solution.py:570
  44.4 10.2 %collective-permute-start.17 = (bf16[96,1024]{1,0:T(8,128)(2,1)S(1)}, bf16[96,1024]{1,0:T(8,128)(2,1)S(1)}, u32[]{:S(2)}, u32[]{:S(2)}) collective-permute-start(bf16[96,1024]{1,0:T(8,128)(2,1)S(1)} %collective-permute-done.16.refs_0_), channel_id=1, source_target_pairs={{0,1},{1,0},{2,3},{3,2},{4,5},{5,4},{6,7},{7,6},{8,9},{9,8},{10,11... | collective-permute-start | bytes 589832 | tf_op jit(solution)/shard_map/ppermute | solution.py:570
  49.1 9.2 %collective-permute-start.7 = (bf16[96,1024]{1,0:T(8,128)(2,1)S(1)}, bf16[96,1024]{1,0:T(8,128)(2,1)S(1)}, u32[]{:S(2)}, u32[]{:S(2)}) collective-permute-start(bf16[96,1024]{1,0:T(8,128)(2,1)S(1)} %collective-permute-done.6.refs_0_), channel_id=1, source_target_pairs={{0,1},{1,0},{2,3},{3,2},{4,5},{5,4},{6,7},{7,6},{8,9},{9,8},{10,11... | collective-permute-start | bytes 589832 | tf_op jit(solution)/shard_map/ppermute | solution.py:570
  55.9 13.6 %collective-permute-start.23 = (bf16[96,1024]{1,0:T(8,128)(2,1)S(1)}, bf16[96,1024]{1,0:T(8,128)(2,1)S(1)}, u32[]{:S(2)}, u32[]{:S(2)}) collective-permute-start(bf16[96,1024]{1,0:T(8,128)(2,1)S(1)} %get-tuple-element.37), channel_id=1, source_target_pairs={{0,2},{2,0},{1,3},{3,1},{4,6},{6,4},{5,7},{7,5},{8,10},{10,8},{9,1... | collective-permute-start | bytes 589832 | tf_op jit(solution)/shard_map/ppermute | solution.py:573
  59.6 12.2 %collective-permute-start.18 = (bf16[96,1024]{1,0:T(8,128)(2,1)S(1)}, bf16[96,1024]{1,0:T(8,128)(2,1)S(1)}, u32[]{:S(2)}, u32[]{:S(2)}) collective-permute-start(bf16[96,1024]{1,0:T(8,128)(2,1)S(1)} %get-tuple-element.35), channel_id=1, source_target_pairs={{0,2},{2,0},{1,3},{3,1},{4,6},{6,4},{5,7},{7,5},{8,10},{10,8},{9,1... | collective-permute-start | bytes 589832 | tf_op jit(solution)/shard_map/ppermute | solution.py:573
  59.9 1.4 %collective-permute-start.19 = (f32[2,8,96]{2,1,0:T(8,128)S(1)}, f32[2,8,96]{2,1,0:T(8,128)S(1)}, u32[]{:S(2)}, u32[]{:S(2)}) collective-permute-start(f32[2,8,96]{2,1,0:T(8,128)S(1)} %get-tuple-element.36), channel_id=1, source_target_pairs={{0,1},{1,0},{2,3},{3,2},{4,5},{5,4},{6,7},{7,6},{8,9},{9,8},{10,11... | collective-permute-start | bytes 18440 | tf_op jit(solution)/shard_map/ppermute | solution.py:570
  61.3 2.8 %collective-permute-start.20 = (f32[2,8,96]{2,1,0:T(8,128)S(1)}, f32[2,8,96]{2,1,0:T(8,128)S(1)}, u32[]{:S(2)}, u32[]{:S(2)}) collective-permute-start(f32[2,8,96]{2,1,0:T(8,128)S(1)} %add.6), channel_id=1, source_target_pairs={{0,4},{4,0},{8,12},{12,8},{1,5},{5,1},{9,13},{13,9},{2,6},{6,2},{1... | collective-permute-start | bytes 18440 | tf_op jit(solution)/shard_map/ppermute | solution.py:576
  64.1 2.9 %collective-permute-start.21 = (f32[2,8,96]{2,1,0:T(8,128)S(1)}, f32[2,8,96]{2,1,0:T(8,128)S(1)}, u32[]{:S(2)}, u32[]{:S(2)}) collective-permute-start(f32[2,8,96]{2,1,0:T(8,128)S(1)} %add.7), channel_id=1, source_target_pairs={{0,2},{2,0},{4,6},{6,4},{8,10},{10,8},{12,14},{14,12},{1,3},{3,1},... | collective-permute-start | bytes 18440 | tf_op jit(solution)/shard_map/ppermute | solution.py:583
  65.3 4.3 %collective-permute-start.22 = (f32[2,8,96]{2,1,0:T(8,128)S(1)}, f32[2,8,96]{2,1,0:T(8,128)S(1)}, u32[]{:S(2)}, u32[]{:S(2)}) collective-permute-start(f32[2,8,96]{2,1,0:T(8,128)S(1)} %add.7), channel_id=1, source_target_pairs={{0,10},{2,8},{4,14},{6,12},{8,2},{10,0},{12,6},{14,4},{1,11},{3,9}... | collective-permute-start | bytes 18440 | tf_op jit(solution)/shard_map/ppermute | solution.py:583
  71.7 5.5 %collective-permute-start.28 = (bf16[96,1024]{1,0:T(8,128)(2,1)S(1)}, bf16[96,1024]{1,0:T(8,128)(2,1)S(1)}, u32[]{:S(2)}, u32[]{:S(2)}) collective-permute-start(bf16[96,1024]{1,0:T(8,128)(2,1)S(1)} %get-tuple-element.40.refs_0_), channel_id=1, source_target_pairs={{0,4},{4,12},{12,8},{8,0},{1,5},{5,13},{13,9},{9,1},{2,6},{6,14},{... | collective-permute-start | bytes 589832 | tf_op jit(solution)/shard_map/ppermute | solution.py:565
  75.0 7.9 %collective-permute-start.24 = (bf16[96,1024]{1,0:T(8,128)(2,1)S(1)}, bf16[96,1024]{1,0:T(8,128)(2,1)S(1)}, u32[]{:S(2)}, u32[]{:S(2)}) collective-permute-start(bf16[96,1024]{1,0:T(8,128)(2,1)S(1)} %gate.7.refs_1_), channel_id=1, source_target_pairs={{0,4},{4,12},{12,8},{8,0},{1,5},{5,13},{13,9},{9,1},{2,6},{6,14},{... | collective-permute-start | bytes 589832 | tf_op jit(solution)/shard_map/ppermute | solution.py:565
  77.2 10.4 %collective-permute-start.29 = (bf16[96,1024]{1,0:T(8,128)(2,1)S(1)}, bf16[96,1024]{1,0:T(8,128)(2,1)S(1)}, u32[]{:S(2)}, u32[]{:S(2)}) collective-permute-start(bf16[96,1024]{1,0:T(8,128)(2,1)S(1)} %collective-permute-done.28.refs_0_), channel_id=1, source_target_pairs={{0,4},{4,12},{12,8},{8,0},{1,5},{5,13},{13,9},{9,1},{2,6},{6,14},{... | collective-permute-start | bytes 589832 | tf_op jit(solution)/shard_map/ppermute | solution.py:565
  82.9 8.2 %collective-permute-start.25 = (bf16[96,1024]{1,0:T(8,128)(2,1)S(1)}, bf16[96,1024]{1,0:T(8,128)(2,1)S(1)}, u32[]{:S(2)}, u32[]{:S(2)}) collective-permute-start(bf16[96,1024]{1,0:T(8,128)(2,1)S(1)} %collective-permute-done.24.refs_1_), channel_id=1, source_target_pairs={{0,4},{4,12},{12,8},{8,0},{1,5},{5,13},{13,9},{9,1},{2,6},{6,14},{... | collective-permute-start | bytes 589832 | tf_op jit(solution)/shard_map/ppermute | solution.py:565
  82.9 8.2 %collective-permute-start.35 = (bf16[96,1024]{1,0:T(8,128)(2,1)S(1)}, bf16[96,1024]{1,0:T(8,128)(2,1)S(1)}, u32[]{:S(2)}, u32[]{:S(2)}) collective-permute-start(bf16[96,1024]{1,0:T(8,128)(2,1)S(1)} %gate.7.refs_1_), channel_id=1, source_target_pairs={{0,1},{1,0},{2,3},{3,2},{4,5},{5,4},{6,7},{7,6},{8,9},{9,8},{10,11... | collective-permute-start | bytes 589832 | tf_op jit(solution)/shard_map/ppermute | solution.py:570
  87.1 8.3 %collective-permute-start.34 = (bf16[96,1024]{1,0:T(8,128)(2,1)S(1)}, bf16[96,1024]{1,0:T(8,128)(2,1)S(1)}, u32[]{:S(2)}, u32[]{:S(2)}) collective-permute-start(bf16[96,1024]{1,0:T(8,128)(2,1)S(1)} %get-tuple-element.40.refs_0_), channel_id=1, source_target_pairs={{0,1},{1,0},{2,3},{3,2},{4,5},{5,4},{6,7},{7,6},{8,9},{9,8},{10,11... | collective-permute-start | bytes 589832 | tf_op jit(solution)/shard_map/ppermute | solution.py:570
  87.1 8.4 %collective-permute-start.33 = (bf16[96,1024]{1,0:T(8,128)(2,1)S(1)}, bf16[96,1024]{1,0:T(8,128)(2,1)S(1)}, u32[]{:S(2)}, u32[]{:S(2)}) collective-permute-start(bf16[96,1024]{1,0:T(8,128)(2,1)S(1)} %collective-permute-done.24.refs_1_), channel_id=1, source_target_pairs={{0,1},{1,0},{2,3},{3,2},{4,5},{5,4},{6,7},{7,6},{8,9},{9,8},{10,11... | collective-permute-start | bytes 589832 | tf_op jit(solution)/shard_map/ppermute | solution.py:570
  87.6 8.3 %collective-permute-start.36 = (bf16[96,1024]{1,0:T(8,128)(2,1)S(1)}, bf16[96,1024]{1,0:T(8,128)(2,1)S(1)}, u32[]{:S(2)}, u32[]{:S(2)}) collective-permute-start(bf16[96,1024]{1,0:T(8,128)(2,1)S(1)} %collective-permute-done.29.refs_0_), channel_id=1, source_target_pairs={{0,4},{4,12},{12,8},{8,0},{1,5},{5,13},{13,9},{9,1},{2,6},{6,14},{... | collective-permute-start | bytes 589832 | tf_op jit(solution)/shard_map/ppermute | solution.py:565
  91.1 10.5 %collective-permute-start.26 = (bf16[96,1024]{1,0:T(8,128)(2,1)S(1)}, bf16[96,1024]{1,0:T(8,128)(2,1)S(1)}, u32[]{:S(2)}, u32[]{:S(2)}) collective-permute-start(bf16[96,1024]{1,0:T(8,128)(2,1)S(1)} %collective-permute-done.25.refs_1_), channel_id=1, source_target_pairs={{0,4},{4,12},{12,8},{8,0},{1,5},{5,13},{13,9},{9,1},{2,6},{6,14},{... | collective-permute-start | bytes 589832 | tf_op jit(solution)/shard_map/ppermute | solution.py:565
  91.1 11.0 %collective-permute-start.32 = (bf16[96,1024]{1,0:T(8,128)(2,1)S(1)}, bf16[96,1024]{1,0:T(8,128)(2,1)S(1)}, u32[]{:S(2)}, u32[]{:S(2)}) collective-permute-start(bf16[96,1024]{1,0:T(8,128)(2,1)S(1)} %collective-permute-done.28.refs_0_), channel_id=1, source_target_pairs={{0,1},{1,0},{2,3},{3,2},{4,5},{5,4},{6,7},{7,6},{8,9},{9,8},{10,11... | collective-permute-start | bytes 589832 | tf_op jit(solution)/shard_map/ppermute | solution.py:570
  95.5 8.2 %collective-permute-start.31 = (bf16[96,1024]{1,0:T(8,128)(2,1)S(1)}, bf16[96,1024]{1,0:T(8,128)(2,1)S(1)}, u32[]{:S(2)}, u32[]{:S(2)}) collective-permute-start(bf16[96,1024]{1,0:T(8,128)(2,1)S(1)} %collective-permute-done.25.refs_1_), channel_id=1, source_target_pairs={{0,1},{1,0},{2,3},{3,2},{4,5},{5,4},{6,7},{7,6},{8,9},{9,8},{10,11... | collective-permute-start | bytes 589832 | tf_op jit(solution)/shard_map/ppermute | solution.py:570
  95.5 8.2 %collective-permute-start.30 = (bf16[96,1024]{1,0:T(8,128)(2,1)S(1)}, bf16[96,1024]{1,0:T(8,128)(2,1)S(1)}, u32[]{:S(2)}, u32[]{:S(2)}) collective-permute-start(bf16[96,1024]{1,0:T(8,128)(2,1)S(1)} %collective-permute-done.29.refs_0_), channel_id=1, source_target_pairs={{0,1},{1,0},{2,3},{3,2},{4,5},{5,4},{6,7},{7,6},{8,9},{9,8},{10,11... | collective-permute-start | bytes 589832 | tf_op jit(solution)/shard_map/ppermute | solution.py:570
  96.0 11.4 %collective-permute-start.37 = (bf16[96,1024]{1,0:T(8,128)(2,1)S(1)}, bf16[96,1024]{1,0:T(8,128)(2,1)S(1)}, u32[]{:S(2)}, u32[]{:S(2)}) collective-permute-start(bf16[96,1024]{1,0:T(8,128)(2,1)S(1)} %collective-permute-done.36.refs_0_), channel_id=1, source_target_pairs={{0,1},{1,0},{2,3},{3,2},{4,5},{5,4},{6,7},{7,6},{8,9},{9,8},{10,11... | collective-permute-start | bytes 589832 | tf_op jit(solution)/shard_map/ppermute | solution.py:570
  101.6 6.9 %collective-permute-start.27 = (bf16[96,1024]{1,0:T(8,128)(2,1)S(1)}, bf16[96,1024]{1,0:T(8,128)(2,1)S(1)}, u32[]{:S(2)}, u32[]{:S(2)}) collective-permute-start(bf16[96,1024]{1,0:T(8,128)(2,1)S(1)} %collective-permute-done.26.refs_0_), channel_id=1, source_target_pairs={{0,1},{1,0},{2,3},{3,2},{4,5},{5,4},{6,7},{7,6},{8,9},{9,8},{10,11... | collective-permute-start | bytes 589832 | tf_op jit(solution)/shard_map/ppermute | solution.py:570

commit v4 on v3

--- a/solution.py
+++ b/solution.py
@@ -66,11 +66,10 @@
     return jnp.broadcast_to(values[m : m + 1, :], (SUB, values.shape[1]))
 
 
-def half_states(side, wide, per_chunk, slot_total, meta, first_span, fetch, held_rows, rates_ref, states):
+def half_states(offset, wide, per_chunk, slot_total, meta, first_span, fetch, held_rows, rates_ref, states):
     slots, rows, half = held_rows.shape
     modes = rates_ref.shape[0]
     rank = meta[0]
-    part = 1 - rank if side == 0 else rank
 
     def one_tile(t, carry):
         @pl.when(lax.rem(t, per_chunk) == 0)
@@ -78,7 +77,7 @@
             fetch(t // per_chunk).wait()
 
         at = pl.ds(pl.multiple_of(t * wide, LANES), wide)
-        rates = rates_ref[:, pl.ds(pl.multiple_of(part * half + t * wide, LANES), wide)]
+        rates = rates_ref[:, pl.ds(pl.multiple_of(offset + t * wide, LANES), wide)]
         decay = jnp.exp(-rates)
         groups = [decay[g : g + SUB, :] for g in range(0, modes, SUB)]
         held = [[jnp.zeros((SUB, wide), f32) for _ in groups] for _ in range(slots)]
@@ -103,6 +102,10 @@
     lax.fori_loop(0, half // wide, one_tile, 0)
 
 
+def early_rows(weight):
+    return weight.shape[0] // 16 * 10
+
+
 def tile_sizes(half):
     chunk = 512 if half % 512 == 0 else LANES
     return chunk, 2 * LANES if chunk % (2 * LANES) == 0 else LANES
@@ -122,15 +125,15 @@
     return fetch
 
 
-def open_body(pieces, sizes, slot_total, meta, span_any, ids_any, table, cache, rates_any, weight, *rest):
-    x_out, sums_out, states, weight_out = rest[:4]
-    ids, span_here, words, rows_buf, held_rows, rates_ref, sems, slot_sems = rest[4:]
+def open_body(pieces, sizes, slot_total, meta, span_any, ids_any, table, cache, rates_any, resid_any, weight, *rest):
+    x_out, sums_out, states, rates_out, resid_out, weight_out = rest[:6]
+    ids, span_here, words, rows_buf, held_rows, rates_ref, sems, slot_sems = rest[6:]
     chunk, wide = sizes
     spans, rows = sums_out.shape[0], sums_out.shape[2]
     half = x_out.shape[2]
     width = words.shape[1]
     depth = words.shape[0] // pieces
-    deep = weight.shape[0] // 2
+    deep = early_rows(weight)
     fetch = slot_fetch(0, chunk, meta, cache, held_rows, slot_sems)
     small = [
         pltpu.make_async_copy(span_any, span_here, sems.at[pieces]),
@@ -143,6 +146,8 @@
         for c in range(pieces)
     ]
     copies.append(pltpu.make_async_copy(ids_any, ids, sems.at[pieces + 2]))
+    own = pl.ds(pl.multiple_of(meta[0] * half, LANES), half)
+    copies.append(pltpu.make_async_copy(resid_any.at[:, own], resid_out, sems.at[pieces + 4]))
     weight_copy = pltpu.make_async_copy(
         weight.at[pl.ds(0, deep), :], weight_out.at[pl.ds(0, deep), :], sems.at[pieces + 3]
     )
@@ -156,8 +161,10 @@
     for copy in small:
         copy.wait()
     first_span = lax.rem(span_here[0], slot_total)
+    rates_out[...] = rates_ref[:, own]
     half_states(
-        0, wide, chunk // wide, slot_total, meta, first_span, fetch, held_rows, rates_ref, states
+        (1 - meta[0]) * half, wide, chunk // wide, slot_total, meta, first_span, fetch, held_rows,
+        rates_ref, states,
     )
     for copy in copies:
         copy.wait()
@@ -178,7 +185,7 @@
     weight_copy.wait()
 
 
-def open_step(meta, first, ids, table, cache, rates, weight, slot_total):
+def open_step(meta, first, ids, table, cache, rates, resid, weight, slot_total):
     spans, rows = ids.shape
     words, width = table.shape
     slots = cache.shape[0]
@@ -193,10 +200,12 @@
             jax.ShapeDtypeStruct((spans, rows, half), f32),
             jax.ShapeDtypeStruct((spans, SUB, rows), f32),
             jax.ShapeDtypeStruct((2, modes, half), f32),
+            jax.ShapeDtypeStruct((modes, half), f32),
+            jax.ShapeDtypeStruct((modes, half), f32),
             pltpu.VMEM(weight.shape, weight.dtype),
         ),
-        in_specs=[pl.BlockSpec(memory_space=pltpu.SMEM)] + [anywhere] * 6,
-        out_specs=(vmem,) * 4,
+        in_specs=[pl.BlockSpec(memory_space=pltpu.SMEM)] + [anywhere] * 7,
+        out_specs=(vmem,) * 6,
         scratch_shapes=[
             pltpu.SMEM((spans, rows), jnp.int32),
             pltpu.SMEM((1,), jnp.int32),
@@ -204,68 +213,61 @@
             pltpu.VMEM((rows, width), f32),
             pltpu.VMEM((slots, rows, half), f32),
             pltpu.VMEM((modes, width), f32),
-            pltpu.SemaphoreType.DMA((pieces + 4,)),
+            pltpu.SemaphoreType.DMA((pieces + 5,)),
             pltpu.SemaphoreType.DMA((half // sizes[0],)),
         ],
         compiler_params=params(10),
         cost_estimate=cost(2 * slots * rows * modes * half, 4 * words * width),
         name="open_step",
-    )(meta, first, in_hbm(ids), in_hbm(table), in_hbm(cache), in_hbm(rates), in_hbm(weight))
-
-
-def history_body(sizes, slot_total, meta, span_any, cache, rates_any, resid_any, weight, held_weight, *rest):
+    )(
+        meta, first, in_hbm(ids), in_hbm(table), in_hbm(cache), in_hbm(rates), in_hbm(resid),
+        in_hbm(weight),
+    )
+
+
+def history_body(sizes, slot_total, meta, span_any, cache, rates_ref, resid_ref, weight, held_weight, *rest):
     del held_weight
-    states, taps, rates_out, resid_out, weight_out = rest[:5]
-    span_here, held_rows, rates_ref, resid_ref, sems, slot_sems = rest[5:]
+    states, taps, weight_out = rest[:3]
+    span_here, held_rows, sems, slot_sems = rest[3:]
     chunk, wide = sizes
     _, rows, half = held_rows.shape
     modes = rates_ref.shape[0]
-    rank = meta[0]
-    deep = weight.shape[0] // 2
+    deep = early_rows(weight)
+    later = weight.shape[0] - deep
     fetch = slot_fetch(1, chunk, meta, cache, held_rows, slot_sems)
-    small = [
-        pltpu.make_async_copy(span_any, span_here, sems.at[0]),
-        pltpu.make_async_copy(rates_any, rates_ref, sems.at[1]),
-        pltpu.make_async_copy(resid_any, resid_ref, sems.at[2]),
-    ]
+    span_copy = pltpu.make_async_copy(span_any, span_here, sems.at[0])
     weight_copy = pltpu.make_async_copy(
-        weight.at[pl.ds(deep, deep), :], weight_out.at[pl.ds(deep, deep), :], sems.at[3]
-    )
-    for copy in small:
-        copy.start()
+        weight.at[pl.ds(deep, later), :], weight_out.at[pl.ds(deep, later), :], sems.at[1]
+    )
+    span_copy.start()
     for j in range(half // chunk):
         fetch(j).start()
     weight_copy.start()
-    for copy in small:
-        copy.wait()
-    own = pl.ds(pl.multiple_of(rank * half, LANES), half)
-    rates_out[...] = rates_ref[:, own]
-    resid_out[...] = resid_ref[:, own]
 
     def tap_tile(t, carry):
-        at = pl.ds(pl.multiple_of(rank * half + t * LANES, LANES), LANES)
-        out_at = pl.ds(pl.multiple_of(t * LANES, LANES), LANES)
+        at = pl.ds(pl.multiple_of(t * LANES, LANES), LANES)
         rates, resid = rates_ref[:, at], resid_ref[:, at]
         place = lax.broadcasted_iota(jnp.int32, (SUB, LANES), 0).astype(f32)
         step8 = jnp.exp(-rates * float(SUB))
         first = [spread(resid, m) * jnp.exp(-spread(rates, m) * place) for m in range(modes)]
 
         def store(k, value):
-            taps[k * SUB : (k + 1) * SUB, out_at] = value
+            taps[k * SUB : (k + 1) * SUB, at] = value
 
         mode_rows(first, [spread(step8, m) for m in range(modes)], rows, store)
         return carry
 
     lax.fori_loop(0, half // LANES, tap_tile, 0)
+    span_copy.wait()
     first_span = lax.rem(span_here[0], slot_total)
     half_states(
-        1, wide, chunk // wide, slot_total, meta, first_span, fetch, held_rows, rates_ref, states
+        0, wide, chunk // wide, slot_total, meta, first_span, fetch, held_rows, rates_ref, states
     )
     weight_copy.wait()
 
 
 def history_states(meta, first, cache, rates, resid, weight, held_weight, slot_total):
-    slots, rows, width = cache.shape
+    slots, rows, _ = cache.shape
     modes = rates.shape[0]
     half = weight.shape[1]
     sizes = tile_sizes(half)
@@ -275,27 +277,25 @@
         out_shape=(
             jax.ShapeDtypeStruct((2, modes, half), f32),
             jax.ShapeDtypeStruct((rows, half), f32),
-            jax.ShapeDtypeStruct((modes, half), f32),
-            jax.ShapeDtypeStruct((modes, half), f32),
             pltpu.VMEM(weight.shape, weight.dtype),
         ),
-        in_specs=[pl.BlockSpec(memory_space=pltpu.SMEM)] + [anywhere] * 6,
-        out_specs=(vmem,) * 5,
+        in_specs=[pl.BlockSpec(memory_space=pltpu.SMEM)]
+        + [anywhere] * 2
+        + [vmem] * 2
+        + [anywhere] * 2,
+        out_specs=(vmem,) * 3,
         scratch_shapes=[
             pltpu.SMEM((1,), jnp.int32),
             pltpu.VMEM((slots, rows, half), f32),
-            pltpu.VMEM((modes, width), f32),
-            pltpu.VMEM((modes, width), f32),
-            pltpu.SemaphoreType.DMA((4,)),
+            pltpu.SemaphoreType.DMA((2,)),
             pltpu.SemaphoreType.DMA((half // sizes[0],)),
         ],
-        input_output_aliases={6: 4},
+        input_output_aliases={6: 2},
         compiler_params=params(6),
         cost_estimate=cost(2 * slots * rows * modes * half, 4 * slots * rows * half),
         name="history_states",
     )(
-        meta, first, in_hbm(cache), in_hbm(rates), in_hbm(resid), in_hbm(weight),
-        in_vmem(held_weight),
+        meta, first, in_hbm(cache), rates, resid, in_hbm(weight), in_vmem(held_weight),
     )
 
 
@@ -585,8 +585,8 @@
     is_first = (section_rank == 0).astype(jnp.int32)
     meta = jnp.stack([seq_rank, is_first, tensor_rank]).astype(jnp.int32)
 
-    base, sums, for_partner, held_weight = open_step(
-        meta, leading_span_index, token_ids, embed_table, cache, rates, weight, slot_total
+    base, sums, for_partner, *modes_here, held_weight = open_step(
+        meta, leading_span_index, token_ids, embed_table, cache, rates, resid, weight, slot_total
     )
     small_ring = ring_fits(tensors)
     first_sums = [sums]
@@ -596,8 +596,8 @@
     else:
         first_sums = [lax.psum(sums, "tensor")]
     partner = swapped(for_partner)
-    states, taps, *modes_here, weight = history_states(
-        meta, leading_span_index, cache, rates, resid, weight, held_weight, slot_total
+    states, taps, weight = history_states(
+        meta, leading_span_index, cache, *modes_here, weight, held_weight, slot_total
     )
 
     every = tuple(range(spans))

time: 111 us -> 110 us (level)
  transfers between devices with their start and end apart: 38 -> 38, of which waited for: 12 -> 12; matrix products, arithmetic and copies ran while one was open for 0% -> 0% of each run, Pallas kernels for 28% -> 27%
where the time goes in v4:
time: 110 us
  Pallas kernels  40.7 us (37%)
  starting transfers between devices  39.1 us (36%)
  waiting for transfers between devices  28.6 us (26%)
  between operations  1.11 us (1%)
    ppermute x18, starting transfers between devices, swapped(): return lax.ppermute(value, 'seq', [(i, seqs - 1 - i) for i in range(seqs)])  25 us
    ppermute x15, waiting for transfers between devices, along_ring(): lax.ppermute(value, 'tensor', [(order[i], order[(i + shift) % tensors]) f...  21.1 us
    pallas_call x14, Pallas kernels, mix(): pl.pallas_call(functools.partial(mix_body, kind, chosen, counts, out_tile...  19 us
    pallas_call x4, Pallas kernels, gate(): pl.pallas_call(functools.partial(gate_body, weight.shape[0], span, counts...  11.2 us
    ppermute x15, starting transfers between devices, along_ring(): lax.ppermute(value, 'tensor', [(order[i], order[(i + shift) % tensors]) f...  11 us
    pallas_call x1, Pallas kernels, open_step(): pl.pallas_call(functools.partial(open_body, pieces, sizes, slot_total), o...  6.68 us
    ppermute x2, waiting for transfers between devices, to_next_across(): return lax.ppermute(value, ('tensor', 'section'), route)  3.89 us
    pallas_call x1, Pallas kernels, history_states(): pl.pallas_call(functools.partial(history_body, sizes, slot_total), out_sh...  3.87 us
  transfers between devices with their start and end apart: 38, of which 12 were waited for; matrix products, arithmetic and copies ran while one was open for 0% of the time, Pallas kernels for 27%

profile of v4, /device:TPU:1, one launch (start us, length us, event | category | flops | bytes accessed | tf_op | source)
XLA Modules:
  0.0 109.6 jit_solution(18077740022503561950)
XLA Ops:
  0.7 6.7 %open_step.1 = (f32[2,96,1024]{2,1,0:T(8,128)S(1)}, f32[2,8,96]{2,1,0:T(8,128)S(1)}, f32[2,16,1024]{2,1,0:T(8,128)S(1)}, f32[16,1024]{1,0:T(8,128)S(1)}, f32[16,...) custom-call(s32[3]{0:T(128)S(1)} %pad_add_fusion.meta, s32[1]{0:T(128)S(6)} %copy.11.span_any, s32[2,96]{1,0:T(2,128)} %ids_any.1, ...), custom_call_target="tpu_custom_call" | custom-call | flops 12582912 | bytes 4194304 | tf_op jit(solution)/shard_map/open_step/pallas_call | solution.py:197
  7.5 2.7 %collective-permute-start.1 = (f32[2,8,96]{2,1,0:T(8,128)S(1)}, f32[2,8,96]{2,1,0:T(8,128)S(1)}, u32[]{:S(2)}, u32[]{:S(2)}) collective-permute-start(f32[2,8,96]{2,1,0:T(8,128)S(1)} %get-tuple-element.31.rest_7_.rest_8_), channel_id=1, source_target_pairs={{0,4},{4,12},{12,8},{8,0},{1,5},{5,13},{13,9},{9,1},{2,6},{6,14},{... | collective-permute-start | bytes 18440 | tf_op jit(solution)/shard_map/ppermute | solution.py:565
  10.2 2.2 %collective-permute-start.2 = (f32[2,8,96]{2,1,0:T(8,128)S(1)}, f32[2,8,96]{2,1,0:T(8,128)S(1)}, u32[]{:S(2)}, u32[]{:S(2)}) collective-permute-start(f32[2,8,96]{2,1,0:T(8,128)S(1)} %get-tuple-element.31.rest_7_.rest_8_), channel_id=1, source_target_pairs={{0,12},{4,8},{12,0},{8,4},{1,13},{5,9},{13,1},{9,5},{2,14},{6,10},... | collective-permute-start | bytes 18440 | tf_op jit(solution)/shard_map/ppermute | solution.py:565
  12.4 1.3 %collective-permute-start.3 = (f32[2,8,96]{2,1,0:T(8,128)S(1)}, f32[2,8,96]{2,1,0:T(8,128)S(1)}, u32[]{:S(2)}, u32[]{:S(2)}) collective-permute-start(f32[2,8,96]{2,1,0:T(8,128)S(1)} %get-tuple-element.31.rest_7_.rest_8_), channel_id=1, source_target_pairs={{0,8},{4,0},{12,4},{8,12},{1,9},{5,1},{13,5},{9,13},{2,10},{6,2},{... | collective-permute-start | bytes 18440 | tf_op jit(solution)/shard_map/ppermute | solution.py:565
  13.7 3.9 %history_states.1 = (f32[2,16,1024]{2,1,0:T(8,128)S(1)}, f32[96,1024]{1,0:T(8,128)S(1)}, bf16[8192,1024]{1,0:T(8,128)(2,1)S(1)}) custom-call(s32[3]{0:T(128)S(1)} %pad_add_fusion.meta, s32[1]{0:T(128)S(6)} %copy.11.span_any, f32[4,96,2048]{2,1,0:T(8,128)} %bitcast.10, ...), custom_call_target="tpu_custom_call", output_to_operand_aliasing={{2}: (6, {})} | custom-call | flops 12582912 | bytes 1572864 | tf_op jit(solution)/shard_map/history_states/pallas_call | solution.py:275
  17.6 2.7 %gate.4 = (bf16[96,1024]{1,0:T(8,128)(2,1)S(1)}, f32[96,1024]{1,0:T(8,128)S(1)}, f32[96,1024]{1,0:T(8,128)S(1)}) custom-call(s32[3]{0:T(128)S(1)} %pad_add_fusion.meta, f32[2,96,1024]{2,1,0:T(8,128)S(1)} %get-tuple-element.23.base.refs_3_, f32[1,2048]{1,0:T(1,128)S(1)} %copy-done, f32[16,1024]{1,0:T(8,128)S(1)} %get-tuple-element.24.rates_ref.rest_1_.rest_2_, ...), custom_call_target="tpu_custom_call" | custom-call | flops 15728640 | bytes 1179648 | tf_op jit(solution)/shard_map/gate/pallas_call | solution.py:418
  20.5 3.1 %gate.5.refs_1_ = bf16[96,1024]{1,0:T(8,128)(2,1)S(1)} custom-call(s32[3]{0:T(128)S(1)} %pad_add_fusion.meta, f32[2,96,1024]{2,1,0:T(8,128)S(1)} %get-tuple-element.23.base.refs_3_, f32[1,2048]{1,0:T(1,128)S(1)} %copy-done, f32[16,1024]{1,0:T(8,128)S(1)} %get-tuple-element.24.rates_ref.rest_1_.rest_2_, ...), custom_call_target="tpu_custom_call" | custom-call | flops 15728640 | bytes 1179648 | tf_op jit(solution)/shard_map/gate/pallas_call | solution.py:418
  23.6 1.1 collective-permute-start.4
  24.7 2.1 %collective-permute-done.8.refs_0_ = bf16[96,1024]{1,0:T(8,128)(2,1)S(1)} collective-permute-done((bf16[96,1024]{1,0:T(8,128)(2,1)S(1)}, bf16[96,1024]{1,0:T(8,128)(2,1)S(1)}, u32[]{:S(2)}, u32[]{:S(2)}) %collective-permute-start.8) | collective-permute-done | bytes 196640 | tf_op jit(solution)/shard_map/ppermute | solution.py:565
  26.8 4.7 %collective-permute-done.4.refs_1_ = bf16[96,1024]{1,0:T(8,128)(2,1)S(1)} collective-permute-done((bf16[96,1024]{1,0:T(8,128)(2,1)S(1)}, bf16[96,1024]{1,0:T(8,128)(2,1)S(1)}, u32[]{:S(2)}, u32[]{:S(2)}) %collective-permute-start.4) | collective-permute-done | bytes 196640 | tf_op jit(solution)/shard_map/ppermute | solution.py:565
  31.5 2.2 %collective-permute-start.15 = (bf16[96,1024]{1,0:T(8,128)(2,1)S(1)}, bf16[96,1024]{1,0:T(8,128)(2,1)S(1)}, u32[]{:S(2)}, u32[]{:S(2)}) collective-permute-start(bf16[96,1024]{1,0:T(8,128)(2,1)S(1)} %gate.5.refs_1_), channel_id=1, source_target_pairs={{0,1},{1,0},{2,3},{3,2},{4,5},{5,4},{6,7},{7,6},{8,9},{9,8},{10,11... | collective-permute-start | bytes 589832 | tf_op jit(solution)/shard_map/ppermute | solution.py:570
  34.2 1.3 %collective-permute-done.9.refs_0_ = bf16[96,1024]{1,0:T(8,128)(2,1)S(1)} collective-permute-done((bf16[96,1024]{1,0:T(8,128)(2,1)S(1)}, bf16[96,1024]{1,0:T(8,128)(2,1)S(1)}, u32[]{:S(2)}, u32[]{:S(2)}) %collective-permute-start.9) | collective-permute-done | bytes 196640 | tf_op jit(solution)/shard_map/ppermute | solution.py:565
  36.0 3.7 %collective-permute-done.5.refs_1_ = bf16[96,1024]{1,0:T(8,128)(2,1)S(1)} collective-permute-done((bf16[96,1024]{1,0:T(8,128)(2,1)S(1)}, bf16[96,1024]{1,0:T(8,128)(2,1)S(1)}, u32[]{:S(2)}, u32[]{:S(2)}) %collective-permute-start.5) | collective-permute-done | bytes 196640 | tf_op jit(solution)/shard_map/ppermute | solution.py:565
  39.7 2.6 %collective-permute-start.12 = (bf16[96,1024]{1,0:T(8,128)(2,1)S(1)}, bf16[96,1024]{1,0:T(8,128)(2,1)S(1)}, u32[]{:S(2)}, u32[]{:S(2)}) collective-permute-start(bf16[96,1024]{1,0:T(8,128)(2,1)S(1)} %collective-permute-done.8.refs_0_), channel_id=1, source_target_pairs={{0,1},{1,0},{2,3},{3,2},{4,5},{5,4},{6,7},{7,6},{8,9},{9,8},{10,11... | collective-permute-start | bytes 589832 | tf_op jit(solution)/shard_map/ppermute | solution.py:570
  42.8 0.8 collective-permute-done.16.refs_0_
  43.7 3.1 %collective-permute-start.17 = (bf16[96,1024]{1,0:T(8,128)(2,1)S(1)}, bf16[96,1024]{1,0:T(8,128)(2,1)S(1)}, u32[]{:S(2)}, u32[]{:S(2)}) collective-permute-start(bf16[96,1024]{1,0:T(8,128)(2,1)S(1)} %collective-permute-done.16.refs_0_), channel_id=1, source_target_pairs={{0,1},{1,0},{2,3},{3,2},{4,5},{5,4},{6,7},{7,6},{8,9},{9,8},{10,11... | collective-permute-start | bytes 589832 | tf_op jit(solution)/shard_map/ppermute | solution.py:570
  46.8 1.6 %shard_map.82.refs_5_ = f32[192,1024]{1,0:T(8,128)S(1)} custom-call(s32[3]{0:T(128)S(1)} %pad_add_fusion.meta, bf16[96,1024]{1,0:T(8,128)(2,1)S(1)} %get-tuple-element.33.refs_0_, bf16[96,1024]{1,0:T(8,128)(2,1)S(1)} %gate.5.refs_1_, bf16[96,1024]{1,0:T(8,128)(2,1)S(1)} %collective-permute-done.14.refs_2_, ...), custom_call_target="tpu_custom_call" | custom-call | flops 805306368 | bytes 4194304 | tf_op jit(solution)/shard_map/pallas_call | solution.py:530
  48.3 1.3 %collective-permute-start.7 = (bf16[96,1024]{1,0:T(8,128)(2,1)S(1)}, bf16[96,1024]{1,0:T(8,128)(2,1)S(1)}, u32[]{:S(2)}, u32[]{:S(2)}) collective-permute-start(bf16[96,1024]{1,0:T(8,128)(2,1)S(1)} %collective-permute-done.6.refs_0_), channel_id=1, source_target_pairs={{0,1},{1,0},{2,3},{3,2},{4,5},{5,4},{6,7},{7,6},{8,9},{9,8},{10,11... | collective-permute-start | bytes 589832 | tf_op jit(solution)/shard_map/ppermute | solution.py:570
  49.6 1.6 %shard_map.83.refs_5_ = f32[192,1024]{1,0:T(8,128)S(1)} custom-call(s32[3]{0:T(128)S(1)} %pad_add_fusion.meta, bf16[96,1024]{1,0:T(8,128)(2,1)S(1)} %collective-permute-done.8.refs_0_, bf16[96,1024]{1,0:T(8,128)(2,1)S(1)} %collective-permute-done.4.refs_1_, bf16[96,1024]{1,0:T(8,128)(2,1)S(1)} %collective-permute-done.12.refs_2_, ...), custom_call_target="tpu_custom_call" | custom-call | flops 805306368 | bytes 4194304 | tf_op jit(solution)/shard_map/pallas_call | solution.py:530
  51.2 1.6 %shard_map.84.refs_2_ = f32[192,1024]{1,0:T(8,128)S(1)} custom-call(s32[3]{0:T(128)S(1)} %pad_add_fusion.meta, bf16[96,1024]{1,0:T(8,128)(2,1)S(1)} %collective-permute-done.9.refs_0_, bf16[96,1024]{1,0:T(8,128)(2,1)S(1)} %collective-permute-done.5.refs_1_, bf16[96,1024]{1,0:T(8,128)(2,1)S(1)} %collective-permute-done.10.refs_2_, ...), custom_call_target="tpu_custom_call" | custom-call | flops 805306368 | bytes 4194304 | tf_op jit(solution)/shard_map/pallas_call | solution.py:530
  52.8 1.0 shard_map.86.refs_2_
  53.8 1.3 %shard_map.87 = (bf16[96,1024]{1,0:T(8,128)(2,1)S(1)}, f32[2,8,96]{2,1,0:T(8,128)S(1)}) custom-call(s32[3]{0:T(128)S(1)} %pad_add_fusion.meta, bf16[96,1024]{1,0:T(8,128)(2,1)S(1)} %collective-permute-done.17.refs_0_, bf16[8192,1024]{1,0:T(8,128)(2,1)S(1)} %get-tuple-element.30.rest_6_.refs_4_.refs_1_.rest_7_, f32[96,1024]{1,0:T(8,128)S(1)} %shard_map.86.refs_2_, ...), custom_call_target="tpu_custom_call" | custom-call | flops 201326592 | bytes 2097152 | tf_op jit(solution)/shard_map/pallas_call | solution.py:530
  55.2 1.2 %collective-permute-start.23 = (bf16[96,1024]{1,0:T(8,128)(2,1)S(1)}, bf16[96,1024]{1,0:T(8,128)(2,1)S(1)}, u32[]{:S(2)}, u32[]{:S(2)}) collective-permute-start(bf16[96,1024]{1,0:T(8,128)(2,1)S(1)} %get-tuple-element.37), channel_id=1, source_target_pairs={{0,2},{2,0},{1,3},{3,1},{4,6},{6,4},{5,7},{7,5},{8,10},{10,8},{9,1... | collective-permute-start | bytes 589832 | tf_op jit(solution)/shard_map/ppermute | solution.py:573
  56.4 1.0 shard_map.85.refs_2_
  57.5 1.3 %shard_map.88 = (bf16[96,1024]{1,0:T(8,128)(2,1)S(1)}, f32[2,8,96]{2,1,0:T(8,128)S(1)}) custom-call(s32[3]{0:T(128)S(1)} %pad_add_fusion.meta, bf16[96,1024]{1,0:T(8,128)(2,1)S(1)} %collective-permute-done.7.refs_0_, bf16[8192,1024]{1,0:T(8,128)(2,1)S(1)} %get-tuple-element.30.rest_6_.refs_4_.refs_1_.rest_7_, f32[96,1024]{1,0:T(8,128)S(1)} %shard_map.85.refs_2_, ...), custom_call_target="tpu_custom_call" | custom-call | flops 201326592 | bytes 2097152 | tf_op jit(solution)/shard_map/pallas_call | solution.py:530
  59.1 0.6 collective-permute-start.19
  59.7 0.8 collective-permute-done.19
  60.5 2.8 %collective-permute-done.20 = f32[2,8,96]{2,1,0:T(8,128)S(1)} collective-permute-done((f32[2,8,96]{2,1,0:T(8,128)S(1)}, f32[2,8,96]{2,1,0:T(8,128)S(1)}, u32[]{:S(2)}, u32[]{:S(2)}) %collective-permute-start.20) | collective-permute-done | bytes 6176 | tf_op jit(solution)/shard_map/ppermute | solution.py:576
  63.3 1.2 %collective-permute-start.21 = (f32[2,8,96]{2,1,0:T(8,128)S(1)}, f32[2,8,96]{2,1,0:T(8,128)S(1)}, u32[]{:S(2)}, u32[]{:S(2)}) collective-permute-start(f32[2,8,96]{2,1,0:T(8,128)S(1)} %add.7), channel_id=1, source_target_pairs={{0,2},{2,0},{4,6},{6,4},{8,10},{10,8},{12,14},{14,12},{1,3},{3,1},... | collective-permute-start | bytes 18440 | tf_op jit(solution)/shard_map/ppermute | solution.py:583
  64.9 1.3 %collective-permute-done.21.rest_12_ = f32[2,8,96]{2,1,0:T(8,128)S(1)} collective-permute-done((f32[2,8,96]{2,1,0:T(8,128)S(1)}, f32[2,8,96]{2,1,0:T(8,128)S(1)}, u32[]{:S(2)}, u32[]{:S(2)}) %collective-permute-start.21) | collective-permute-done | bytes 6176 | tf_op jit(solution)/shard_map/ppermute | solution.py:583
  66.2 2.6 %collective-permute-done.22.rest_13_ = f32[2,8,96]{2,1,0:T(8,128)S(1)} collective-permute-done((f32[2,8,96]{2,1,0:T(8,128)S(1)}, f32[2,8,96]{2,1,0:T(8,128)S(1)}, u32[]{:S(2)}, u32[]{:S(2)}) %collective-permute-start.22) | collective-permute-done | bytes 6176 | tf_op jit(solution)/shard_map/ppermute | solution.py:583
  68.8 2.2 %gate.6 = (bf16[96,1024]{1,0:T(8,128)(2,1)S(1)}, f32[96,1024]{1,0:T(8,128)S(1)}) custom-call(s32[3]{0:T(128)S(1)} %pad_add_fusion.meta, f32[2,96,1024]{2,1,0:T(8,128)S(1)} %get-tuple-element.23.base.refs_3_, bf16[96,1024]{1,0:T(8,128)(2,1)S(1)} %collective-permute-done.23.rest_0_.refs_4_, f32[1,2048]{1,0:T(1,128)S(1)} %copy-done, ...), custom_call_target="tpu_custom_call" | custom-call | flops 15728640 | bytes 1179648 | tf_op jit(solution)/shard_map/gate/pallas_call | solution.py:418
  71.1 3.2 %gate.7.refs_1_ = bf16[96,1024]{1,0:T(8,128)(2,1)S(1)} custom-call(s32[3]{0:T(128)S(1)} %pad_add_fusion.meta, f32[2,96,1024]{2,1,0:T(8,128)S(1)} %get-tuple-element.23.base.refs_3_, bf16[96,1024]{1,0:T(8,128)(2,1)S(1)} %collective-permute-done.18.rest_0_.refs_4_, f32[1,2048]{1,0:T(1,128)S(1)} %copy-done, ...), custom_call_target="tpu_custom_call" | custom-call | flops 15728640 | bytes 1179648 | tf_op jit(solution)/shard_map/gate/pallas_call | solution.py:418
  74.3 1.2 %collective-permute-start.24 = (bf16[96,1024]{1,0:T(8,128)(2,1)S(1)}, bf16[96,1024]{1,0:T(8,128)(2,1)S(1)}, u32[]{:S(2)}, u32[]{:S(2)}) collective-permute-start(bf16[96,1024]{1,0:T(8,128)(2,1)S(1)} %gate.7.refs_1_), channel_id=1, source_target_pairs={{0,4},{4,12},{12,8},{8,0},{1,5},{5,13},{13,9},{9,1},{2,6},{6,14},{... | collective-permute-start | bytes 589832 | tf_op jit(solution)/shard_map/ppermute | solution.py:565
  75.5 1.0 collective-permute-done.28.refs_0_
  76.5 5.7 %collective-permute-done.24.refs_1_ = bf16[96,1024]{1,0:T(8,128)(2,1)S(1)} collective-permute-done((bf16[96,1024]{1,0:T(8,128)(2,1)S(1)}, bf16[96,1024]{1,0:T(8,128)(2,1)S(1)}, u32[]{:S(2)}, u32[]{:S(2)}) %collective-permute-start.24) | collective-permute-done | bytes 196640 | tf_op jit(solution)/shard_map/ppermute | solution.py:565
  82.2 4.2 %collective-permute-start.35 = (bf16[96,1024]{1,0:T(8,128)(2,1)S(1)}, bf16[96,1024]{1,0:T(8,128)(2,1)S(1)}, u32[]{:S(2)}, u32[]{:S(2)}) collective-permute-start(bf16[96,1024]{1,0:T(8,128)(2,1)S(1)} %gate.7.refs_1_), channel_id=1, source_target_pairs={{0,1},{1,0},{2,3},{3,2},{4,5},{5,4},{6,7},{7,6},{8,9},{9,8},{10,11... | collective-permute-start | bytes 589832 | tf_op jit(solution)/shard_map/ppermute | solution.py:570
  86.9 1.7 %collective-permute-start.36 = (bf16[96,1024]{1,0:T(8,128)(2,1)S(1)}, bf16[96,1024]{1,0:T(8,128)(2,1)S(1)}, u32[]{:S(2)}, u32[]{:S(2)}) collective-permute-start(bf16[96,1024]{1,0:T(8,128)(2,1)S(1)} %collective-permute-done.29.refs_0_), channel_id=1, source_target_pairs={{0,4},{4,12},{12,8},{8,0},{1,5},{5,13},{13,9},{9,1},{2,6},{6,14},{... | collective-permute-start | bytes 589832 | tf_op jit(solution)/shard_map/ppermute | solution.py:565
  88.6 1.8 %collective-permute-done.25.refs_1_ = bf16[96,1024]{1,0:T(8,128)(2,1)S(1)} collective-permute-done((bf16[96,1024]{1,0:T(8,128)(2,1)S(1)}, bf16[96,1024]{1,0:T(8,128)(2,1)S(1)}, u32[]{:S(2)}, u32[]{:S(2)}) %collective-permute-start.25) | collective-permute-done | bytes 196640 | tf_op jit(solution)/shard_map/ppermute | solution.py:565
  90.3 4.4 %collective-permute-start.32 = (bf16[96,1024]{1,0:T(8,128)(2,1)S(1)}, bf16[96,1024]{1,0:T(8,128)(2,1)S(1)}, u32[]{:S(2)}, u32[]{:S(2)}) collective-permute-start(bf16[96,1024]{1,0:T(8,128)(2,1)S(1)} %collective-permute-done.28.refs_0_), channel_id=1, source_target_pairs={{0,1},{1,0},{2,3},{3,2},{4,5},{5,4},{6,7},{7,6},{8,9},{9,8},{10,11... | collective-permute-start | bytes 589832 | tf_op jit(solution)/shard_map/ppermute | solution.py:570
  95.2 4.0 %collective-permute-start.37 = (bf16[96,1024]{1,0:T(8,128)(2,1)S(1)}, bf16[96,1024]{1,0:T(8,128)(2,1)S(1)}, u32[]{:S(2)}, u32[]{:S(2)}) collective-permute-start(bf16[96,1024]{1,0:T(8,128)(2,1)S(1)} %collective-permute-done.36.refs_0_), channel_id=1, source_target_pairs={{0,1},{1,0},{2,3},{3,2},{4,5},{5,4},{6,7},{7,6},{8,9},{9,8},{10,11... | collective-permute-start | bytes 589832 | tf_op jit(solution)/shard_map/ppermute | solution.py:570
  99.2 1.6 %shard_map.89.refs_5_ = f32[192,1024]{1,0:T(8,128)S(1)} custom-call(s32[3]{0:T(128)S(1)} %pad_add_fusion.meta, bf16[96,1024]{1,0:T(8,128)(2,1)S(1)} %get-tuple-element.40.refs_0_, bf16[96,1024]{1,0:T(8,128)(2,1)S(1)} %gate.7.refs_1_, bf16[96,1024]{1,0:T(8,128)(2,1)S(1)} %collective-permute-done.34.refs_2_, ...), custom_call_target="tpu_custom_call" | custom-call | flops 805306368 | bytes 4194304 | tf_op jit(solution)/shard_map/pallas_call | solution.py:530
  101.4 1.6 %shard_map.90.refs_5_ = f32[192,1024]{1,0:T(8,128)S(1)} custom-call(s32[3]{0:T(128)S(1)} %pad_add_fusion.meta, bf16[96,1024]{1,0:T(8,128)(2,1)S(1)} %collective-permute-done.28.refs_0_, bf16[96,1024]{1,0:T(8,128)(2,1)S(1)} %collective-permute-done.24.refs_1_, bf16[96,1024]{1,0:T(8,128)(2,1)S(1)} %collective-permute-done.32.refs_2_, ...), custom_call_target="tpu_custom_call" | custom-call | flops 805306368 | bytes 4194304 | tf_op jit(solution)/shard_map/pallas_call | solution.py:530
  102.9 1.6 %shard_map.91.refs_2_ = f32[192,1024]{1,0:T(8,128)S(1)} custom-call(s32[3]{0:T(128)S(1)} %pad_add_fusion.meta, bf16[96,1024]{1,0:T(8,128)(2,1)S(1)} %collective-permute-done.29.refs_0_, bf16[96,1024]{1,0:T(8,128)(2,1)S(1)} %collective-permute-done.25.refs_1_, bf16[96,1024]{1,0:T(8,128)(2,1)S(1)} %collective-permute-done.30.refs_2_, ...), custom_call_target="tpu_custom_call" | custom-call | flops 805306368 | bytes 4194304 | tf_op jit(solution)/shard_map/pallas_call | solution.py:530
  104.5 1.0 shard_map.93.refs_2_
  105.5 1.0 shard_map.92.refs_2_
  106.6 1.1 shard_map.94.refs_5_
  107.7 1.8 %shard_map.95 = f32[1,2,96,1024]{3,2,1,0:T(8,128)} custom-call(s32[3]{0:T(128)S(1)} %pad_add_fusion.meta, bf16[96,1024]{1,0:T(8,128)(2,1)S(1)} %collective-permute-done.27.refs_0_, bf16[8192,1024]{1,0:T(8,128)(2,1)S(1)} %get-tuple-element.30.rest_6_.refs_4_.refs_1_.rest_7_, f32[96,1024]{1,0:T(8,128)S(1)} %shard_map.92.refs_2_, ...), custom_call_target="tpu_custom_call" | custom-call | flops 201326592 | bytes 2097152 | tf_op jit(solution)/shard_map/pallas_call | solution.py:530
  (53 shorter events, 4.3 us)
Async XLA Ops:
  7.4 10.2 %collective-permute-start = (f32[2,16,1024]{2,1,0:T(8,128)S(1)}, f32[2,16,1024]{2,1,0:T(8,128)S(1)}, u32[]{:S(2)}, u32[]{:S(2)}) collective-permute-start(f32[2,16,1024]{2,1,0:T(8,128)S(1)} %get-tuple-element.29), channel_id=1, source_target_pairs={{0,1},{1,0},{2,3},{3,2},{4,5},{5,4},{6,7},{7,6},{8,9},{9,8},{10,11... | collective-permute-start | bytes 393224 | tf_op jit(solution)/shard_map/ppermute | solution.py:570
  7.5 10.1 %collective-permute-start.1 = (f32[2,8,96]{2,1,0:T(8,128)S(1)}, f32[2,8,96]{2,1,0:T(8,128)S(1)}, u32[]{:S(2)}, u32[]{:S(2)}) collective-permute-start(f32[2,8,96]{2,1,0:T(8,128)S(1)} %get-tuple-element.31.rest_7_.rest_8_), channel_id=1, source_target_pairs={{0,4},{4,12},{12,8},{8,0},{1,5},{5,13},{13,9},{9,1},{2,6},{6,14},{... | collective-permute-start | bytes 18440 | tf_op jit(solution)/shard_map/ppermute | solution.py:565
  10.2 7.4 %collective-permute-start.2 = (f32[2,8,96]{2,1,0:T(8,128)S(1)}, f32[2,8,96]{2,1,0:T(8,128)S(1)}, u32[]{:S(2)}, u32[]{:S(2)}) collective-permute-start(f32[2,8,96]{2,1,0:T(8,128)S(1)} %get-tuple-element.31.rest_7_.rest_8_), channel_id=1, source_target_pairs={{0,12},{4,8},{12,0},{8,4},{1,13},{5,9},{13,1},{9,5},{2,14},{6,10},... | collective-permute-start | bytes 18440 | tf_op jit(solution)/shard_map/ppermute | solution.py:565
  12.4 5.2 %collective-permute-start.3 = (f32[2,8,96]{2,1,0:T(8,128)S(1)}, f32[2,8,96]{2,1,0:T(8,128)S(1)}, u32[]{:S(2)}, u32[]{:S(2)}) collective-permute-start(f32[2,8,96]{2,1,0:T(8,128)S(1)} %get-tuple-element.31.rest_7_.rest_8_), channel_id=1, source_target_pairs={{0,8},{4,0},{12,4},{8,12},{1,9},{5,1},{13,5},{9,13},{2,10},{6,2},{... | collective-permute-start | bytes 18440 | tf_op jit(solution)/shard_map/ppermute | solution.py:565
  13.7 3.9 %copy-start = (f32[1,2048]{1,0:T(1,128)S(1)}, f32[1,2048]{1,0:T(1,128)}, u32[]{:S(2)}) copy-start(f32[1,2048]{1,0:T(1,128)} %rest_1_.3) | copy-start | bytes 24580
  20.3 6.5 %collective-permute-start.8 = (bf16[96,1024]{1,0:T(8,128)(2,1)S(1)}, bf16[96,1024]{1,0:T(8,128)(2,1)S(1)}, u32[]{:S(2)}, u32[]{:S(2)}) collective-permute-start(bf16[96,1024]{1,0:T(8,128)(2,1)S(1)} %get-tuple-element.33.refs_0_), channel_id=1, source_target_pairs={{0,4},{4,12},{12,8},{8,0},{1,5},{5,13},{13,9},{9,1},{2,6},{6,14},{... | collective-permute-start | bytes 589832 | tf_op jit(solution)/shard_map/ppermute | solution.py:565
  23.6 7.9 %collective-permute-start.4 = (bf16[96,1024]{1,0:T(8,128)(2,1)S(1)}, bf16[96,1024]{1,0:T(8,128)(2,1)S(1)}, u32[]{:S(2)}, u32[]{:S(2)}) collective-permute-start(bf16[96,1024]{1,0:T(8,128)(2,1)S(1)} %gate.5.refs_1_), channel_id=1, source_target_pairs={{0,4},{4,12},{12,8},{8,0},{1,5},{5,13},{13,9},{9,1},{2,6},{6,14},{... | collective-permute-start | bytes 589832 | tf_op jit(solution)/shard_map/ppermute | solution.py:565
  26.8 8.7 %collective-permute-start.9 = (bf16[96,1024]{1,0:T(8,128)(2,1)S(1)}, bf16[96,1024]{1,0:T(8,128)(2,1)S(1)}, u32[]{:S(2)}, u32[]{:S(2)}) collective-permute-start(bf16[96,1024]{1,0:T(8,128)(2,1)S(1)} %collective-permute-done.8.refs_0_), channel_id=1, source_target_pairs={{0,4},{4,12},{12,8},{8,0},{1,5},{5,13},{13,9},{9,1},{2,6},{6,14},{... | collective-permute-start | bytes 589832 | tf_op jit(solution)/shard_map/ppermute | solution.py:565
  31.5 8.2 %collective-permute-start.5 = (bf16[96,1024]{1,0:T(8,128)(2,1)S(1)}, bf16[96,1024]{1,0:T(8,128)(2,1)S(1)}, u32[]{:S(2)}, u32[]{:S(2)}) collective-permute-start(bf16[96,1024]{1,0:T(8,128)(2,1)S(1)} %collective-permute-done.4.refs_1_), channel_id=1, source_target_pairs={{0,4},{4,12},{12,8},{8,0},{1,5},{5,13},{13,9},{9,1},{2,6},{6,14},{... | collective-permute-start | bytes 589832 | tf_op jit(solution)/shard_map/ppermute | solution.py:565
  31.5 8.2 %collective-permute-start.15 = (bf16[96,1024]{1,0:T(8,128)(2,1)S(1)}, bf16[96,1024]{1,0:T(8,128)(2,1)S(1)}, u32[]{:S(2)}, u32[]{:S(2)}) collective-permute-start(bf16[96,1024]{1,0:T(8,128)(2,1)S(1)} %gate.5.refs_1_), channel_id=1, source_target_pairs={{0,1},{1,0},{2,3},{3,2},{4,5},{5,4},{6,7},{7,6},{8,9},{9,8},{10,11... | collective-permute-start | bytes 589832 | tf_op jit(solution)/shard_map/ppermute | solution.py:570
  33.7 8.6 %collective-permute-start.14 = (bf16[96,1024]{1,0:T(8,128)(2,1)S(1)}, bf16[96,1024]{1,0:T(8,128)(2,1)S(1)}, u32[]{:S(2)}, u32[]{:S(2)}) collective-permute-start(bf16[96,1024]{1,0:T(8,128)(2,1)S(1)} %get-tuple-element.33.refs_0_), channel_id=1, source_target_pairs={{0,1},{1,0},{2,3},{3,2},{4,5},{5,4},{6,7},{7,6},{8,9},{9,8},{10,11... | collective-permute-start | bytes 589832 | tf_op jit(solution)/shard_map/ppermute | solution.py:570
  33.7 8.7 %collective-permute-start.13 = (bf16[96,1024]{1,0:T(8,128)(2,1)S(1)}, bf16[96,1024]{1,0:T(8,128)(2,1)S(1)}, u32[]{:S(2)}, u32[]{:S(2)}) collective-permute-start(bf16[96,1024]{1,0:T(8,128)(2,1)S(1)} %collective-permute-done.4.refs_1_), channel_id=1, source_target_pairs={{0,1},{1,0},{2,3},{3,2},{4,5},{5,4},{6,7},{7,6},{8,9},{9,8},{10,11... | collective-permute-start | bytes 589832 | tf_op jit(solution)/shard_map/ppermute | solution.py:570
  35.5 8.2 %collective-permute-start.16 = (bf16[96,1024]{1,0:T(8,128)(2,1)S(1)}, bf16[96,1024]{1,0:T(8,128)(2,1)S(1)}, u32[]{:S(2)}, u32[]{:S(2)}) collective-permute-start(bf16[96,1024]{1,0:T(8,128)(2,1)S(1)} %collective-permute-done.9.refs_0_), channel_id=1, source_target_pairs={{0,4},{4,12},{12,8},{8,0},{1,5},{5,13},{13,9},{9,1},{2,6},{6,14},{... | collective-permute-start | bytes 589832 | tf_op jit(solution)/shard_map/ppermute | solution.py:565
  39.7 8.6 %collective-permute-start.6 = (bf16[96,1024]{1,0:T(8,128)(2,1)S(1)}, bf16[96,1024]{1,0:T(8,128)(2,1)S(1)}, u32[]{:S(2)}, u32[]{:S(2)}) collective-permute-start(bf16[96,1024]{1,0:T(8,128)(2,1)S(1)} %collective-permute-done.5.refs_1_), channel_id=1, source_target_pairs={{0,4},{4,12},{12,8},{8,0},{1,5},{5,13},{13,9},{9,1},{2,6},{6,14},{... | collective-permute-start | bytes 589832 | tf_op jit(solution)/shard_map/ppermute | solution.py:565
  39.7 9.9 %collective-permute-start.12 = (bf16[96,1024]{1,0:T(8,128)(2,1)S(1)}, bf16[96,1024]{1,0:T(8,128)(2,1)S(1)}, u32[]{:S(2)}, u32[]{:S(2)}) collective-permute-start(bf16[96,1024]{1,0:T(8,128)(2,1)S(1)} %collective-permute-done.8.refs_0_), channel_id=1, source_target_pairs={{0,1},{1,0},{2,3},{3,2},{4,5},{5,4},{6,7},{7,6},{8,9},{9,8},{10,11... | collective-permute-start | bytes 589832 | tf_op jit(solution)/shard_map/ppermute | solution.py:570
  42.3 8.9 %collective-permute-start.11 = (bf16[96,1024]{1,0:T(8,128)(2,1)S(1)}, bf16[96,1024]{1,0:T(8,128)(2,1)S(1)}, u32[]{:S(2)}, u32[]{:S(2)}) collective-permute-start(bf16[96,1024]{1,0:T(8,128)(2,1)S(1)} %collective-permute-done.5.refs_1_), channel_id=1, source_target_pairs={{0,1},{1,0},{2,3},{3,2},{4,5},{5,4},{6,7},{7,6},{8,9},{9,8},{10,11... | collective-permute-start | bytes 589832 | tf_op jit(solution)/shard_map/ppermute | solution.py:570
  42.4 8.8 %collective-permute-start.10 = (bf16[96,1024]{1,0:T(8,128)(2,1)S(1)}, bf16[96,1024]{1,0:T(8,128)(2,1)S(1)}, u32[]{:S(2)}, u32[]{:S(2)}) collective-permute-start(bf16[96,1024]{1,0:T(8,128)(2,1)S(1)} %collective-permute-done.9.refs_0_), channel_id=1, source_target_pairs={{0,1},{1,0},{2,3},{3,2},{4,5},{5,4},{6,7},{7,6},{8,9},{9,8},{10,11... | collective-permute-start | bytes 589832 | tf_op jit(solution)/shard_map/ppermute | solution.py:570
  43.7 10.2 %collective-permute-start.17 = (bf16[96,1024]{1,0:T(8,128)(2,1)S(1)}, bf16[96,1024]{1,0:T(8,128)(2,1)S(1)}, u32[]{:S(2)}, u32[]{:S(2)}) collective-permute-start(bf16[96,1024]{1,0:T(8,128)(2,1)S(1)} %collective-permute-done.16.refs_0_), channel_id=1, source_target_pairs={{0,1},{1,0},{2,3},{3,2},{4,5},{5,4},{6,7},{7,6},{8,9},{9,8},{10,11... | collective-permute-start | bytes 589832 | tf_op jit(solution)/shard_map/ppermute | solution.py:570
  48.3 9.1 %collective-permute-start.7 = (bf16[96,1024]{1,0:T(8,128)(2,1)S(1)}, bf16[96,1024]{1,0:T(8,128)(2,1)S(1)}, u32[]{:S(2)}, u32[]{:S(2)}) collective-permute-start(bf16[96,1024]{1,0:T(8,128)(2,1)S(1)} %collective-permute-done.6.refs_0_), channel_id=1, source_target_pairs={{0,1},{1,0},{2,3},{3,2},{4,5},{5,4},{6,7},{7,6},{8,9},{9,8},{10,11... | collective-permute-start | bytes 589832 | tf_op jit(solution)/shard_map/ppermute | solution.py:570
  55.2 13.6 %collective-permute-start.23 = (bf16[96,1024]{1,0:T(8,128)(2,1)S(1)}, bf16[96,1024]{1,0:T(8,128)(2,1)S(1)}, u32[]{:S(2)}, u32[]{:S(2)}) collective-permute-start(bf16[96,1024]{1,0:T(8,128)(2,1)S(1)} %get-tuple-element.37), channel_id=1, source_target_pairs={{0,2},{2,0},{1,3},{3,1},{4,6},{6,4},{5,7},{7,5},{8,10},{10,8},{9,1... | collective-permute-start | bytes 589832 | tf_op jit(solution)/shard_map/ppermute | solution.py:573
  58.8 12.3 %collective-permute-start.18 = (bf16[96,1024]{1,0:T(8,128)(2,1)S(1)}, bf16[96,1024]{1,0:T(8,128)(2,1)S(1)}, u32[]{:S(2)}, u32[]{:S(2)}) collective-permute-start(bf16[96,1024]{1,0:T(8,128)(2,1)S(1)} %get-tuple-element.35), channel_id=1, source_target_pairs={{0,2},{2,0},{1,3},{3,1},{4,6},{6,4},{5,7},{7,5},{8,10},{10,8},{9,1... | collective-permute-start | bytes 589832 | tf_op jit(solution)/shard_map/ppermute | solution.py:573
  59.1 1.4 %collective-permute-start.19 = (f32[2,8,96]{2,1,0:T(8,128)S(1)}, f32[2,8,96]{2,1,0:T(8,128)S(1)}, u32[]{:S(2)}, u32[]{:S(2)}) collective-permute-start(f32[2,8,96]{2,1,0:T(8,128)S(1)} %get-tuple-element.36), channel_id=1, source_target_pairs={{0,1},{1,0},{2,3},{3,2},{4,5},{5,4},{6,7},{7,6},{8,9},{9,8},{10,11... | collective-permute-start | bytes 18440 | tf_op jit(solution)/shard_map/ppermute | solution.py:570
  60.5 2.8 %collective-permute-start.20 = (f32[2,8,96]{2,1,0:T(8,128)S(1)}, f32[2,8,96]{2,1,0:T(8,128)S(1)}, u32[]{:S(2)}, u32[]{:S(2)}) collective-permute-start(f32[2,8,96]{2,1,0:T(8,128)S(1)} %add.6), channel_id=1, source_target_pairs={{0,4},{4,0},{8,12},{12,8},{1,5},{5,1},{9,13},{13,9},{2,6},{6,2},{1... | collective-permute-start | bytes 18440 | tf_op jit(solution)/shard_map/ppermute | solution.py:576
  63.3 2.9 %collective-permute-start.21 = (f32[2,8,96]{2,1,0:T(8,128)S(1)}, f32[2,8,96]{2,1,0:T(8,128)S(1)}, u32[]{:S(2)}, u32[]{:S(2)}) collective-permute-start(f32[2,8,96]{2,1,0:T(8,128)S(1)} %add.7), channel_id=1, source_target_pairs={{0,2},{2,0},{4,6},{6,4},{8,10},{10,8},{12,14},{14,12},{1,3},{3,1},... | collective-permute-start | bytes 18440 | tf_op jit(solution)/shard_map/ppermute | solution.py:583
  64.5 4.3 %collective-permute-start.22 = (f32[2,8,96]{2,1,0:T(8,128)S(1)}, f32[2,8,96]{2,1,0:T(8,128)S(1)}, u32[]{:S(2)}, u32[]{:S(2)}) collective-permute-start(f32[2,8,96]{2,1,0:T(8,128)S(1)} %add.7), channel_id=1, source_target_pairs={{0,10},{2,8},{4,14},{6,12},{8,2},{10,0},{12,6},{14,4},{1,11},{3,9}... | collective-permute-start | bytes 18440 | tf_op jit(solution)/shard_map/ppermute | solution.py:583
  71.0 5.5 %collective-permute-start.28 = (bf16[96,1024]{1,0:T(8,128)(2,1)S(1)}, bf16[96,1024]{1,0:T(8,128)(2,1)S(1)}, u32[]{:S(2)}, u32[]{:S(2)}) collective-permute-start(bf16[96,1024]{1,0:T(8,128)(2,1)S(1)} %get-tuple-element.40.refs_0_), channel_id=1, source_target_pairs={{0,4},{4,12},{12,8},{8,0},{1,5},{5,13},{13,9},{9,1},{2,6},{6,14},{... | collective-permute-start | bytes 589832 | tf_op jit(solution)/shard_map/ppermute | solution.py:565
  74.3 7.9 %collective-permute-start.24 = (bf16[96,1024]{1,0:T(8,128)(2,1)S(1)}, bf16[96,1024]{1,0:T(8,128)(2,1)S(1)}, u32[]{:S(2)}, u32[]{:S(2)}) collective-permute-start(bf16[96,1024]{1,0:T(8,128)(2,1)S(1)} %gate.7.refs_1_), channel_id=1, source_target_pairs={{0,4},{4,12},{12,8},{8,0},{1,5},{5,13},{13,9},{9,1},{2,6},{6,14},{... | collective-permute-start | bytes 589832 | tf_op jit(solution)/shard_map/ppermute | solution.py:565
  76.5 10.4 %collective-permute-start.29 = (bf16[96,1024]{1,0:T(8,128)(2,1)S(1)}, bf16[96,1024]{1,0:T(8,128)(2,1)S(1)}, u32[]{:S(2)}, u32[]{:S(2)}) collective-permute-start(bf16[96,1024]{1,0:T(8,128)(2,1)S(1)} %collective-permute-done.28.refs_0_), channel_id=1, source_target_pairs={{0,4},{4,12},{12,8},{8,0},{1,5},{5,13},{13,9},{9,1},{2,6},{6,14},{... | collective-permute-start | bytes 589832 | tf_op jit(solution)/shard_map/ppermute | solution.py:565
  82.1 8.2 %collective-permute-start.25 = (bf16[96,1024]{1,0:T(8,128)(2,1)S(1)}, bf16[96,1024]{1,0:T(8,128)(2,1)S(1)}, u32[]{:S(2)}, u32[]{:S(2)}) collective-permute-start(bf16[96,1024]{1,0:T(8,128)(2,1)S(1)} %collective-permute-done.24.refs_1_), channel_id=1, source_target_pairs={{0,4},{4,12},{12,8},{8,0},{1,5},{5,13},{13,9},{9,1},{2,6},{6,14},{... | collective-permute-start | bytes 589832 | tf_op jit(solution)/shard_map/ppermute | solution.py:565
  82.2 8.2 %collective-permute-start.35 = (bf16[96,1024]{1,0:T(8,128)(2,1)S(1)}, bf16[96,1024]{1,0:T(8,128)(2,1)S(1)}, u32[]{:S(2)}, u32[]{:S(2)}) collective-permute-start(bf16[96,1024]{1,0:T(8,128)(2,1)S(1)} %gate.7.refs_1_), channel_id=1, source_target_pairs={{0,1},{1,0},{2,3},{3,2},{4,5},{5,4},{6,7},{7,6},{8,9},{9,8},{10,11... | collective-permute-start | bytes 589832 | tf_op jit(solution)/shard_map/ppermute | solution.py:570
  86.4 8.3 %collective-permute-start.34 = (bf16[96,1024]{1,0:T(8,128)(2,1)S(1)}, bf16[96,1024]{1,0:T(8,128)(2,1)S(1)}, u32[]{:S(2)}, u32[]{:S(2)}) collective-permute-start(bf16[96,1024]{1,0:T(8,128)(2,1)S(1)} %get-tuple-element.40.refs_0_), channel_id=1, source_target_pairs={{0,1},{1,0},{2,3},{3,2},{4,5},{5,4},{6,7},{7,6},{8,9},{9,8},{10,11... | collective-permute-start | bytes 589832 | tf_op jit(solution)/shard_map/ppermute | solution.py:570
  86.4 8.4 %collective-permute-start.33 = (bf16[96,1024]{1,0:T(8,128)(2,1)S(1)}, bf16[96,1024]{1,0:T(8,128)(2,1)S(1)}, u32[]{:S(2)}, u32[]{:S(2)}) collective-permute-start(bf16[96,1024]{1,0:T(8,128)(2,1)S(1)} %collective-permute-done.24.refs_1_), channel_id=1, source_target_pairs={{0,1},{1,0},{2,3},{3,2},{4,5},{5,4},{6,7},{7,6},{8,9},{9,8},{10,11... | collective-permute-start | bytes 589832 | tf_op jit(solution)/shard_map/ppermute | solution.py:570
  86.9 8.3 %collective-permute-start.36 = (bf16[96,1024]{1,0:T(8,128)(2,1)S(1)}, bf16[96,1024]{1,0:T(8,128)(2,1)S(1)}, u32[]{:S(2)}, u32[]{:S(2)}) collective-permute-start(bf16[96,1024]{1,0:T(8,128)(2,1)S(1)} %collective-permute-done.29.refs_0_), channel_id=1, source_target_pairs={{0,4},{4,12},{12,8},{8,0},{1,5},{5,13},{13,9},{9,1},{2,6},{6,14},{... | collective-permute-start | bytes 589832 | tf_op jit(solution)/shard_map/ppermute | solution.py:565
  90.3 10.5 %collective-permute-start.26 = (bf16[96,1024]{1,0:T(8,128)(2,1)S(1)}, bf16[96,1024]{1,0:T(8,128)(2,1)S(1)}, u32[]{:S(2)}, u32[]{:S(2)}) collective-permute-start(bf16[96,1024]{1,0:T(8,128)(2,1)S(1)} %collective-permute-done.25.refs_1_), channel_id=1, source_target_pairs={{0,4},{4,12},{12,8},{8,0},{1,5},{5,13},{13,9},{9,1},{2,6},{6,14},{... | collective-permute-start | bytes 589832 | tf_op jit(solution)/shard_map/ppermute | solution.py:565
  90.3 11.0 %collective-permute-start.32 = (bf16[96,1024]{1,0:T(8,128)(2,1)S(1)}, bf16[96,1024]{1,0:T(8,128)(2,1)S(1)}, u32[]{:S(2)}, u32[]{:S(2)}) collective-permute-start(bf16[96,1024]{1,0:T(8,128)(2,1)S(1)} %collective-permute-done.28.refs_0_), channel_id=1, source_target_pairs={{0,1},{1,0},{2,3},{3,2},{4,5},{5,4},{6,7},{7,6},{8,9},{9,8},{10,11... | collective-permute-start | bytes 589832 | tf_op jit(solution)/shard_map/ppermute | solution.py:570
  94.7 8.2 %collective-permute-start.31 = (bf16[96,1024]{1,0:T(8,128)(2,1)S(1)}, bf16[96,1024]{1,0:T(8,128)(2,1)S(1)}, u32[]{:S(2)}, u32[]{:S(2)}) collective-permute-start(bf16[96,1024]{1,0:T(8,128)(2,1)S(1)} %collective-permute-done.25.refs_1_), channel_id=1, source_target_pairs={{0,1},{1,0},{2,3},{3,2},{4,5},{5,4},{6,7},{7,6},{8,9},{9,8},{10,11... | collective-permute-start | bytes 589832 | tf_op jit(solution)/shard_map/ppermute | solution.py:570
  94.8 8.1 %collective-permute-start.30 = (bf16[96,1024]{1,0:T(8,128)(2,1)S(1)}, bf16[96,1024]{1,0:T(8,128)(2,1)S(1)}, u32[]{:S(2)}, u32[]{:S(2)}) collective-permute-start(bf16[96,1024]{1,0:T(8,128)(2,1)S(1)} %collective-permute-done.29.refs_0_), channel_id=1, source_target_pairs={{0,1},{1,0},{2,3},{3,2},{4,5},{5,4},{6,7},{7,6},{8,9},{9,8},{10,11... | collective-permute-start | bytes 589832 | tf_op jit(solution)/shard_map/ppermute | solution.py:570
  95.2 11.4 %collective-permute-start.37 = (bf16[96,1024]{1,0:T(8,128)(2,1)S(1)}, bf16[96,1024]{1,0:T(8,128)(2,1)S(1)}, u32[]{:S(2)}, u32[]{:S(2)}) collective-permute-start(bf16[96,1024]{1,0:T(8,128)(2,1)S(1)} %collective-permute-done.36.refs_0_), channel_id=1, source_target_pairs={{0,1},{1,0},{2,3},{3,2},{4,5},{5,4},{6,7},{7,6},{8,9},{9,8},{10,11... | collective-permute-start | bytes 589832 | tf_op jit(solution)/shard_map/ppermute | solution.py:570
  100.8 6.8 %collective-permute-start.27 = (bf16[96,1024]{1,0:T(8,128)(2,1)S(1)}, bf16[96,1024]{1,0:T(8,128)(2,1)S(1)}, u32[]{:S(2)}, u32[]{:S(2)}) collective-permute-start(bf16[96,1024]{1,0:T(8,128)(2,1)S(1)} %collective-permute-done.26.refs_0_), channel_id=1, source_target_pairs={{0,1},{1,0},{2,3},{3,2},{4,5},{5,4},{6,7},{7,6},{8,9},{9,8},{10,11... | collective-permute-start | bytes 589832 | tf_op jit(solution)/shard_map/ppermute | solution.py:570
